TPU v7x, 32 devices: a whole 2x2x4 slice. The times are simulated.
32 devices in a mesh: dp: 4 (over z), expert: 8 (over y, x, core).
Axes of the slice: x: 2, y: 2, z: 4, core: 2. Of those that a mesh axis runs over, the one named last changes fastest.
Arguments:
- tokens: bfloat16 [32768, 768], P(('dp', 'expert')), may hold values from -6 to 6
- lengths: int32 [32], P(('dp', 'expert')), may hold values from 128 to 1024, as said below
- expert_index: int32 [32768], P(('dp', 'expert')), may hold values from 0 to 7, as said below
- centroids: float32 [8, 768], replicated, may hold values from -0.15625 to 0.15625
- input_weight: bfloat16 [768, 2304], replicated, may hold values from -0.3125 to 0.3125
- output_weight: bfloat16 [768, 768], replicated, may hold values from -0.875 to 0.875
- first_gain: float32 [768], replicated, may hold values from 0.5 to 1.5
- first_shift: float32 [768], replicated, may hold values from -1 to 1
- second_gain: float32 [768], replicated, may hold values from 0.5 to 1.5
- second_shift: float32 [768], replicated, may hold values from -1 to 1
- up_weight: bfloat16 [8, 768, 3072], P('expert'), may hold values from -0.21875 to 0.21875
- down_weight: bfloat16 [8, 3072, 768], P('expert'), may hold values from -0.3125 to 0.3125
- cotangent: bfloat16 [32768, 768], P(('dp', 'expert')), may hold values from -6 to 6
Outputs:
- layer_output: bfloat16 [32768, 768], P(('dp', 'expert'))
- input_gradient: bfloat16 [32768, 768], P(('dp', 'expert'))
- input_weight_gradient: float32 [768, 2304], P('dp')
- output_weight_gradient: float32 [768, 768], P('dp')
- first_gain_gradient: float32 [768], P('dp')
- first_shift_gradient: float32 [768], P('dp')
- second_gain_gradient: float32 [768], P('dp')
- second_shift_gradient: float32 [768], P('dp')
- up_weight_gradient: float32 [8, 768, 3072], P('expert', 'dp')
- down_weight_gradient: float32 [8, 3072, 768], P('expert', 'dp')
Inputs may be any that keep to these rules, and one draw needn't show every extreme that they name: `lengths`: some sequence has exactly 1024 live positions. `expert_index`: in each aligned block of 1024 rows (the sequences of one device), at most 128 rows inside their sequence's length name any one expert, and one expert, the same in every block, is named by exactly 128 of them.
All inputs are finite; a program needn't handle non-finite values.
Results may differ from a plain program's by a relative error of at most 0.015.
Values may be sent and summed in bfloat16 or wider, within the bound.
No kernel may reach another device: no remote copies, remote signals or barrier semaphores. Data moves between devices by JAX's collectives and lax.ppermute only.
A program may use at most 256 MiB of HBM per device.

v0:
```python
import functools

import jax
import jax.numpy as jnp
from jax import lax
from jax.experimental import pallas as pl
from jax.experimental.pallas import tpu as pltpu
from jax.sharding import PartitionSpec as P

HEADS = 12
EPS = 1e-05
EXCLUDED = -1e30
BF = jnp.bfloat16
F32 = jnp.float32
QUERY_ROWS = 256
SEEN = 1
EXPERT_MIB = 54
HIDDEN_MIB = 60


def dot(left, right, left_axis=1, right_axis=0):
    return lax.dot_general(
        left,
        right,
        (((left_axis,), (right_axis,)), ((), ())),
        preferred_element_type=F32,
    )


def params(limit=60):
    return pltpu.CompilerParams(vmem_limit_bytes=limit << 20)


def cost(flops, bytes_accessed, transcendentals=0):
    return pl.CostEstimate(
        flops=int(flops * SEEN),
        bytes_accessed=int(bytes_accessed * SEEN),
        transcendentals=int(transcendentals * SEEN),
    )


def split_three(values):
    high = values.astype(BF)
    rest = values - high.astype(F32)
    middle = rest.astype(BF)
    return high, middle, (rest - middle.astype(F32)).astype(BF)


def normalise(values):
    average = jnp.mean(values, axis=-1, keepdims=True)
    centred = values - average
    variance = jnp.mean(centred * centred, axis=-1, keepdims=True)
    inverse = lax.rsqrt(variance + EPS)
    return centred * inverse, inverse


def norm_backward(normal, inverse, gain, gradient):
    scaled = gain * gradient
    first = jnp.mean(scaled, axis=-1, keepdims=True)
    second = jnp.mean(scaled * normal, axis=-1, keepdims=True)
    return (scaled - first - normal * second) * inverse


def selection(target, first, count):
    rows = lax.broadcasted_iota(jnp.int32, (count, target.shape[1]), 0) + first
    return jnp.where(rows == target, 1.0, 0.0).astype(BF)


def route_kernel(length_ref, expert_ref, cotangent_ref, out_ref, row_ref, column_ref, *, experts):
    step = pl.program_id(0)
    rows = cotangent_ref.shape[0]
    block = out_ref.shape[0]

    @pl.when(step == 0)
    def _():
        length = length_ref[0]
        position = lax.broadcasted_iota(jnp.int32, (1, rows), 1)
        named = jnp.where(position < length, expert_ref[...], -1)
        number = lax.broadcasted_iota(jnp.int32, (experts, rows), 0)
        onehot = jnp.where(number == named, 1.0, 0.0)
        before = lax.broadcasted_iota(jnp.int32, (rows, rows), 0)
        after = lax.broadcasted_iota(jnp.int32, (rows, rows), 1)
        earlier = jnp.where(before < after, 1.0, 0.0).astype(BF)
        counts = dot(onehot.astype(BF), earlier)
        slot = jnp.sum(onehot * counts, axis=0, keepdims=True).astype(jnp.int32)
        target = jnp.where(named >= 0, named * (rows // experts) + slot, -1)
        row_ref[...] = jnp.broadcast_to(target, row_ref.shape)
        wide = jnp.broadcast_to(target.astype(F32), (128, rows))
        column_ref[...] = wide.T.astype(jnp.int32)

    chosen = selection(row_ref[0:1, :], step * block, block)
    out_ref[...] = dot(chosen, cotangent_ref[...]).astype(BF)


def route(length, expert_index, cotangent, experts):
    rows, width = cotangent.shape
    block = 256
    return pl.pallas_call(
        functools.partial(route_kernel, experts=experts),
        out_shape=[
            jax.ShapeDtypeStruct((rows, width), BF),
            jax.ShapeDtypeStruct((8, rows), jnp.int32),
            jax.ShapeDtypeStruct((rows, 128), jnp.int32),
        ],
        grid_spec=pltpu.PrefetchScalarGridSpec(
            num_scalar_prefetch=1,
            grid=(rows // block,),
            in_specs=[
                pl.BlockSpec((1, rows), lambda i, l: (0, 0)),
                pl.BlockSpec((rows, width), lambda i, l: (0, 0)),
            ],
            out_specs=[
                pl.BlockSpec((block, width), lambda i, l: (i, 0)),
                pl.BlockSpec((8, rows), lambda i, l: (0, 0)),
                pl.BlockSpec((rows, 128), lambda i, l: (0, 0)),
            ],
        ),
        compiler_params=params(60),
        cost_estimate=cost(2 * rows * rows * width, 4 * rows * width),
        name="route",
    )(length, expert_index.reshape(1, rows), cotangent)


def project_kernel(tokens_ref, weight_ref, norms_ref, out_ref):
    normal, _ = normalise(tokens_ref[...].astype(F32))
    normed = (normal * norms_ref[0:1, :] + norms_ref[1:2, :]).astype(BF)
    out_ref[...] = dot(normed, weight_ref[...]).astype(BF)


def project(tokens, weight, norms):
    rows, width = tokens.shape
    columns = weight.shape[1]
    block = 256
    return pl.pallas_call(
        project_kernel,
        out_shape=jax.ShapeDtypeStruct((rows, columns), BF),
        grid=(rows // block,),
        in_specs=[
            pl.BlockSpec((block, width), lambda i: (i, 0)),
            pl.BlockSpec((width, columns), lambda i: (0, 0)),
            pl.BlockSpec((4, width), lambda i: (0, 0)),
        ],
        out_specs=pl.BlockSpec((block, columns), lambda i: (i, 0)),
        compiler_params=params(24),
        cost_estimate=cost(2 * rows * width * columns, 2 * (rows + width) * columns),
        name="project",
    )(tokens, weight, norms)


def staggered(items, begin, finish, ahead=1):
    waiting = []
    for item in items:
        waiting.append((item, begin(item)))
        if len(waiting) > ahead:
            finish(*waiting.pop(0))
    for item, values in waiting:
        finish(item, values)


def length_bias(rows, length):
    row = lax.broadcasted_iota(jnp.int32, (rows, 1), 0)
    return jnp.where(row < length, 0.0, EXCLUDED).astype(BF)


def attend_kernel(length_ref, query_ref, key_ref, value_ref, mixed_ref, total_ref, *, scale, half):
    rows = query_ref.shape[0]
    lane = lax.broadcasted_iota(jnp.int32, (1, 2 * half), 1)
    zero, one = jnp.zeros((), BF), jnp.ones((), BF)
    bias = length_bias(rows, length_ref[0])
    done = {}
    place = lax.broadcasted_iota(jnp.int32, (1, 128), 1)
    first = 2 * pl.program_id(0)
    keys = [jnp.where(lane == half * (1 - head), bias, key_ref[...]) for head in range(2)]

    def scores_of(item):
        start, head = item
        end = start + QUERY_ROWS
        row = lax.broadcasted_iota(jnp.int32, (QUERY_ROWS, QUERY_ROWS), 0)
        column = lax.broadcasted_iota(jnp.int32, (QUERY_ROWS, QUERY_ROWS), 1)
        scaled = query_ref[start:end, :] * jnp.asarray(scale, BF)
        rest = jnp.where(lane == half * (1 - head), one, zero)
        scores = dot(jnp.where((lane // half) == head, scaled, rest), keys[head][:end], 1, 1)
        last = jnp.where(column <= row, scores[:, start:], EXCLUDED)
        return jnp.concatenate([scores[:, :start], last], axis=1) if start else last

    def mix(item, scores):
        start, head = item
        end = start + QUERY_ROWS
        other = half * (1 - head)
        ones = jnp.where(lane == other, one, zero)
        value = jnp.where((lane // half) == head, value_ref[:end, :], ones)
        top = jnp.max(scores, axis=1, keepdims=True)
        out = dot(jnp.exp(scores - top).astype(BF), value)
        total = out[:, other : other + 1]
        done[item] = (out / total, top + jnp.log(total))
        if head == 1:
            low, high = done[start, 0], done[start, 1]
            mixed_ref[start:end, :] = jnp.where(lane < half, low[0], high[0]).astype(BF)
            other = jnp.where(place == first + 1, high[1], total_ref[start:end, :])
            total_ref[start:end, :] = jnp.where(place == first, low[1], other)

    starts = range(0, rows, QUERY_ROWS)
    staggered([(start, head) for start in starts for head in range(2)], scores_of, mix, 2)


def pair_specs(rows, wide, pairs, thirds):
    return [pl.BlockSpec((rows, wide), lambda i, l, o=o: (0, i + o * pairs)) for o in range(thirds)]


def attend(length, projected):
    rows, width = projected.shape[0], projected.shape[1] // 3
    size = width // HEADS
    pairs = HEADS // 2
    one = pl.BlockSpec((rows, 2 * size), lambda i, l: (0, i))
    return pl.pallas_call(
        functools.partial(attend_kernel, scale=size**-0.5, half=size),
        out_shape=[
            jax.ShapeDtypeStruct((rows, width), BF),
            jax.ShapeDtypeStruct((rows, 128), F32),
        ],
        grid_spec=pltpu.PrefetchScalarGridSpec(
            num_scalar_prefetch=1,
            grid=(pairs,),
            in_specs=pair_specs(rows, 2 * size, pairs, 3),
            out_specs=[one, pl.BlockSpec((rows, 128), lambda i, l: (0, 0))],
        ),
        compiler_params=params(16),
        cost_estimate=cost(
            16 * rows * rows * width, 12 * rows * width, HEADS * rows * rows // 2
        ),
        name="attend",
    )(length, projected, projected, projected)


def attend_back_kernel(
    length_ref,
    query_ref,
    key_ref,
    value_ref,
    mixed_ref,
    total_ref,
    incoming_ref,
    out_ref,
    key_sum,
    value_sum,
    *,
    scale,
    half,
):
    lane = lax.broadcasted_iota(jnp.int32, (1, 2 * half), 1)
    bias = length_bias(query_ref.shape[0], length_ref[0])
    zero, one = jnp.zeros((), BF), jnp.ones((), BF)
    key_sum[...] = jnp.zeros_like(key_sum)
    value_sum[...] = jnp.zeros_like(value_sum)
    parts = {}

    def products(item):
        start, head = item
        end = start + QUERY_ROWS
        mine = (lane // half) == head
        other = half * (1 - head)
        ones = jnp.where((lane >= other) & (lane < other + 3), one, zero)

        def extend(base, column, spare):
            a, b, c = split_three(-column)
            rest = jnp.where(lane == other + 2, c, jnp.where(lane == other + 3, spare, zero))
            rest = jnp.where(lane == other + 1, b, rest)
            return jnp.where(mine, base, jnp.where(lane == other, a, rest))

        row = lax.broadcasted_iota(jnp.int32, (QUERY_ROWS, QUERY_ROWS), 0)
        column = lax.broadcasted_iota(jnp.int32, (QUERY_ROWS, QUERY_ROWS), 1)
        incoming = incoming_ref[start:end, :]
        product = incoming.astype(F32) * mixed_ref[start:end, :].astype(F32)
        query = jnp.where(mine, query_ref[start:end, :] * jnp.asarray(scale, BF), zero)
        grad = jnp.where(mine, incoming, zero)
        inner = jnp.sum(jnp.where(mine, product, 0.0), axis=1, keepdims=True)
        at = lax.broadcasted_iota(jnp.int32, (1, 128), 1) == 2 * pl.program_id(0) + head
        total = jnp.sum(jnp.where(at, total_ref[start:end, :], 0.0), axis=1, keepdims=True)
        spare = jnp.where(lane == other + 3, bias[:end], ones)
        key = jnp.where(mine, key_ref[:end, :], spare)
        scores = dot(key, extend(query, total, one), 1, 1)
        last = jnp.where(row <= column, scores[start:, :], EXCLUDED)
        scores = jnp.concatenate([scores[:start, :], last], axis=0) if start else last
        value = jnp.where(mine, value_ref[:end, :], ones)
        return scores, dot(value, extend(grad, inner, zero), 1, 1), query, grad

    def gradients(item, values):
        start, head = item
        scores, centred, query, grad = values
        end = start + QUERY_ROWS
        probs = jnp.exp(scores)
        score_gradient = (probs * centred).astype(BF)
        value_sum[:end, :] += dot(probs.astype(BF), grad)
        key_sum[:end, :] += dot(score_gradient, query)
        key = jnp.where((lane // half) == head, key_ref[:end, :], zero)
        parts[item] = dot(score_gradient, key, 0, 0)
        if head == 1:
            total = parts[start, 0] + parts[start, 1]
            out_ref[0, start:end, :] = (total * scale).astype(BF)

    starts = range(0, query_ref.shape[0], QUERY_ROWS)
    staggered([(start, head) for start in starts for head in range(2)], products, gradients)
    out_ref[1] = key_sum[...].astype(BF)
    out_ref[2] = value_sum[...].astype(BF)


def attend_back(length, projected, mixed, total, incoming):
    rows, width = projected.shape[0], projected.shape[1] // 3
    size = width // HEADS
    pairs = HEADS // 2
    one = pl.BlockSpec((rows, 2 * size), lambda i, l: (0, i))
    return pl.pallas_call(
        functools.partial(attend_back_kernel, scale=size**-0.5, half=size),
        out_shape=jax.ShapeDtypeStruct((3, rows, width), BF),
        grid_spec=pltpu.PrefetchScalarGridSpec(
            num_scalar_prefetch=1,
            grid=(pairs,),
            in_specs=pair_specs(rows, 2 * size, pairs, 3)
            + [one, pl.BlockSpec((rows, 128), lambda i, l: (0, 0)), one],
            out_specs=pl.BlockSpec((3, rows, 2 * size), lambda i, l: (0, 0, i)),
            scratch_shapes=[pltpu.VMEM((rows, 2 * size), F32)] * 2,
        ),
        compiler_params=params(24),
        cost_estimate=cost(
            30 * rows * rows * width, 20 * rows * width, HEADS * rows * rows // 2
        ),
        name="attend_back",
    )(length, projected, projected, projected, mixed, total, incoming)


def picked_rows(target, centroids_ref, capacity):
    experts, width = centroids_ref.shape
    pieces = [piece.astype(F32) for piece in split_three(centroids_ref[...])]
    rest = jnp.zeros((128 - 3 * experts, width), F32)
    table = jnp.concatenate(pieces + [rest], axis=0).astype(BF)
    lane = lax.broadcasted_iota(jnp.int32, (1, 128), 1)
    low = jnp.where(lane < 3 * experts, (lane % experts) * capacity, 1 << 20)
    onehot = jnp.where((target >= low) & (target < low + capacity), 1.0, 0.0).astype(BF)
    return dot(onehot, table)


def present_rows(block_index, count, length):
    row = lax.broadcasted_iota(jnp.int32, (count, 1), 0) + block_index * count
    return jnp.where(row < length, 1.0, 0.0)


def hidden_kernel(
    length_ref,
    mixed_ref,
    tokens_ref,
    weight_ref,
    norms_ref,
    centroids_ref,
    row_ref,
    column_ref,
    residual_ref,
    gate_ref,
    out_ref,
    hidden_low,
):
    rows = row_ref.shape[1]
    count = 256

    def branch_of(number):
        return dot(mixed_ref[number * count : (number + 1) * count, :], weight_ref[...])

    def finish(number, branch):
        at = slice(number * count, (number + 1) * count)
        mask = present_rows(number, count, length_ref[0])
        residual = tokens_ref[at, :].astype(F32) + mask * branch
        residual_ref[at, :] = residual
        normal, _ = normalise(residual)
        hidden = normal * norms_ref[2:3, :] + norms_ref[3:4, :]
        picked = picked_rows(column_ref[at, :], centroids_ref, rows // centroids_ref.shape[0])
        gate = jax.nn.sigmoid(jnp.sum(hidden * picked, axis=-1, keepdims=True))
        gate_ref[at, :] = jnp.broadcast_to(gate, (count, 128))
        hidden_low[at, :] = hidden.astype(BF)

    staggered(range(rows // count), branch_of, finish)

    @pl.loop(0, rows // (2 * count))
    def _(number):
        for part in range(2):
            first = pl.multiple_of((2 * number + part) * count, count)
            chosen = selection(row_ref[0:1, :], first, count)
            out_ref[pl.ds(first, count), :] = dot(chosen, hidden_low[...]).astype(BF)


def hidden_rows(length, mixed, tokens, weight, norms, centroids, target_row, target_column):
    rows, width = tokens.shape
    experts = centroids.shape[0]
    whole = lambda *shape: pl.BlockSpec(shape, lambda i, l: (0,) * len(shape))
    return pl.pallas_call(
        hidden_kernel,
        out_shape=[
            jax.ShapeDtypeStruct((rows, width), F32),
            jax.ShapeDtypeStruct((rows, 128), F32),
            jax.ShapeDtypeStruct((rows, width), BF),
        ],
        grid_spec=pltpu.PrefetchScalarGridSpec(
            num_scalar_prefetch=1,
            grid=(1,),
            in_specs=[
                whole(rows, width),
                whole(rows, width),
                whole(width, width),
                whole(4, width),
                whole(experts, width),
                whole(8, rows),
                whole(rows, 128),
            ],
            out_specs=[whole(rows, width), whole(rows, 128), whole(rows, width)],
            scratch_shapes=[pltpu.VMEM((rows, width), BF)],
        ),
        compiler_params=params(HIDDEN_MIB),
        cost_estimate=cost(2 * rows * (rows + width) * width, 12 * rows * width),
        name="hidden_rows",
    )(length, mixed, tokens, weight, norms, centroids, target_row, target_column)


LINE = 4
MIDDLE = 2


def far_first(number, place, shares):
    return jnp.where(place < shares // 2, shares - 1 - number, number)


def expert_kernel(
    me_ref,
    place_ref,
    rows_ref,
    cotangent_ref,
    centroids_ref,
    up_ref,
    down_ref,
    back_ref,
    *refs,
    shares,
    together,
):
    outs, scratch = refs[:-7], refs[-7:]
    produced_sum, back_sum, transposed, gradient, downs, ups, sems = scratch
    step = pl.program_id(0)
    width = rows_ref.shape[1]
    share = width // shares

    @pl.when(step == 0)
    def _():
        hidden = rows_ref[...].astype(F32)
        centroid = centroids_ref[pl.ds(me_ref[0], 1), :]
        gate = jax.nn.sigmoid(jnp.sum(hidden * centroid, axis=-1, keepdims=True))
        gradient[...] = (gate * cotangent_ref[...].astype(F32)).astype(BF)
        produced_sum[...] = jnp.zeros_like(produced_sum)
        back_sum[...] = jnp.zeros_like(back_sum)
        values = rows_ref[...].T
        for number in range(shares):
            to = pl.multiple_of(far_first(number, place_ref[0], shares) * share, 16)
            transposed[pl.ds(to, share), :] = values[number * share : (number + 1) * share]

    upper = dot(rows_ref[...], up_ref[...])
    part = 0.5 + 0.5 * lax.erf(upper * (0.5**0.5))
    density = jnp.exp(upper * upper * -0.5) * 0.3989422804014327
    active = (upper * part).astype(BF)
    slope = part + upper * density
    active_gradient = dot(gradient[...], down_ref[...], 1, 1)
    upper_gradient = (active_gradient * slope).astype(BF)
    produced_sum[...] += dot(active, down_ref[...])
    down = dot(active, gradient[...], 0, 0).astype(BF)
    back_sum[...] += dot(upper_gradient, up_ref[...], 1, 1)
    up = dot(transposed[...], upper_gradient).astype(BF)
    real = far_first(step, place_ref[0], shares)
    slot = lax.rem(step, 2)
    pieces = down.shape[0] // share
    places = out_places(shares, pieces, together)

    def down_copy(number, slot):
        target = outs[places[number][0][0]].at[pl.ds(0, pieces)]
        return pltpu.make_async_copy(downs.at[slot], target, sems.at[slot, shares])

    def up_copy(number, slot, piece):
        array, first = places[number][1]
        target = outs[array].at[first + piece]
        return pltpu.make_async_copy(ups.at[slot, number], target, sems.at[slot, number])

    def wait(slot):
        down_copy(0, slot).wait()
        for number in range(shares):
            up_copy(number, slot, 0).wait()

    @pl.when(step >= 2)
    def _():
        wait(slot)

    for piece in range(pieces):
        downs[slot, piece] = down[piece * share : (piece + 1) * share]
    for number in range(shares):
        ups[slot, number] = up[number * share : (number + 1) * share]
        up_copy(number, slot, real).start()

        @pl.when(step == number)
        def _(number=number):
            down_copy(number, slot).start()

    @pl.when(step == pl.num_programs(0) - 1)
    def _():
        back_ref[:, :width] = produced_sum[...].astype(BF)
        back_ref[:, width:] = back_sum[...].astype(BF)
        wait(1 - slot)
        wait(slot)


def out_places(shares, pieces, together):
    places, count = [], 0
    for number in range(shares):
        if together and number != MIDDLE:
            places.append(((count, 0), (count, pieces)))
            count += 1
        else:
            places.append(((count, 0), (count + 1, 0)))
            count += 2
    return places


def expert(me, place, hidden, cotangent, centroids, up, down, shares):
    count, width = hidden.shape
    inner = up.shape[1]
    chunk, share = inner // shares, width // shares
    together = shares == LINE and chunk == width
    still = lambda c, m, p: (0, 0)
    once = pl.Buffered(1)
    whole = pl.BlockSpec((count, width), still, pipeline_mode=once)
    real = lambda c, p: far_first(c, p[0], shares)
    pieces = chunk // share
    places = out_places(shares, pieces, together)
    shapes = []
    for number in range(shares):
        if together and number != MIDDLE:
            shapes.append((pieces + shares, share, width))
        else:
            shapes += [(pieces, share, width), (shares, share, chunk)]
    outs = pl.pallas_call(
        functools.partial(expert_kernel, shares=shares, together=together),
        out_shape=[jax.ShapeDtypeStruct((count, 2 * width), BF)]
        + [jax.ShapeDtypeStruct(shape, BF) for shape in shapes],
        grid_spec=pltpu.PrefetchScalarGridSpec(
            num_scalar_prefetch=2,
            grid=(shares,),
            in_specs=[
                whole,
                whole,
                pl.BlockSpec(centroids.shape, still, pipeline_mode=once),
                pl.BlockSpec((width, chunk), lambda c, m, p: (0, real(c, p))),
                pl.BlockSpec((chunk, width), lambda c, m, p: (real(c, p), 0)),
            ],
            out_specs=[pl.BlockSpec((count, 2 * width), still, pipeline_mode=once)]
            + [pl.BlockSpec(memory_space=pl.ANY)] * len(shapes),
            scratch_shapes=[
                pltpu.VMEM((count, width), F32),
                pltpu.VMEM((count, width), F32),
                pltpu.VMEM((width, count), BF),
                pltpu.VMEM((count, width), BF),
                pltpu.VMEM((2, pieces, share, width), BF),
                pltpu.VMEM((2, shares, share, chunk), BF),
                pltpu.SemaphoreType.DMA((2, shares + 1)),
            ],
        ),
        compiler_params=params(EXPERT_MIB),
        cost_estimate=cost(12 * count * width * inner, 8 * inner * width, 2 * count * inner),
        name="expert",
    )(me, place, hidden, cotangent, centroids, up, down)
    back, arrays = outs[0], outs[1:]
    return back, [[(arrays[number], first) for number, first in pair] for pair in places]


def combine_kernel(
    length_ref,
    returned_ref,
    column_ref,
    cotangent_ref,
    residual_ref,
    gate_ref,
    norms_ref,
    centroids_ref,
    mixed_ref,
    weight_ref,
    layer_ref,
    residual_grad_ref,
    mixed_grad_ref,
    weight_grad_ref,
    gains_ref,
    weight_sum,
):
    step = pl.program_id(0)
    count, width = cotangent_ref.shape
    slots = returned_ref.shape[0]

    @pl.when(step == 0)
    def _():
        weight_sum[...] = jnp.zeros_like(weight_sum)
        gains_ref[...] = jnp.zeros_like(gains_ref)

    target = column_ref[:, 0:1]
    place = lax.broadcasted_iota(jnp.int32, (count, slots), 1)
    chosen = jnp.where(place == target, 1.0, 0.0).astype(BF)
    term = dot(chosen, returned_ref[:, :width])
    back = dot(chosen, returned_ref[:, width:])
    mask = present_rows(step, count, length_ref[0])
    gate = gate_ref[:, 0:1]
    cotangent = cotangent_ref[...].astype(F32)
    residual = residual_ref[...]
    layer_ref[...] = (residual + mask * gate * term).astype(BF)
    along = jnp.sum(cotangent * term, axis=-1, keepdims=True)
    logit_gradient = mask * along * gate * (1.0 - gate)
    picked = picked_rows(column_ref[...], centroids_ref, slots // centroids_ref.shape[0])
    hidden_gradient = back + logit_gradient * picked
    normal, inverse = normalise(residual)
    gains_ref[0:1, :] += jnp.sum(hidden_gradient * normal, axis=0, keepdims=True)
    gains_ref[1:2, :] += jnp.sum(hidden_gradient, axis=0, keepdims=True)
    residual_gradient = cotangent + norm_backward(
        normal, inverse, norms_ref[2:3, :], hidden_gradient
    )
    residual_grad_ref[...] = residual_gradient
    branch_gradient = (mask * residual_gradient).astype(BF)
    mixed_grad_ref[...] = dot(branch_gradient, weight_ref[...], 1, 1).astype(BF)
    weight_sum[...] += dot(mixed_ref[...], branch_gradient, 0, 0)

    @pl.when(step == pl.num_programs(0) - 1)
    def _():
        weight_grad_ref[...] = weight_sum[...].astype(BF)


def combine(
    length, returned, target_column, cotangent, residual, gate, norms, centroids, mixed, weight
):
    rows, width = cotangent.shape
    experts = centroids.shape[0]
    block = 256
    part = pl.BlockSpec((block, width), lambda i, l: (i, 0))
    thin = pl.BlockSpec((block, 128), lambda i, l: (i, 0))
    still = lambda i, l: (0, 0)
    return pl.pallas_call(
        combine_kernel,
        out_shape=[
            jax.ShapeDtypeStruct((rows, width), BF),
            jax.ShapeDtypeStruct((rows, width), F32),
            jax.ShapeDtypeStruct((rows, width), BF),
            jax.ShapeDtypeStruct((width, width), BF),
            jax.ShapeDtypeStruct((8, width), F32),
        ],
        grid_spec=pltpu.PrefetchScalarGridSpec(
            num_scalar_prefetch=1,
            grid=(rows // block,),
            in_specs=[
                pl.BlockSpec((rows, 2 * width), still),
                thin,
                part,
                part,
                thin,
                pl.BlockSpec((4, width), still),
                pl.BlockSpec((experts, width), still),
                part,
                pl.BlockSpec((width, width), still),
            ],
            out_specs=[
                part,
                part,
                part,
                pl.BlockSpec((width, width), still),
                pl.BlockSpec((8, width), still),
            ],
            scratch_shapes=[pltpu.VMEM((width, width), F32)],
        ),
        compiler_params=params(60),
        cost_estimate=cost(4 * rows * (rows + width) * width, 24 * rows * width),
        name="combine",
    )(
        length,
        returned,
        target_column,
        cotangent,
        residual,
        gate,
        norms,
        centroids,
        mixed,
        weight,
    )


def packed_rows(share, devices):
    unit = 16 * max(1, devices // 2)
    units = -(-(4 * share + 5) // unit)
    return [-(-units // 2) * unit, units // 2 * unit]


def pack_kernel(
    me_ref,
    grads_ref,
    tokens_ref,
    norms_ref,
    output_grad_ref,
    second_ref,
    *refs,
    shares,
):
    keeps, sends, (normed, sums, product) = refs[0:2], refs[2:4], refs[4:]
    step = pl.program_id(0)
    width = tokens_ref.shape[1]
    share = width // shares
    half = width // 2
    upper = (me_ref[0] & 1) != 0

    def put(number, first, values):
        border = keeps[0].shape[1]
        low, high = values[:, :half], values[:, half:]
        keep = jnp.where(upper, high, low).astype(BF)
        send = jnp.where(upper, low, high).astype(BF)
        for stream, (begin, end) in enumerate(((0, border), (border, 1 << 30))):
            a, b = max(first, begin), min(first + values.shape[0], end)
            if a < b:
                keeps[stream][number, a - begin : b - begin, :] = keep[a - first : b - first]
                sends[stream][number, a - begin : b - begin, :] = send[a - first : b - first]

    @pl.when(step == 0)
    def _():
        for first in range(0, tokens_ref.shape[0], 256):
            at = slice(first, first + 256)
            normal, _ = normalise(tokens_ref[at, :].astype(F32))
            low = (normal * norms_ref[0:1, :] + norms_ref[1:2, :]).astype(BF)
            normed[:, at] = low.T

    product[...] = dot(normed[...], grads_ref[...])
    sums[pl.ds(step, 1), :] = jnp.sum(grads_ref[...].astype(F32), axis=0, keepdims=True)
    for third in range(3):

        @pl.when(step == third)
        def _(third=third):
            @pl.loop(0, shares)
            def _(number):
                first = pl.multiple_of(number * share, 16)
                put(number, third * share, product[pl.ds(first, share), :])

    @pl.when(step == pl.num_programs(0) - 1)
    def _():
        total_rows = keeps[0].shape[1] + keeps[1].shape[1]
        rest = jnp.zeros((total_rows - 4 * share - 5, width), F32)
        tail = jnp.concatenate([sums[0:3, :], second_ref[0:2, :], rest], axis=0)

        @pl.loop(0, shares)
        def _(number):
            first = pl.multiple_of(number * share, 16)
            put(number, 3 * share, output_grad_ref[pl.ds(first, share), :].astype(F32))
            put(number, 4 * share, tail)


def pack(me, grads, tokens, norms, output_grad, second, shares, devices):
    rows, width = tokens.shape
    shapes = [(shares, count, width // 2) for count in packed_rows(width // shares, devices)] * 2
    whole = lambda shape: pl.BlockSpec(shape, lambda i, m: (0,) * len(shape))
    outs = pl.pallas_call(
        functools.partial(pack_kernel, shares=shares),
        out_shape=[jax.ShapeDtypeStruct(shape, BF) for shape in shapes],
        grid_spec=pltpu.PrefetchScalarGridSpec(
            num_scalar_prefetch=1,
            grid=(3,),
            in_specs=[
                pl.BlockSpec((None, rows, width), lambda i, m: (i, 0, 0)),
                whole((rows, width)),
                whole((4, width)),
                whole((width, width)),
                whole((8, width)),
            ],
            out_specs=[whole(shape) for shape in shapes],
            scratch_shapes=[
                pltpu.VMEM((width, rows), BF),
                pltpu.VMEM((8, width), F32),
                pltpu.VMEM((width, width), F32),
            ],
        ),
        compiler_params=params(40),
        cost_estimate=cost(6 * rows * width * width, 20 * rows * width),
        name="pack",
    )(me, grads, tokens, norms, output_grad, second)
    return outs[:2], outs[2:]


def project_back_kernel(
    grads_ref, tokens_ref, residual_grad_ref, weight_ref, norms_ref, out_ref
):
    width = tokens_ref.shape[1]
    gradient = None
    for number in range(3):
        columns = slice(number * width, (number + 1) * width)
        part = dot(grads_ref[number], weight_ref[:, columns], 1, 1)
        gradient = part if gradient is None else gradient + part
    normal, inverse = normalise(tokens_ref[...].astype(F32))
    input_part = norm_backward(normal, inverse, norms_ref[0:1, :], gradient)
    out_ref[...] = (residual_grad_ref[...] + input_part).astype(BF)


def project_back(grads, tokens, residual_grad, weight, norms):
    rows, width = tokens.shape
    block = 256
    part = pl.BlockSpec((block, width), lambda i: (i, 0))
    return pl.pallas_call(
        project_back_kernel,
        out_shape=jax.ShapeDtypeStruct((rows, width), BF),
        grid=(rows // block,),
        in_specs=[pl.BlockSpec((3, block, width), lambda i: (0, i, 0)), part, part]
        + [pl.BlockSpec(weight.shape, lambda i: (0, 0)), pl.BlockSpec((4, width), lambda i: (0, 0))],
        out_specs=part,
        compiler_params=params(24),
        cost_estimate=cost(18 * rows * width * width, 60 * rows * width),
        name="project_back",
    )(grads, tokens, residual_grad, weight, norms)


def add_kernel(left_ref, right_ref, out_ref):
    out_ref[...] = (left_ref[...].astype(F32) + right_ref[...].astype(F32)).astype(BF)


def add(left, right, pieces):
    (left, i), (right, j) = left, right
    _, rows, columns = left.shape
    half = pieces // 2
    spec = lambda first: pl.BlockSpec((half, rows, columns), lambda a: (first // half + a, 0, 0))
    size = pieces * rows * columns
    return pl.pallas_call(
        add_kernel,
        out_shape=jax.ShapeDtypeStruct((pieces, rows, columns), BF),
        grid=(2,),
        in_specs=[spec(i), spec(j)],
        out_specs=spec(0),
        compiler_params=params(10),
        cost_estimate=cost(0, 0),
        name="add",
    )(left, right)


def total_kernel(place_ref, middle_ref, end_ref, *refs, across):
    arrived, out_ref = refs[:-1], refs[-1]
    end = (place_ref[0] == 0) | (place_ref[0] == LINE - 1)
    rows, columns = middle_ref.shape[1:]
    for piece in range(middle_ref.shape[0]):
        total = jnp.where(end, end_ref[piece].astype(F32), middle_ref[piece].astype(F32))
        for ref in arrived:
            total = total + ref[piece].astype(F32)
        if across:
            out_ref[:, piece * columns : (piece + 1) * columns] = total
        else:
            out_ref[piece * rows : (piece + 1) * rows, :] = total


def line_total(place, middle, end, arrived, across):
    ins = [middle, end, *arrived]
    pieces, rows, columns = middle[0].shape
    shape = (rows, pieces * columns) if across else (pieces * rows, columns)
    half = pieces // 2
    block = (rows, half * columns) if across else (half * rows, columns)
    spec = lambda first: pl.BlockSpec((half, rows, columns), lambda a, p: (first // half + a, 0, 0))
    return pl.pallas_call(
        functools.partial(total_kernel, across=across),
        out_shape=jax.ShapeDtypeStruct(shape, F32),
        grid_spec=pltpu.PrefetchScalarGridSpec(
            num_scalar_prefetch=1,
            grid=(2,),
            in_specs=[spec(first) for _, first in ins],
            out_specs=pl.BlockSpec(block, lambda a, p: (0, a) if across else (a, 0)),
        ),
        compiler_params=params(16),
        cost_estimate=cost(0, 0),
        name="line_total",
    )(place, *[array for array, _ in ins])


class LineSum:
    def __init__(self, pairs, axis, place):
        self.axis, self.place = axis, place
        self.shares = lax.axis_size(axis)
        self.pairs = pairs
        self.line = self.shares == LINE and pairs[0][0][0] is pairs[0][1][0]
        self.got = {}

    def send(self, name, matrix=None):
        if not self.line:
            return
        ends = [(0, 1), (3, 2)]
        middles = [(1, 2), (2, 1)]
        out = [(2, 3), (1, 0)]

        def plus(number, before):
            if matrix is None:
                own = (self.pairs[number][0][0], 0)
                return add(own, (self.got[before], 0), own[0].shape[0])
            own = self.pairs[number][matrix]
            return add(own, (self.got[before], own[1]), self.pairs[MIDDLE][matrix][0].shape[0])

        values, route = {
            "far": lambda: (self.pairs[0][0][0], ends),
            "near": lambda: (self.pairs[1][0][0], ends),
            "own": lambda: (self.pairs[MIDDLE][matrix][0], ends),
            "far_on": lambda: (plus(0, "far"), middles),
            "near_on": lambda: (plus(1, "near"), middles),
            "far_out": lambda: (plus(3, "far_on"), out),
        }[name]()
        key = name if matrix is None else (name, matrix)
        self.got[key] = lax.ppermute(values, self.axis, route)

    def hold(self, name, values):
        if not self.line:
            return values
        self.got[name], values = lax.optimization_barrier((self.got[name], values))
        return values

    def totals(self):
        if self.line:
            sums = []
            for matrix in range(2):
                arrived = [(self.got[name, matrix], 0) for name in ("own", "near_on", "far_out")]
                ins = self.pairs[2][matrix], self.pairs[3][matrix]
                sums.append(line_total(self.place, *ins, arrived, across=matrix == 1))
            return sums
        sums = []
        for matrix in range(2):
            stacked = jnp.stack([pair[matrix][0] for pair in self.pairs])
            total = lax.psum_scatter(stacked, self.axis, scatter_dimension=0).astype(F32)
            pieces, rows, columns = total.shape
            if matrix:
                sums.append(total.swapaxes(0, 1).reshape(rows, pieces * columns))
            else:
                sums.append(total.reshape(pieces * rows, columns))
        return sums


def partner_pairs(axis, bit):
    return [(i, i ^ bit) for i in range(lax.axis_size(axis))]


def halves_kernel(me_ref, *refs, edges, bits):
    streams = len(bits)
    ins, outs = refs[: len(refs) - 2 * streams], refs[len(refs) - 2 * streams :]
    for stream, (first, last) in enumerate(edges):
        keep, got = ins[:2] if len(ins) == 2 else ins[2 * stream : 2 * stream + 2]
        kept, sent = outs[2 * stream : 2 * stream + 2]
        size = (last - first) // 2
        upper = (me_ref[0] // bits[stream]) % 2
        mine = pl.multiple_of(first + upper * size, 16)
        other = pl.multiple_of(first + (1 - upper) * size, 16)
        for at, out in ((mine, kept), (other, sent)):
            total = keep[:, pl.ds(at, size), :].astype(F32) + got[:, pl.ds(at, size), :].astype(F32)
            out[...] = total.astype(BF)


def halves(me, bits, edges, pairs):
    shares = pairs[0][0].shape[0]
    spec = lambda rows, columns: pl.BlockSpec((1, rows, columns), lambda z, m: (z, 0, 0))
    in_specs, out_specs, out_shape = [], [], []
    for keep, _ in pairs:
        in_specs += [spec(*keep.shape[1:])] * 2
    columns = pairs[0][0].shape[2]
    for first, last in edges:
        rows = (last - first) // 2
        out_specs += [spec(rows, columns)] * 2
        out_shape += [jax.ShapeDtypeStruct((shares, rows, columns), BF)] * 2
    size = sum(keep.size for keep, _ in pairs)
    outs = pl.pallas_call(
        functools.partial(halves_kernel, edges=edges, bits=bits),
        out_shape=out_shape,
        grid_spec=pltpu.PrefetchScalarGridSpec(
            num_scalar_prefetch=1, grid=(shares,), in_specs=in_specs, out_specs=out_specs
        ),
        compiler_params=params(20),
        cost_estimate=cost(0, 0),
        name="halves",
    )(me, *[array for pair in pairs for array in pair])
    return [(outs[2 * i], outs[2 * i + 1]) for i in range(len(bits))]


def join_kernel(*refs):
    ins, out_ref = refs[:-1], refs[-1]
    first = 0
    for keep, got in zip(ins[::2], ins[1::2]):
        last = first + keep.shape[1]
        total = keep[...].astype(F32) + got[...].astype(F32)
        out_ref[:, first:last, :] = total.astype(BF)
        first = last


def join(pairs):
    shares, _, columns = pairs[0][0].shape
    rows = sum(keep.shape[1] for keep, _ in pairs)
    size = shares * rows * columns
    return pl.pallas_call(
        join_kernel,
        out_shape=jax.ShapeDtypeStruct((shares, rows, columns), BF),
        compiler_params=params(12),
        cost_estimate=cost(0, 0),
        name="join",
    )(*[array for pair in pairs for array in pair])


def spread_kernel(parts_ref, out_ref):
    total = jnp.sum(parts_ref[...].astype(F32), axis=0).astype(BF)
    for number in range(out_ref.shape[0]):
        out_ref[number] = total


def spread(parts, devices):
    _, rows, columns = parts.shape
    size = parts.size + devices * rows * columns
    return pl.pallas_call(
        spread_kernel,
        out_shape=jax.ShapeDtypeStruct((devices, rows, columns), BF),
        compiler_params=params(12),
        cost_estimate=cost(0, 0),
        name="spread",
    )(parts)


def assemble_kernel(
    place_ref,
    gathered_ref,
    weight_ref,
    norms_ref,
    input_ref,
    output_ref,
    column_ref,
    tail_ref,
    summed,
    *,
    sources,
):
    half = gathered_ref.shape[2]
    share, width = output_ref.shape
    for device, first, count, to, side in sources:
        values = gathered_ref[device, first : first + count, :].astype(F32)
        summed[to : to + count, side * half : (side + 1) * half] = values
    shift_sum = gain_sum = 0.0
    for third in range(3):
        columns = slice(third * width, (third + 1) * width)
        values = summed[third * share : (third + 1) * share, :]
        input_ref[:, columns] = values
        weight = weight_ref[:, columns].astype(F32)
        line = summed[4 * share + third : 4 * share + third + 1, :]
        shift_sum = shift_sum + jnp.sum(weight * line, axis=1, keepdims=True)
        gain_sum = gain_sum + jnp.sum(weight * values, axis=1, keepdims=True)
    output_ref[...] = summed[3 * share : 4 * share, :]
    lane = lax.broadcasted_iota(jnp.int32, (1, 128), 1)
    column_ref[...] = jnp.where(lane == 0, gain_sum, shift_sum)
    tail_ref[...] = summed[4 * share : 4 * share + 8, :]


def assemble(place, gathered, weight, norms, share, orders, streams):
    devices, _, half = gathered.shape
    width = 2 * half
    levels = len(orders[0])
    sources = []
    for side in range(2):
        first, to = 0, 0
        for count, order in zip(streams, orders):
            for number in range(2**levels):
                digits = [(number >> (levels - 1 - level)) & 1 for level in range(levels)]
                device = side + sum(digit * bit for digit, bit in zip(digits, order))
                sources.append((device, first, count, to, side))
                to += count
            first += count
    total = sum(streams) * 2**levels
    whole = lambda shape: pl.BlockSpec(shape, lambda i, p: (0,) * len(shape))
    return pl.pallas_call(
        functools.partial(assemble_kernel, sources=sources),
        out_shape=[
            jax.ShapeDtypeStruct((share, 3 * width), F32),
            jax.ShapeDtypeStruct((share, width), F32),
            jax.ShapeDtypeStruct((share, 128), F32),
            jax.ShapeDtypeStruct((8, width), F32),
        ],
        grid_spec=pltpu.PrefetchScalarGridSpec(
            num_scalar_prefetch=1,
            grid=(1,),
            in_specs=[
                whole(gathered.shape),
                pl.BlockSpec((share, 3 * width), lambda i, p: (p[0], 0)),
                whole(norms.shape),
            ],
            out_specs=[
                whole((share, 3 * width)),
                whole((share, width)),
                whole((share, 128)),
                whole((8, width)),
            ],
            scratch_shapes=[pltpu.VMEM((total, width), F32)],
        ),
        compiler_params=params(24),
        cost_estimate=cost(0, 0),
        name="assemble",
    )(place, gathered, weight, norms)


def on_device(
    tokens,
    lengths,
    expert_index,
    centroids,
    input_weight,
    output_weight,
    first_gain,
    first_shift,
    second_gain,
    second_shift,
    up_weight,
    down_weight,
    cotangent,
):
    rows, width = tokens.shape
    experts = centroids.shape[0]
    capacity = rows // experts
    shares = lax.axis_size("dp")
    share = width // shares
    me = lax.axis_index("expert").reshape(1).astype(jnp.int32)
    place = lax.axis_index("dp").reshape(1).astype(jnp.int32)
    norms = jnp.stack([first_gain, first_shift, second_gain, second_shift])

    def exchange(values, axis="expert"):
        return lax.all_to_all(values, axis, split_axis=0, concat_axis=0, tiled=True)

    def dispatch(values):
        return exchange(values.reshape(experts, capacity, -1)).reshape(rows, -1)

    outgoing_cotangent, target_row, target_column = route(
        lengths, expert_index, cotangent, experts
    )
    arrived_cotangent = dispatch(outgoing_cotangent)
    held_tokens, target_row = lax.optimization_barrier((tokens, target_row))
    projected = project(held_tokens, input_weight, norms)
    mixed, total = attend(lengths, projected)
    mixed, arrived_cotangent = lax.optimization_barrier((mixed, arrived_cotangent))
    residual, gate, outgoing = hidden_rows(
        lengths, mixed, tokens, output_weight, norms, centroids, target_row, target_column
    )
    arrived = dispatch(outgoing)
    order = place if shares == LINE else jnp.full_like(place, shares)
    back, pairs = expert(
        me, order, arrived, arrived_cotangent, centroids, up_weight[0], down_weight[0], shares
    )
    line = LineSum(pairs, "dp", place)
    line.send("far")
    line.send("near")
    returned = dispatch(back)
    layer_output, residual_grad, mixed_grad, output_grad, second_gains = combine(
        lengths,
        returned,
        target_column,
        cotangent,
        residual,
        gate,
        norms,
        centroids,
        mixed,
        output_weight,
    )
    mixed_grad = line.hold("far", mixed_grad)
    line.send("far_on")
    grads = attend_back(lengths, projected, mixed, total, mixed_grad)
    keeps, sends = pack(
        me, grads, tokens, norms, output_grad, second_gains, shares, experts
    )
    swap = lambda values, bit: lax.ppermute(values, "expert", partner_pairs("expert", bit))
    pairs = [(keep, swap(send, 1)) for keep, send in zip(keeps, sends)]
    bits = [2**i for i in range(1, (experts - 1).bit_length())]
    orders = [bits, bits[::-1]]
    for level, now in enumerate(zip(*orders)):
        if level == 0:
            pairs = line.hold("near", pairs)
            line.send("near_on", 0)
            line.send("own", 0)
        made = halves(me, now, [(0, keep.shape[1]) for keep, _ in pairs], pairs)
        pairs = [(kept, swap(sent, bit)) for (kept, sent), bit in zip(made, now)]
        if level == 0:
            kept, got = pairs[0]
            pairs[0] = (line.hold("far_on", kept), got)
            line.send("far_out", 0)
    grads = line.hold(("own", 0), grads)
    input_gradient = project_back(grads, tokens, residual_grad, input_weight, norms)
    input_gradient, pairs = lax.optimization_barrier((input_gradient, pairs))
    for name in ("far_out", "near_on"):
        pairs = line.hold((name, 0), pairs)
    streams = [keep.shape[1] for keep, _ in pairs]
    over_line = exchange(join(pairs), "dp")
    for name in ("far_out", "near_on", "own"):
        line.send(name, 1)
    gathered = exchange(spread(over_line, experts))
    input_share, output_share, sums, tail = assemble(
        place, gathered, input_weight, norms, share, orders, streams
    )
    for name in ("far_out", "near_on", "own"):
        sums = line.hold((name, 1), sums)
    begin = lax.axis_index("dp") * share
    mine = lambda vector: lax.dynamic_slice_in_dim(vector, begin, share, vector.ndim - 1)
    shift_sum = sums[:, 1]
    gain_sum = (sums[:, 0] - mine(first_shift) * shift_sum) / mine(first_gain)
    second = mine(tail[3:5])
    down_share, up_share = line.totals()
    return (
        layer_output,
        input_gradient,
        input_share,
        output_share,
        gain_sum,
        shift_sum,
        second[0],
        second[1],
        up_share[None],
        down_share[None],
    )


def solution(mesh):
    both = P(("dp", "expert"))
    rows = P(("dp", "expert"), None)
    weights = P("expert", None, None)
    return jax.shard_map(
        on_device,
        mesh=mesh,
        in_specs=(rows, both, both, P(), P(), P(), P(), P(), P(), P(), weights, weights, rows),
        out_specs=(
            rows,
            rows,
            P("dp", None),
            P("dp", None),
            P("dp"),
            P("dp"),
            P("dp"),
            P("dp"),
            P("expert", "dp", None),
            P("expert", "dp", None),
        ),
        check_vma=False,
    )
```

profile of v0, /device:TPU:0, one launch (start us, length us, event | category | flops | bytes accessed | tf_op | source)
XLA Modules:
  0.0 318.8 jit_solution(14068435473155538893)
XLA Ops:
  1.3 5.2 %route.1 = (bf16[1024,768]{1,0:T(8,128)(2,1)}, s32[8,1024]{1,0:T(8,128)}, s32[1024,128]{1,0:T(8,128)}) custom-call(s32[1]{0:T(128)S(6)} %copy.23.length_ref, s32[1,1024]{1,0:T(1,128)} %bitcast.25, bf16[1024,768]{1,0:T(8,128)(2,1)} %cotangent_ref.3), custom_call_target="tpu_custom_call" | custom-call | flops 1610612736 | bytes 3145728 | tf_op jit(solution)/shard_map/route/pallas_call | solution.py:98
  6.5 5.3 %all-to-all-start = ((bf16[8,128,768]{2,1,0:T(8,128)(2,1)}), bf16[8,128,768]{2,1,0:T(8,128)(2,1)}, u32[]{:S(2)}, u32[]{:S(2)}) async-start(bf16[8,128,768]{2,1,0:T(8,128)(2,1)} %bitcast.19), calls=%async_computation | async-start | bytes 3145728 | tf_op jit(solution)/shard_map/all_to_all | solution.py:1125
  11.9 2.0 copy-done.7
  13.9 5.2 %project.1.query_ref.key_ref.value_ref = bf16[1024,2304]{1,0:T(8,128)(2,1)S(1)} custom-call(bf16[1024,768]{1,0:T(8,128)(2,1)S(1)} %copy-done.22, bf16[768,2304]{1,0:T(8,128)(2,1)S(1)} %copy-done.7, f32[4,768]{1,0:T(4,128)S(1)} %pad_maximum_fusion.norms_ref), custom_call_target="tpu_custom_call" | custom-call | flops 3623878656 | bytes 8257536 | tf_op jit(solution)/shard_map/project/pallas_call | solution.py:134
  19.1 13.9 %attend.1 = (bf16[1024,768]{1,0:T(8,128)(2,1)S(1)}, f32[1024,128]{1,0:T(8,128)S(1)}) custom-call(s32[1]{0:T(128)S(6)} %copy.23.length_ref, bf16[1024,2304]{1,0:T(8,128)(2,1)S(1)} %project.1.query_ref.key_ref.value_ref, bf16[1024,2304]{1,0:T(8,128)(2,1)S(1)} %project.1.query_ref.key_ref.value_ref, bf16[1024,2304]{1,0:T(8,128)(2,1)S(1)} %project.1.query_ref.key_ref.value_ref), custom_call_target="tpu_custom_call" | custom-call | flops 12884901888 | bytes 9437184 | tf_op jit(solution)/shard_map/attend/pallas_call | solution.py:215
  33.0 2.2 copy-done.24
  35.2 1.1 copy-done.26
  36.3 8.0 %hidden_rows.1 = (f32[1024,768]{1,0:T(8,128)}, f32[1024,128]{1,0:T(8,128)}, bf16[1024,768]{1,0:T(8,128)(2,1)}) custom-call(s32[1]{0:T(128)S(6)} %copy.23.length_ref, bf16[1024,768]{1,0:T(8,128)(2,1)} %copy-done.26, bf16[1024,768]{1,0:T(8,128)(2,1)} %tokens_ref.6, bf16[768,768]{1,0:T(8,128)(2,1)} %weight_ref.7, f32[4,768]{1,0:T(4,128)} %copy-done.20, ...), custom_call_target="tpu_custom_call" | custom-call | flops 2818572288 | bytes 9437184 | tf_op jit(solution)/shard_map/hidden_rows/pallas_call | solution.py:393
  44.4 4.2 %all-to-all-start.1 = ((bf16[8,128,768]{2,1,0:T(8,128)(2,1)}), bf16[8,128,768]{2,1,0:T(8,128)(2,1)S(1)}, u32[]{:S(2)}, u32[]{:S(2)}) async-start(bf16[8,128,768]{2,1,0:T(8,128)(2,1)} %bitcast.20), calls=%async_computation.1 | async-start | bytes 3145728 | tf_op jit(solution)/shard_map/all_to_all | solution.py:1125
  48.6 21.0 %all-to-all-done.1 = bf16[8,128,768]{2,1,0:T(8,128)(2,1)S(1)} async-done(((bf16[8,128,768]{2,1,0:T(8,128)(2,1)}), bf16[8,128,768]{2,1,0:T(8,128)(2,1)S(1)}, u32[]{:S(2)}, u32[]{:S(2)}) %all-to-all-start.1) | async-done | bytes 1572896 | tf_op jit(solution)/shard_map/all_to_all | solution.py:1125
  69.7 1.1 copy-done.32
  70.8 38.3 %expert.1 = (bf16[1024,1536]{1,0:T(8,128)(2,1)}, bf16[8,192,768]{2,1,0:T(8,128)(2,1)}, bf16[8,192,768]{2,1,0:T(8,128)(2,1)}, bf16[4,192,768]{2,1,0:T(8,128)(2,1)...) custom-call(s32[1]{0:T(128)} %bitcast.me_ref, s32[1]{0:T(128)} %bitcast.1.place_ref, ...), custom_call_target="tpu_custom_call" | custom-call | flops 28991029248 | bytes 18874368 | tf_op jit(solution)/shard_map/expert/pallas_call | solution.py:542
  109.2 4.6 %all-to-all-start.2 = ((bf16[8,128,1536]{2,1,0:T(8,128)(2,1)}), bf16[8,128,1536]{2,1,0:T(8,128)(2,1)}, u32[]{:S(2)}, u32[]{:S(2)}) async-start(bf16[8,128,1536]{2,1,0:T(8,128)(2,1)} %bitcast.15), calls=%async_computation.2 | async-start | bytes 6291456 | tf_op jit(solution)/shard_map/all_to_all | solution.py:1125
  113.8 5.4 %collective-permute-start.1 = (bf16[8,192,768]{2,1,0:T(8,128)(2,1)}, bf16[8,192,768]{2,1,0:T(8,128)(2,1)}, u32[]{:S(2)}, u32[]{:S(2)}) collective-permute-start(bf16[8,192,768]{2,1,0:T(8,128)(2,1)} %get-tuple-element.96.left_ref), channel_id=1, source_target_pairs={{0,8},{24,16},{1,9},{25,17},{2,10},{26,18},{3,11},{27,19},{4,12},{... | collective-permute-start | bytes 7077896 | tf_op jit(solution)/shard_map/ppermute | solution.py:908
  119.1 2.7 collective-permute-start.3
  121.8 29.9 %all-to-all-done.2 = bf16[8,128,1536]{2,1,0:T(8,128)(2,1)} async-done(((bf16[8,128,1536]{2,1,0:T(8,128)(2,1)}), bf16[8,128,1536]{2,1,0:T(8,128)(2,1)}, u32[]{:S(2)}, u32[]{:S(2)}) %all-to-all-start.2) | async-done | bytes 3145760 | tf_op jit(solution)/shard_map/all_to_all | solution.py:1125
  151.7 14.4 %combine.1 = (bf16[1024,768]{1,0:T(8,128)(2,1)}, f32[1024,768]{1,0:T(8,128)}, bf16[1024,768]{1,0:T(8,128)(2,1)}, bf16[768,768]{1,0:T(8,128)(2,1)}, f32[8,768]{1,0:T(8,128)}) custom-call(s32[1]{0:T(128)S(6)} %copy.23.length_ref, bf16[1024,1536]{1,0:T(8,128)(2,1)} %bitcast.10.returned_ref, s32[1024,128]{1,0:T(8,128)} %get-tuple-element.87.column_ref, ...), custom_call_target="tpu_custom_call" | custom-call | flops 5637144576 | bytes 18874368 | tf_op jit(solution)/shard_map/combine/pallas_call | solution.py:642
  166.0 3.5 %collective-permute-done.1.right_ref = bf16[8,192,768]{2,1,0:T(8,128)(2,1)} collective-permute-done((bf16[8,192,768]{2,1,0:T(8,128)(2,1)}, bf16[8,192,768]{2,1,0:T(8,128)(2,1)}, u32[]{:S(2)}, u32[]{:S(2)}) %collective-permute-start.1) | collective-permute-done | bytes 2359328 | tf_op jit(solution)/shard_map/ppermute | solution.py:908
  169.6 1.7 copy-done.11
  171.2 2.1 add.14
  173.3 1.0 collective-permute-start.2
  174.4 2.3 copy-done.25
  176.7 26.5 %attend_back.1.grads_ref = bf16[3,1024,768]{2,1,0:T(8,128)(2,1)S(1)} custom-call(s32[1]{0:T(128)S(6)} %copy.23.length_ref, bf16[1024,2304]{1,0:T(8,128)(2,1)S(1)} %copy-done.25, bf16[1024,2304]{1,0:T(8,128)(2,1)S(1)} %copy-done.25, bf16[1024,2304]{1,0:T(8,128)(2,1)S(1)} %copy-done.25, bf16[1024,768]{1,0:T(8,128)(2,1)S(1)} %copy-done.27, ...), custom_call_target="tpu_custom_call" | custom-call | flops 24159191040 | bytes 15728640 | tf_op jit(solution)/shard_map/attend_back/pallas_call | solution.py:312
  203.2 6.7 %pack.1 = (bf16[4,448,384]{2,1,0:T(8,128)(2,1)S(1)}, bf16[4,384,384]{2,1,0:T(8,128)(2,1)S(1)}, bf16[4,448,384]{2,1,0:T(8,128)(2,1)S(1)}, bf16[4,384,384]{2,1,0:T(8,128)(2,1)S(1)}) custom-call(s32[1]{0:T(128)} %bitcast.me_ref, bf16[3,1024,768]{2,1,0:T(8,128)(2,1)S(1)} %attend_back.1.grads_ref, bf16[1024,768]{1,0:T(8,128)(2,1)S(1)} %copy-done.23, ...), custom_call_target="tpu_custom_call" | custom-call | flops 3623878656 | bytes 15728640 | tf_op jit(solution)/shard_map/pack/pallas_call | solution.py:761
  210.0 0.5 collective-permute-start.5
  210.5 7.1 %collective-permute-start = (bf16[4,192,768]{2,1,0:T(8,128)(2,1)S(1)}, bf16[4,192,768]{2,1,0:T(8,128)(2,1)S(1)}, u32[]{:S(2)}, u32[]{:S(2)}) collective-permute-start(bf16[4,192,768]{2,1,0:T(8,128)(2,1)S(1)} %copy-done.12), channel_id=1, source_target_pairs={{0,8},{24,16},{1,9},{25,17},{2,10},{26,18},{3,11},{27,19},{4,12},{... | collective-permute-start | bytes 3538952 | tf_op jit(solution)/shard_map/ppermute | solution.py:908
  217.7 2.4 collective-permute-done.3.right_ref
  220.0 0.7 halves.2
  220.8 2.0 collective-permute-start.6
  222.7 1.5 collective-permute-start.7
  224.2 0.3 add.16
  224.6 1.1 copy-done.4
  225.6 1.4 collective-permute-start.11
  227.1 1.6 add.15
  228.7 0.9 collective-permute-start.10
  229.5 15.2 %collective-permute-done.refs_0_ = bf16[4,192,768]{2,1,0:T(8,128)(2,1)S(1)} collective-permute-done((bf16[4,192,768]{2,1,0:T(8,128)(2,1)S(1)}, bf16[4,192,768]{2,1,0:T(8,128)(2,1)S(1)}, u32[]{:S(2)}, u32[]{:S(2)}) %collective-permute-start) | collective-permute-done | bytes 1179680 | tf_op jit(solution)/shard_map/ppermute | solution.py:908
  244.7 1.1 copy-done.14
  245.8 0.4 halves.3
  246.2 1.8 collective-permute-start.8
  248.0 1.5 collective-permute-start.9
  249.4 6.7 %project_back.1 = bf16[1024,768]{1,0:T(8,128)(2,1)} custom-call(bf16[3,1024,768]{2,1,0:T(8,128)(2,1)S(1)} %attend_back.1.grads_ref, bf16[1024,768]{1,0:T(8,128)(2,1)S(1)} %copy-done.23, f32[1024,768]{1,0:T(8,128)S(1)} %copy-done.28, bf16[768,2304]{1,0:T(8,128)(2,1)S(1)} %copy-done.8, f32[4,768]{1,0:T(4,128)S(1)} %copy-done.21), custom_call_target="tpu_custom_call" | custom-call | flops 10871635968 | bytes 47185920 | tf_op jit(solution)/shard_map/project_back/pallas_call | solution.py:806
  256.1 0.7 collective-permute-done.11.refs_2_
  256.8 1.0 copy-done.16
  257.8 1.0 copy-done.18
  259.0 0.8 copy-done.10
  259.9 6.7 %all-to-all-start.3 = ((bf16[4,208,384]{2,1,0:T(8,128)(2,1)}), bf16[4,208,384]{2,1,0:T(8,128)(2,1)S(1)}, u32[]{:S(2)}, u32[]{:S(2)}) async-start(bf16[4,208,384]{2,1,0:T(8,128)(2,1)} %copy-done.10), calls=%async_computation.3 | async-start | bytes 1277952 | tf_op jit(solution)/shard_map/all_to_all | solution.py:1125
  266.6 1.7 copy-done.5
  268.2 1.2 add.18
  269.4 1.3 collective-permute-start.14
  270.7 2.2 add.17
  272.9 1.7 collective-permute-start.13
  274.6 9.8 %collective-permute-start.12 = (bf16[4,192,768]{2,1,0:T(8,128)(2,1)}, bf16[4,192,768]{2,1,0:T(8,128)(2,1)}, u32[]{:S(2)}, u32[]{:S(2)}) collective-permute-start(bf16[4,192,768]{2,1,0:T(8,128)(2,1)} %get-tuple-element.140.middle_ref), channel_id=1, source_target_pairs={{0,8},{24,16},{1,9},{25,17},{2,10},{26,18},{3,11},{27,19},{4,12},{... | collective-permute-start | bytes 3538952 | tf_op jit(solution)/shard_map/ppermute | solution.py:908
  284.5 1.0 copy-done.6
  285.5 4.4 %all-to-all-start.4 = ((bf16[8,208,384]{2,1,0:T(8,128)(2,1)}), bf16[8,208,384]{2,1,0:T(8,128)(2,1)}, u32[]{:S(2)}, u32[]{:S(2)}) async-start(bf16[8,208,384]{2,1,0:T(8,128)(2,1)} %copy-done.6), calls=%async_computation.4 | async-start | bytes 2555904 | tf_op jit(solution)/shard_map/all_to_all | solution.py:1125
  290.0 1.3 copy-done.15
  291.2 1.3 copy-done.17
  292.5 1.3 copy-done.19
  293.8 1.7 line_total.3
  295.5 12.3 %all-to-all-done.4.gathered_ref = bf16[8,208,384]{2,1,0:T(8,128)(2,1)} async-done(((bf16[8,208,384]{2,1,0:T(8,128)(2,1)}), bf16[8,208,384]{2,1,0:T(8,128)(2,1)}, u32[]{:S(2)}, u32[]{:S(2)}) %all-to-all-start.4) | async-done | bytes 1277984 | tf_op jit(solution)/shard_map/all_to_all | solution.py:1125
  307.8 2.0 copy-done.9
  309.8 3.1 assemble.1
  313.2 1.3 dynamic-slice_divide_fusion
  314.5 0.6 fusion
  315.1 3.7 %line_total.2 = f32[192,3072]{1,0:T(8,128)} custom-call(s32[1]{0:T(128)} %bitcast.1.place_ref, bf16[4,192,768]{2,1,0:T(8,128)(2,1)} %get-tuple-element.140.middle_ref, bf16[8,192,768]{2,1,0:T(8,128)(2,1)S(1)} %copy-done, bf16[4,192,768]{2,1,0:T(8,128)(2,1)} %collective-permute-done.12.refs_0_, bf16[4,192,768]{2,1,0:T(8,128)(2,1)} %collective-permute-done.13.refs_1_, ...), custom_call_target="tpu_custom_call" | custom-call | tf_op jit(solution)/shard_map/line_total/pallas_call | solution.py:862
  (82 shorter events, 0.8 us)
Async XLA Ops:
  6.5 5.3 %copy-start.34 = (f32[768]{0:T(1024)S(1)}, f32[768]{0:T(1024)}, u32[]{:S(2)}) copy-start(f32[768]{0:T(1024)} %param.19) | copy-start | bytes 9220
  6.5 5.4 %copy-start.33 = (f32[768]{0:T(1024)S(1)}, f32[768]{0:T(1024)}, u32[]{:S(2)}) copy-start(f32[768]{0:T(1024)} %param.20) | copy-start | bytes 9220
  6.5 5.4 %copy-start.36 = (f32[768]{0:T(1024)S(1)}, f32[768]{0:T(1024)}, u32[]{:S(2)}) copy-start(f32[768]{0:T(1024)} %param.21) | copy-start | bytes 9220
  6.5 5.4 %copy-start.37 = (f32[768]{0:T(1024)S(1)}, f32[768]{0:T(1024)}, u32[]{:S(2)}) copy-start(f32[768]{0:T(1024)} %param.22) | copy-start | bytes 9220
  6.5 5.4 %copy-start.22 = (bf16[1024,768]{1,0:T(8,128)(2,1)S(1)}, bf16[1024,768]{1,0:T(8,128)(2,1)}, u32[]{:S(2)}) copy-start(bf16[1024,768]{1,0:T(8,128)(2,1)} %tokens_ref.6) | copy-start | bytes 4718596
  6.5 29.9 %all-to-all-start = ((bf16[8,128,768]{2,1,0:T(8,128)(2,1)}), bf16[8,128,768]{2,1,0:T(8,128)(2,1)}, u32[]{:S(2)}, u32[]{:S(2)}) async-start(bf16[8,128,768]{2,1,0:T(8,128)(2,1)} %bitcast.19), calls=%async_computation | async-start | bytes 3145728 | tf_op jit(solution)/shard_map/all_to_all | solution.py:1125
  11.9 2.0 copy-start.7
  13.9 5.2 %copy-start.20 = (f32[4,768]{1,0:T(4,128)}, f32[4,768]{1,0:T(4,128)S(1)}, u32[]{:S(2)}) copy-start(f32[4,768]{1,0:T(4,128)S(1)} %pad_maximum_fusion.norms_ref) | copy-start | bytes 36868
  33.0 2.2 copy-start.24
  35.2 1.1 copy-start.26
  44.4 25.3 %all-to-all-start.1 = ((bf16[8,128,768]{2,1,0:T(8,128)(2,1)}), bf16[8,128,768]{2,1,0:T(8,128)(2,1)S(1)}, u32[]{:S(2)}, u32[]{:S(2)}) async-start(bf16[8,128,768]{2,1,0:T(8,128)(2,1)} %bitcast.20), calls=%async_computation.1 | async-start | bytes 3145728 | tf_op jit(solution)/shard_map/all_to_all | solution.py:1125
  69.7 1.1 copy-start.32
  109.2 10.0 %copy-start.1 = (bf16[8,192,768]{2,1,0:T(8,128)(2,1)S(1)}, bf16[8,192,768]{2,1,0:T(8,128)(2,1)}, u32[]{:S(2)}) copy-start(bf16[8,192,768]{2,1,0:T(8,128)(2,1)} %get-tuple-element.102.left_ref) | copy-start | bytes 7077892
  109.2 42.5 %all-to-all-start.2 = ((bf16[8,128,1536]{2,1,0:T(8,128)(2,1)}), bf16[8,128,1536]{2,1,0:T(8,128)(2,1)}, u32[]{:S(2)}, u32[]{:S(2)}) async-start(bf16[8,128,1536]{2,1,0:T(8,128)(2,1)} %bitcast.15), calls=%async_computation.2 | async-start | bytes 6291456 | tf_op jit(solution)/shard_map/all_to_all | solution.py:1125
  113.8 55.8 %collective-permute-start.1 = (bf16[8,192,768]{2,1,0:T(8,128)(2,1)}, bf16[8,192,768]{2,1,0:T(8,128)(2,1)}, u32[]{:S(2)}, u32[]{:S(2)}) collective-permute-start(bf16[8,192,768]{2,1,0:T(8,128)(2,1)} %get-tuple-element.96.left_ref), channel_id=1, source_target_pairs={{0,8},{24,16},{1,9},{25,17},{2,10},{26,18},{3,11},{27,19},{4,12},{... | collective-permute-start | bytes 7077896 | tf_op jit(solution)/shard_map/ppermute | solution.py:908
  119.1 100.9 %collective-permute-start.3 = (bf16[8,192,768]{2,1,0:T(8,128)(2,1)S(1)}, bf16[8,192,768]{2,1,0:T(8,128)(2,1)}, u32[]{:S(2)}, u32[]{:S(2)}) collective-permute-start(bf16[8,192,768]{2,1,0:T(8,128)(2,1)S(1)} %copy-done.1), channel_id=1, source_target_pairs={{0,8},{24,16},{1,9},{25,17},{2,10},{26,18},{3,11},{27,19},{4,12},{... | collective-permute-start | bytes 7077896 | tf_op jit(solution)/shard_map/ppermute | solution.py:908
  169.6 1.7 copy-start.11
  171.2 3.1 copy-start.27
  171.2 3.1 copy-start.30
  173.3 50.9 %collective-permute-start.2 = (bf16[8,192,768]{2,1,0:T(8,128)(2,1)S(1)}, bf16[8,192,768]{2,1,0:T(8,128)(2,1)S(1)}, u32[]{:S(2)}, u32[]{:S(2)}) collective-permute-start(bf16[8,192,768]{2,1,0:T(8,128)(2,1)S(1)} %add.14), channel_id=1, source_target_pairs={{8,16},{16,8},{9,17},{17,9},{10,18},{18,10},{11,19},{19,11},{12,20... | collective-permute-start | bytes 7077896 | tf_op jit(solution)/shard_map/ppermute | solution.py:908
  174.4 2.3 copy-start.25
  176.7 26.5 %copy-start.21 = (f32[4,768]{1,0:T(4,128)S(1)}, f32[4,768]{1,0:T(4,128)}, u32[]{:S(2)}) copy-start(f32[4,768]{1,0:T(4,128)} %copy-done.20) | copy-start | bytes 36868
  176.7 26.5 %copy-start.23 = (bf16[1024,768]{1,0:T(8,128)(2,1)S(1)}, bf16[1024,768]{1,0:T(8,128)(2,1)}, u32[]{:S(2)}) copy-start(bf16[1024,768]{1,0:T(8,128)(2,1)} %tokens_ref.6) | copy-start | bytes 4718596
  176.7 26.5 %copy-start.29 = (bf16[768,768]{1,0:T(8,128)(2,1)S(1)}, bf16[768,768]{1,0:T(8,128)(2,1)}, u32[]{:S(2)}) copy-start(bf16[768,768]{1,0:T(8,128)(2,1)} %get-tuple-element.103.output_grad_ref) | copy-start | bytes 3538948
  176.7 26.5 %copy-start.31 = (f32[8,768]{1,0:T(8,128)S(1)}, f32[8,768]{1,0:T(8,128)}, u32[]{:S(2)}) copy-start(f32[8,768]{1,0:T(8,128)} %get-tuple-element.104.second_ref) | copy-start | bytes 73732
  203.2 7.3 %copy-start.12 = (bf16[4,192,768]{2,1,0:T(8,128)(2,1)S(1)}, bf16[4,192,768]{2,1,0:T(8,128)(2,1)}, u32[]{:S(2)}) copy-start(bf16[4,192,768]{2,1,0:T(8,128)(2,1)} %get-tuple-element.94.middle_ref) | copy-start | bytes 3538948
  209.9 10.1 %collective-permute-start.4 = (bf16[4,448,384]{2,1,0:T(8,128)(2,1)S(1)}, bf16[4,448,384]{2,1,0:T(8,128)(2,1)S(1)}, u32[]{:S(2)}, u32[]{:S(2)}) collective-permute-start(bf16[4,448,384]{2,1,0:T(8,128)(2,1)S(1)} %get-tuple-element.106), channel_id=1, source_target_pairs={{0,1},{1,0},{2,3},{3,2},{4,5},{5,4},{6,7},{7,6},{8,9},{9,8},{10,11... | collective-permute-start | bytes 4128776 | tf_op jit(solution)/shard_map/ppermute | solution.py:1168
  210.0 10.0 %collective-permute-start.5 = (bf16[4,384,384]{2,1,0:T(8,128)(2,1)S(1)}, bf16[4,384,384]{2,1,0:T(8,128)(2,1)S(1)}, u32[]{:S(2)}, u32[]{:S(2)}) collective-permute-start(bf16[4,384,384]{2,1,0:T(8,128)(2,1)S(1)} %get-tuple-element.108), channel_id=1, source_target_pairs={{0,1},{1,0},{2,3},{3,2},{4,5},{5,4},{6,7},{7,6},{8,9},{9,8},{10,11... | collective-permute-start | bytes 3538952 | tf_op jit(solution)/shard_map/ppermute | solution.py:1168
  210.5 34.2 %collective-permute-start = (bf16[4,192,768]{2,1,0:T(8,128)(2,1)S(1)}, bf16[4,192,768]{2,1,0:T(8,128)(2,1)S(1)}, u32[]{:S(2)}, u32[]{:S(2)}) collective-permute-start(bf16[4,192,768]{2,1,0:T(8,128)(2,1)S(1)} %copy-done.12), channel_id=1, source_target_pairs={{0,8},{24,16},{1,9},{25,17},{2,10},{26,18},{3,11},{27,19},{4,12},{... | collective-permute-start | bytes 3538952 | tf_op jit(solution)/shard_map/ppermute | solution.py:908
  220.0 4.2 %copy-start = (bf16[8,192,768]{2,1,0:T(8,128)(2,1)S(1)}, bf16[8,192,768]{2,1,0:T(8,128)(2,1)}, u32[]{:S(2)}) copy-start(bf16[8,192,768]{2,1,0:T(8,128)(2,1)} %get-tuple-element.124.left_ref.end_ref) | copy-start | bytes 7077892
  220.8 25.0 %collective-permute-start.6 = (bf16[4,224,384]{2,1,0:T(8,128)(2,1)S(1)}, bf16[4,224,384]{2,1,0:T(8,128)(2,1)S(1)}, u32[]{:S(2)}, u32[]{:S(2)}) collective-permute-start(bf16[4,224,384]{2,1,0:T(8,128)(2,1)S(1)} %get-tuple-element.115), channel_id=1, source_target_pairs={{0,2},{1,3},{2,0},{3,1},{4,6},{5,7},{6,4},{7,5},{8,10},{9,11},{10,... | collective-permute-start | bytes 2064392 | tf_op jit(solution)/shard_map/ppermute | solution.py:1168
  222.7 23.1 %collective-permute-start.7 = (bf16[4,192,384]{2,1,0:T(8,128)(2,1)S(1)}, bf16[4,192,384]{2,1,0:T(8,128)(2,1)S(1)}, u32[]{:S(2)}, u32[]{:S(2)}) collective-permute-start(bf16[4,192,384]{2,1,0:T(8,128)(2,1)S(1)} %get-tuple-element.117), channel_id=1, source_target_pairs={{0,4},{1,5},{2,6},{3,7},{4,0},{5,1},{6,2},{7,3},{8,12},{9,13},{10,... | collective-permute-start | bytes 1769480 | tf_op jit(solution)/shard_map/ppermute | solution.py:1168
  224.2 1.4 copy-start.4
  224.2 2.8 copy-start.2
  225.6 31.2 %collective-permute-start.11 = (bf16[4,192,768]{2,1,0:T(8,128)(2,1)S(1)}, bf16[4,192,768]{2,1,0:T(8,128)(2,1)S(1)}, u32[]{:S(2)}, u32[]{:S(2)}) collective-permute-start(bf16[4,192,768]{2,1,0:T(8,128)(2,1)S(1)} %add.16), channel_id=1, source_target_pairs={{16,24},{8,0},{17,25},{9,1},{18,26},{10,2},{19,27},{11,3},{20,28},... | collective-permute-start | bytes 3538952 | tf_op jit(solution)/shard_map/ppermute | solution.py:908
  227.1 22.4 %copy-start.8 = (bf16[768,2304]{1,0:T(8,128)(2,1)S(1)}, bf16[768,2304]{1,0:T(8,128)(2,1)}, u32[]{:S(2)}) copy-start(bf16[768,2304]{1,0:T(8,128)(2,1)} %weight_ref.9) | copy-start | bytes 10616836
  227.1 22.4 %copy-start.28 = (f32[1024,768]{1,0:T(8,128)S(1)}, f32[1024,768]{1,0:T(8,128)}, u32[]{:S(2)}) copy-start(f32[1024,768]{1,0:T(8,128)} %get-tuple-element.100.residual_grad_ref) | copy-start | bytes 9437188
  228.7 29.2 %collective-permute-start.10 = (bf16[4,192,768]{2,1,0:T(8,128)(2,1)S(1)}, bf16[4,192,768]{2,1,0:T(8,128)(2,1)S(1)}, u32[]{:S(2)}, u32[]{:S(2)}) collective-permute-start(bf16[4,192,768]{2,1,0:T(8,128)(2,1)S(1)} %add.15), channel_id=1, source_target_pairs={{8,16},{16,8},{9,17},{17,9},{10,18},{18,10},{11,19},{19,11},{12,20... | collective-permute-start | bytes 3538952 | tf_op jit(solution)/shard_map/ppermute | solution.py:908
  244.7 1.1 copy-start.14
  246.2 9.9 %collective-permute-start.8 = (bf16[4,112,384]{2,1,0:T(8,128)(2,1)S(1)}, bf16[4,112,384]{2,1,0:T(8,128)(2,1)S(1)}, u32[]{:S(2)}, u32[]{:S(2)}) collective-permute-start(bf16[4,112,384]{2,1,0:T(8,128)(2,1)S(1)} %get-tuple-element.119), channel_id=1, source_target_pairs={{0,4},{1,5},{2,6},{3,7},{4,0},{5,1},{6,2},{7,3},{8,12},{9,13},{10,... | collective-permute-start | bytes 1032200 | tf_op jit(solution)/shard_map/ppermute | solution.py:1168
  248.0 8.2 %collective-permute-start.9 = (bf16[4,96,384]{2,1,0:T(8,128)(2,1)S(1)}, bf16[4,96,384]{2,1,0:T(8,128)(2,1)S(1)}, u32[]{:S(2)}, u32[]{:S(2)}) collective-permute-start(bf16[4,96,384]{2,1,0:T(8,128)(2,1)S(1)} %get-tuple-element.121), channel_id=1, source_target_pairs={{0,2},{1,3},{2,0},{3,1},{4,6},{5,7},{6,4},{7,5},{8,10},{9,11},{10,... | collective-permute-start | bytes 884744 | tf_op jit(solution)/shard_map/ppermute | solution.py:1168
  256.8 1.0 copy-start.16
  257.8 1.0 copy-start.18
  259.0 0.8 copy-start.10
  259.9 24.5 %all-to-all-start.3 = ((bf16[4,208,384]{2,1,0:T(8,128)(2,1)}), bf16[4,208,384]{2,1,0:T(8,128)(2,1)S(1)}, u32[]{:S(2)}, u32[]{:S(2)}) async-start(bf16[4,208,384]{2,1,0:T(8,128)(2,1)} %copy-done.10), calls=%async_computation.3 | async-start | bytes 1277952 | tf_op jit(solution)/shard_map/all_to_all | solution.py:1125
  266.6 1.7 copy-start.5
  268.2 2.5 copy-start.3
  269.4 43.5 %collective-permute-start.14 = (bf16[4,192,768]{2,1,0:T(8,128)(2,1)}, bf16[4,192,768]{2,1,0:T(8,128)(2,1)}, u32[]{:S(2)}, u32[]{:S(2)}) collective-permute-start(bf16[4,192,768]{2,1,0:T(8,128)(2,1)} %add.18), channel_id=1, source_target_pairs={{16,24},{8,0},{17,25},{9,1},{18,26},{10,2},{19,27},{11,3},{20,28},... | collective-permute-start | bytes 3538952 | tf_op jit(solution)/shard_map/ppermute | solution.py:908
  272.9 40.0 %collective-permute-start.13 = (bf16[4,192,768]{2,1,0:T(8,128)(2,1)}, bf16[4,192,768]{2,1,0:T(8,128)(2,1)}, u32[]{:S(2)}, u32[]{:S(2)}) collective-permute-start(bf16[4,192,768]{2,1,0:T(8,128)(2,1)} %add.17), channel_id=1, source_target_pairs={{8,16},{16,8},{9,17},{17,9},{10,18},{18,10},{11,19},{19,11},{12,20... | collective-permute-start | bytes 3538952 | tf_op jit(solution)/shard_map/ppermute | solution.py:908
  274.6 38.3 %collective-permute-start.12 = (bf16[4,192,768]{2,1,0:T(8,128)(2,1)}, bf16[4,192,768]{2,1,0:T(8,128)(2,1)}, u32[]{:S(2)}, u32[]{:S(2)}) collective-permute-start(bf16[4,192,768]{2,1,0:T(8,128)(2,1)} %get-tuple-element.140.middle_ref), channel_id=1, source_target_pairs={{0,8},{24,16},{1,9},{25,17},{2,10},{26,18},{3,11},{27,19},{4,12},{... | collective-permute-start | bytes 3538952 | tf_op jit(solution)/shard_map/ppermute | solution.py:908
  284.5 1.0 copy-start.6
  285.5 4.4 %copy-start.13 = (bf16[4,192,768]{2,1,0:T(8,128)(2,1)S(1)}, bf16[4,192,768]{2,1,0:T(8,128)(2,1)}, u32[]{:S(2)}) copy-start(bf16[4,192,768]{2,1,0:T(8,128)(2,1)} %get-tuple-element.94.middle_ref) | copy-start | bytes 3538948
  285.5 22.3 %all-to-all-start.4 = ((bf16[8,208,384]{2,1,0:T(8,128)(2,1)}), bf16[8,208,384]{2,1,0:T(8,128)(2,1)}, u32[]{:S(2)}, u32[]{:S(2)}) async-start(bf16[8,208,384]{2,1,0:T(8,128)(2,1)} %copy-done.6), calls=%async_computation.4 | async-start | bytes 2555904 | tf_op jit(solution)/shard_map/all_to_all | solution.py:1125
  290.0 1.3 copy-start.15
  291.2 1.3 copy-start.17
  292.5 1.3 copy-start.19
  307.8 2.0 copy-start.9
  313.1 5.7 %copy-start.35 = (f32[192]{0:T(256)}, f32[192]{0:T(256)S(1)}, u32[]{:S(2)}) copy-start(f32[192]{0:T(256)S(1)} %get-tuple-element.152) | copy-start | bytes 2308
where the time goes:
time: 320 us; the launch traced here: 319 us
  Pallas kernels  142 us (44%)
  waiting for transfers between devices  85 us (27%)
  starting transfers between devices  63.7 us (20%)
  local copies, waits for them, and re-layouts  24.9 us (8%)
    all_to_all x5, waiting for transfers between devices, exchange(): return lax.all_to_all(values, axis, split_axis=0, concat_axis=0, tiled=True)  63.2 us
    pallas_call x1, Pallas kernels, expert(): pl.pallas_call(functools.partial(expert_kernel, shares=shares, together=t...  38.3 us
    ppermute x9, starting transfers between devices, send(): self.got[key] = lax.ppermute(values, self.axis, route)  31.2 us
    pallas_call x1, Pallas kernels, attend_back(): pl.pallas_call(functools.partial(attend_back_kernel, scale=size ** (-0.5)...  26.5 us
    all_to_all x5, starting transfers between devices, exchange(): return lax.all_to_all(values, axis, split_axis=0, concat_axis=0, tiled=True)  25.3 us
    unnamed x76, local copies, waits for them, and re-layouts  24 us
    ppermute x9, waiting for transfers between devices, send(): self.got[key] = lax.ppermute(values, self.axis, route)  21.8 us
    pallas_call x1, Pallas kernels, combine(): pl.pallas_call(combine_kernel, out_shape=[jax.ShapeDtypeStruct((rows, wid...  14.4 us
  transfers between devices with their start and end apart: 20, of which 7 were waited for; matrix products, arithmetic and copies ran while one was open for 0% of the time, Pallas kernels for 27%

commit v1 on v0

--- a/solution.py
+++ b/solution.py
@@ -16,6 +16,7 @@
 SEEN = 1
 EXPERT_MIB = 54
 HIDDEN_MIB = 60
+OWN_EARLY = True
 
 
 def dot(left, right, left_axis=1, right_axis=0):
@@ -274,7 +275,8 @@
         query = jnp.where(mine, query_ref[start:end, :] * jnp.asarray(scale, BF), zero)
         grad = jnp.where(mine, incoming, zero)
         inner = jnp.sum(jnp.where(mine, product, 0.0), axis=1, keepdims=True)
-        at = lax.broadcasted_iota(jnp.int32, (1, 128), 1) == 2 * pl.program_id(0) + head
+        number = 2 * pl.program_id(0) + head
+        at = lax.broadcasted_iota(jnp.int32, (1, 128), 1) == number
         total = jnp.sum(jnp.where(at, total_ref[start:end, :], 0.0), axis=1, keepdims=True)
         spare = jnp.where(lane == other + 3, bias[:end], ones)
         key = jnp.where(mine, key_ref[:end, :], spare)
@@ -322,7 +324,7 @@
         ),
         compiler_params=params(24),
         cost_estimate=cost(
-            30 * rows * rows * width, 20 * rows * width, HEADS * rows * rows // 2
+            30 * rows * rows * width, 20 * rows * width
         ),
         name="attend_back",
     )(length, projected, projected, projected, mixed, total, incoming)
@@ -434,15 +436,16 @@
     centroids_ref,
     up_ref,
     down_ref,
+    produced_ref,
     back_ref,
     *refs,
     shares,
     together,
 ):
-    outs, scratch = refs[:-7], refs[-7:]
-    produced_sum, back_sum, transposed, gradient, downs, ups, sems = scratch
+    outs, scratch = refs[:-8], refs[-8:]
+    produced_sum, back_sum, transposed, gradient, gates, downs, ups, sems = scratch
     step = pl.program_id(0)
-    width = rows_ref.shape[1]
+    count, width = rows_ref.shape
     share = width // shares
 
     @pl.when(step == 0)
@@ -451,6 +454,7 @@
         centroid = centroids_ref[pl.ds(me_ref[0], 1), :]
         gate = jax.nn.sigmoid(jnp.sum(hidden * centroid, axis=-1, keepdims=True))
         gradient[...] = (gate * cotangent_ref[...].astype(F32)).astype(BF)
+        gates[...] = jnp.broadcast_to(gate, gates.shape)
         produced_sum[...] = jnp.zeros_like(produced_sum)
         back_sum[...] = jnp.zeros_like(back_sum)
         values = rows_ref[...].T
@@ -504,8 +508,18 @@
 
     @pl.when(step == pl.num_programs(0) - 1)
     def _():
-        back_ref[:, :width] = produced_sum[...].astype(BF)
-        back_ref[:, width:] = back_sum[...].astype(BF)
+        centroid = centroids_ref[pl.ds(me_ref[0], 1), :]
+
+        @pl.loop(0, count // 256)
+        def _(number):
+            at = pl.ds(pl.multiple_of(number * 256, 256), 256)
+            produced = produced_sum[at, :].astype(BF)
+            produced_ref[at, :] = produced
+            gate = gates[at, 0:1]
+            cotangent = cotangent_ref[at, :].astype(F32)
+            along = jnp.sum(cotangent * produced.astype(F32), axis=-1, keepdims=True)
+            logit_gradient = along * gate * (1.0 - gate)
+            back_ref[at, :] = (back_sum[at, :] + logit_gradient * centroid).astype(BF)
         wait(1 - slot)
         wait(slot)
 
@@ -541,7 +555,7 @@
             shapes += [(pieces, share, width), (shares, share, chunk)]
     outs = pl.pallas_call(
         functools.partial(expert_kernel, shares=shares, together=together),
-        out_shape=[jax.ShapeDtypeStruct((count, 2 * width), BF)]
+        out_shape=[jax.ShapeDtypeStruct((count, width), BF)] * 2
         + [jax.ShapeDtypeStruct(shape, BF) for shape in shapes],
         grid_spec=pltpu.PrefetchScalarGridSpec(
             num_scalar_prefetch=2,
@@ -553,13 +567,13 @@
                 pl.BlockSpec((width, chunk), lambda c, m, p: (0, real(c, p))),
                 pl.BlockSpec((chunk, width), lambda c, m, p: (real(c, p), 0)),
             ],
-            out_specs=[pl.BlockSpec((count, 2 * width), still, pipeline_mode=once)]
-            + [pl.BlockSpec(memory_space=pl.ANY)] * len(shapes),
+            out_specs=[whole, whole] + [pl.BlockSpec(memory_space=pl.ANY)] * len(shapes),
             scratch_shapes=[
                 pltpu.VMEM((count, width), F32),
                 pltpu.VMEM((count, width), F32),
                 pltpu.VMEM((width, count), BF),
                 pltpu.VMEM((count, width), BF),
+                pltpu.VMEM((count, 128), F32),
                 pltpu.VMEM((2, pieces, share, width), BF),
                 pltpu.VMEM((2, shares, share, chunk), BF),
                 pltpu.SemaphoreType.DMA((2, shares + 1)),
@@ -569,8 +583,9 @@
         cost_estimate=cost(12 * count * width * inner, 8 * inner * width, 2 * count * inner),
         name="expert",
     )(me, place, hidden, cotangent, centroids, up, down)
-    back, arrays = outs[0], outs[1:]
-    return back, [[(arrays[number], first) for number, first in pair] for pair in places]
+    arrays = outs[2:]
+    pairs = [[(arrays[number], first) for number, first in pair] for pair in places]
+    return outs[0], outs[1], pairs
 
 
 def combine_kernel(
@@ -579,12 +594,9 @@
     column_ref,
     cotangent_ref,
     residual_ref,
-    gate_ref,
     norms_ref,
-    centroids_ref,
     mixed_ref,
     weight_ref,
-    layer_ref,
     residual_grad_ref,
     mixed_grad_ref,
     weight_grad_ref,
@@ -592,32 +604,19 @@
     weight_sum,
 ):
     step = pl.program_id(0)
-    count, width = cotangent_ref.shape
-    slots = returned_ref.shape[0]
+    count = cotangent_ref.shape[0]
 
     @pl.when(step == 0)
     def _():
         weight_sum[...] = jnp.zeros_like(weight_sum)
         gains_ref[...] = jnp.zeros_like(gains_ref)
 
-    target = column_ref[:, 0:1]
-    place = lax.broadcasted_iota(jnp.int32, (count, slots), 1)
-    chosen = jnp.where(place == target, 1.0, 0.0).astype(BF)
-    term = dot(chosen, returned_ref[:, :width])
-    back = dot(chosen, returned_ref[:, width:])
+    hidden_gradient = gathered_rows(column_ref, returned_ref)
     mask = present_rows(step, count, length_ref[0])
-    gate = gate_ref[:, 0:1]
-    cotangent = cotangent_ref[...].astype(F32)
-    residual = residual_ref[...]
-    layer_ref[...] = (residual + mask * gate * term).astype(BF)
-    along = jnp.sum(cotangent * term, axis=-1, keepdims=True)
-    logit_gradient = mask * along * gate * (1.0 - gate)
-    picked = picked_rows(column_ref[...], centroids_ref, slots // centroids_ref.shape[0])
-    hidden_gradient = back + logit_gradient * picked
-    normal, inverse = normalise(residual)
+    normal, inverse = normalise(residual_ref[...])
     gains_ref[0:1, :] += jnp.sum(hidden_gradient * normal, axis=0, keepdims=True)
     gains_ref[1:2, :] += jnp.sum(hidden_gradient, axis=0, keepdims=True)
-    residual_gradient = cotangent + norm_backward(
+    residual_gradient = cotangent_ref[...].astype(F32) + norm_backward(
         normal, inverse, norms_ref[2:3, :], hidden_gradient
     )
     residual_grad_ref[...] = residual_gradient
@@ -630,11 +629,14 @@
         weight_grad_ref[...] = weight_sum[...].astype(BF)
 
 
-def combine(
-    length, returned, target_column, cotangent, residual, gate, norms, centroids, mixed, weight
-):
+def gathered_rows(column_ref, slots_ref):
+    place = lax.broadcasted_iota(jnp.int32, (column_ref.shape[0], slots_ref.shape[0]), 1)
+    chosen = jnp.where(place == column_ref[:, 0:1], 1.0, 0.0).astype(BF)
+    return dot(chosen, slots_ref[...])
+
+
+def combine(length, returned, target_column, cotangent, residual, norms, mixed, weight):
     rows, width = cotangent.shape
-    experts = centroids.shape[0]
     block = 256
     part = pl.BlockSpec((block, width), lambda i, l: (i, 0))
     thin = pl.BlockSpec((block, 128), lambda i, l: (i, 0))
@@ -642,7 +644,6 @@
     return pl.pallas_call(
         combine_kernel,
         out_shape=[
-            jax.ShapeDtypeStruct((rows, width), BF),
             jax.ShapeDtypeStruct((rows, width), F32),
             jax.ShapeDtypeStruct((rows, width), BF),
             jax.ShapeDtypeStruct((width, width), BF),
@@ -652,20 +653,17 @@
             num_scalar_prefetch=1,
             grid=(rows // block,),
             in_specs=[
-                pl.BlockSpec((rows, 2 * width), still),
+                pl.BlockSpec((rows, width), still),
                 thin,
                 part,
                 part,
-                thin,
                 pl.BlockSpec((4, width), still),
-                pl.BlockSpec((experts, width), still),
                 part,
                 pl.BlockSpec((width, width), still),
             ],
             out_specs=[
                 part,
                 part,
-                part,
                 pl.BlockSpec((width, width), still),
                 pl.BlockSpec((8, width), still),
             ],
@@ -674,18 +672,33 @@
         compiler_params=params(60),
         cost_estimate=cost(4 * rows * (rows + width) * width, 24 * rows * width),
         name="combine",
-    )(
-        length,
-        returned,
-        target_column,
-        cotangent,
-        residual,
-        gate,
-        norms,
-        centroids,
-        mixed,
-        weight,
-    )
+    )(length, returned, target_column, cotangent, residual, norms, mixed, weight)
+
+
+def layer_kernel(length_ref, returned_ref, column_ref, residual_ref, gate_ref, out_ref):
+    term = gathered_rows(column_ref, returned_ref)
+    mask = present_rows(pl.program_id(0), column_ref.shape[0], length_ref[0])
+    out_ref[...] = (residual_ref[...] + mask * gate_ref[:, 0:1] * term).astype(BF)
+
+
+def layer(length, returned, target_column, residual, gate):
+    rows, width = residual.shape
+    block = 256
+    part = pl.BlockSpec((block, width), lambda i, l: (i, 0))
+    thin = pl.BlockSpec((block, 128), lambda i, l: (i, 0))
+    return pl.pallas_call(
+        layer_kernel,
+        out_shape=jax.ShapeDtypeStruct((rows, width), BF),
+        grid_spec=pltpu.PrefetchScalarGridSpec(
+            num_scalar_prefetch=1,
+            grid=(rows // block,),
+            in_specs=[pl.BlockSpec((rows, width), lambda i, l: (0, 0)), thin, part, thin],
+            out_specs=part,
+        ),
+        compiler_params=params(60),
+        cost_estimate=cost(2 * rows * rows * width, 10 * rows * width),
+        name="layer",
+    )(length, returned, target_column, residual, gate)
 
 
 def packed_rows(share, devices):
@@ -724,8 +737,10 @@
 
     @pl.when(step == 0)
     def _():
-        for first in range(0, tokens_ref.shape[0], 256):
-            at = slice(first, first + 256)
+
+        @pl.loop(0, tokens_ref.shape[0] // 256)
+        def _(number):
+            at = pl.ds(pl.multiple_of(number * 256, 256), 256)
             normal, _ = normalise(tokens_ref[at, :].astype(F32))
             low = (normal * norms_ref[0:1, :] + norms_ref[1:2, :]).astype(BF)
             normed[:, at] = low.T
@@ -811,7 +826,7 @@
         + [pl.BlockSpec(weight.shape, lambda i: (0, 0)), pl.BlockSpec((4, width), lambda i: (0, 0))],
         out_specs=part,
         compiler_params=params(24),
-        cost_estimate=cost(18 * rows * width * width, 60 * rows * width),
+        cost_estimate=cost(1.8 * rows * width * width, 6 * rows * width),
         name="project_back",
     )(grads, tokens, residual_grad, weight, norms)
 
@@ -868,7 +883,7 @@
             in_specs=[spec(first) for _, first in ins],
             out_specs=pl.BlockSpec(block, lambda a, p: (0, a) if across else (a, 0)),
         ),
-        compiler_params=params(16),
+        compiler_params=params(60),
         cost_estimate=cost(0, 0),
         name="line_total",
     )(place, *[array for array, _ in ins])
@@ -952,7 +967,7 @@
             out[...] = total.astype(BF)
 
 
-def halves(me, bits, edges, pairs):
+def halves(me, bits, edges, pairs, level):
     shares = pairs[0][0].shape[0]
     spec = lambda rows, columns: pl.BlockSpec((1, rows, columns), lambda z, m: (z, 0, 0))
     in_specs, out_specs, out_shape = [], [], []
@@ -971,7 +986,7 @@
             num_scalar_prefetch=1, grid=(shares,), in_specs=in_specs, out_specs=out_specs
         ),
         compiler_params=params(20),
-        cost_estimate=cost(0, 0),
+        cost_estimate=cost(0, 60 * size * level),
         name="halves",
     )(me, *[array for pair in pairs for array in pair])
     return [(outs[2 * i], outs[2 * i + 1]) for i in range(len(bits))]
@@ -1140,28 +1155,22 @@
     )
     arrived = dispatch(outgoing)
     order = place if shares == LINE else jnp.full_like(place, shares)
-    back, pairs = expert(
+    produced, back, pairs = expert(
         me, order, arrived, arrived_cotangent, centroids, up_weight[0], down_weight[0], shares
     )
     line = LineSum(pairs, "dp", place)
     line.send("far")
     line.send("near")
-    returned = dispatch(back)
-    layer_output, residual_grad, mixed_grad, output_grad, second_gains = combine(
-        lengths,
-        returned,
-        target_column,
-        cotangent,
-        residual,
-        gate,
-        norms,
-        centroids,
-        mixed,
-        output_weight,
+    produced, returned = lax.optimization_barrier((produced, dispatch(back)))
+    residual_grad, mixed_grad, output_grad, second_gains = combine(
+        lengths, returned, target_column, cotangent, residual, norms, mixed, output_weight
     )
+    produced, mixed_grad = lax.optimization_barrier((produced, mixed_grad))
+    returned = dispatch(produced)
     mixed_grad = line.hold("far", mixed_grad)
     line.send("far_on")
     grads = attend_back(lengths, projected, mixed, total, mixed_grad)
+    grads, returned = lax.optimization_barrier((grads, returned))
     keeps, sends = pack(
         me, grads, tokens, norms, output_grad, second_gains, shares, experts
     )
@@ -1170,23 +1179,27 @@
     bits = [2**i for i in range(1, (experts - 1).bit_length())]
     orders = [bits, bits[::-1]]
     for level, now in enumerate(zip(*orders)):
-        if level == 0:
-            pairs = line.hold("near", pairs)
-            line.send("near_on", 0)
-            line.send("own", 0)
-        made = halves(me, now, [(0, keep.shape[1]) for keep, _ in pairs], pairs)
+        made = halves(me, now, [(0, keep.shape[1]) for keep, _ in pairs], pairs, level)
         pairs = [(kept, swap(sent, bit)) for (kept, sent), bit in zip(made, now)]
         if level == 0:
             kept, got = pairs[0]
-            pairs[0] = (line.hold("far_on", kept), got)
+            kept = line.hold("near", kept)
+            line.send("own", 0)
+            line.send("near_on", 0)
+            kept = line.hold("far_on", kept)
             line.send("far_out", 0)
-    grads = line.hold(("own", 0), grads)
+            pairs[0] = (kept, got)
+    if OWN_EARLY:
+        grads = line.hold(("own", 0), grads)
     input_gradient = project_back(grads, tokens, residual_grad, input_weight, norms)
     input_gradient, pairs = lax.optimization_barrier((input_gradient, pairs))
-    for name in ("far_out", "near_on"):
+    for name in ("far_out", "near_on") if OWN_EARLY else ("far_out", "near_on", "own"):
         pairs = line.hold((name, 0), pairs)
     streams = [keep.shape[1] for keep, _ in pairs]
-    over_line = exchange(join(pairs), "dp")
+    joined = join(pairs)
+    joined, returned = lax.optimization_barrier((joined, returned))
+    over_line = exchange(joined, "dp")
+    layer_output = layer(lengths, returned, target_column, residual, gate)
     for name in ("far_out", "near_on", "own"):
         line.send(name, 1)
     gathered = exchange(spread(over_line, experts))

time: 320 us -> 313 us (0.978)
  waiting for transfers between devices: 85 us -> 72.4 us
  Pallas kernels: 142 us -> 154 us
  local copies, waits for them, and re-layouts: 24.9 us -> 20 us
    ppermute x6, waiting for transfers between devices: 0.02 us -> 17.1 us  [on_device(): lax.ppermute(values, 'expert', partner_pairs('expert', bit))]
    all_to_all x5 -> x6, waiting for transfers between devices: 63.2 us -> 46.8 us  [exchange(): return lax.all_to_all(values, axis, split_axis=0, concat_axis=0, tiled=True)]
    ppermute x9, waiting for transfers between devices: 21.8 us -> 8.43 us  [send(): self.got[key] = lax.ppermute(values, self.axis, route)]
    pallas_call x0 -> x1, Pallas kernels: none -> 6.28 us  [layer(): pl.pallas_call(layer_kernel, out_shape=jax.ShapeDtypeStruct((rows, width)...]
    unnamed x76 -> x64, local copies, waits for them, and re-layouts: 24 us -> 19.1 us
    ppermute x6, starting transfers between devices: 7.25 us -> 2.96 us  [on_device(): lax.ppermute(values, 'expert', partner_pairs('expert', bit))]
    pallas_call x5, Pallas kernels: 7.32 us -> 11.1 us  [add(): pl.pallas_call(add_kernel, out_shape=jax.ShapeDtypeStruct((pieces, rows,...]
    all_to_all x5 -> x6, starting transfers between devices: 25.3 us -> 28 us  [exchange(): return lax.all_to_all(values, axis, split_axis=0, concat_axis=0, tiled=True)]
  transfers between devices with their start and end apart: 20 -> 21, of which waited for: 7 -> 8; matrix products, arithmetic and copies ran while one was open for 0% -> 0% of each run, Pallas kernels for 27% -> 32%
where the time goes in v1:
time: 313 us; the launch traced here: 312 us
  Pallas kernels  154 us (49%)
  waiting for transfers between devices  72.4 us (23%)
  starting transfers between devices  62 us (20%)
  local copies, waits for them, and re-layouts  20 us (6%)
    all_to_all x6, waiting for transfers between devices, exchange(): return lax.all_to_all(values, axis, split_axis=0, concat_axis=0, tiled=True)  46.8 us
    pallas_call x1, Pallas kernels, expert(): pl.pallas_call(functools.partial(expert_kernel, shares=shares, together=t...  38.4 us
    ppermute x9, starting transfers between devices, send(): self.got[key] = lax.ppermute(values, self.axis, route)  31 us
    all_to_all x6, starting transfers between devices, exchange(): return lax.all_to_all(values, axis, split_axis=0, concat_axis=0, tiled=True)  28 us
    pallas_call x1, Pallas kernels, attend_back(): pl.pallas_call(functools.partial(attend_back_kernel, scale=size ** (-0.5)...  26.6 us
    unnamed x64, local copies, waits for them, and re-layouts  19.1 us
    ppermute x6, waiting for transfers between devices, on_device(): lax.ppermute(values, 'expert', partner_pairs('expert', bit))  17.1 us
    pallas_call x1, Pallas kernels, attend(): pl.pallas_call(functools.partial(attend_kernel, scale=size ** (-0.5), hal...  14 us
  transfers between devices with their start and end apart: 21, of which 8 were waited for; matrix products, arithmetic and copies ran while one was open for 0% of the time, Pallas kernels for 32%

profile of v1, /device:TPU:0, one launch (start us, length us, event | category | flops | bytes accessed | tf_op | source)
XLA Modules:
  0.0 311.6 jit_solution(353659058882966154)
XLA Ops:
  1.3 5.3 %route.1 = (bf16[1024,768]{1,0:T(8,128)(2,1)}, s32[8,1024]{1,0:T(8,128)}, s32[1024,128]{1,0:T(8,128)}) custom-call(s32[1]{0:T(128)S(6)} %copy.23.length_ref, s32[1,1024]{1,0:T(1,128)} %bitcast.29, bf16[1024,768]{1,0:T(8,128)(2,1)} %cotangent_ref.3), custom_call_target="tpu_custom_call" | custom-call | flops 1610612736 | bytes 3145728 | tf_op jit(solution)/shard_map/route/pallas_call | solution.py:99
  6.6 5.3 %all-to-all-start = ((bf16[8,128,768]{2,1,0:T(8,128)(2,1)}), bf16[8,128,768]{2,1,0:T(8,128)(2,1)}, u32[]{:S(2)}, u32[]{:S(2)}) async-start(bf16[8,128,768]{2,1,0:T(8,128)(2,1)} %bitcast.22), calls=%async_computation | async-start | bytes 3145728 | tf_op jit(solution)/shard_map/all_to_all | solution.py:1140
  12.1 1.4 copy-done.9
  13.5 5.2 %project.1.query_ref.key_ref.value_ref = bf16[1024,2304]{1,0:T(8,128)(2,1)S(1)} custom-call(bf16[1024,768]{1,0:T(8,128)(2,1)S(1)} %copy-done.9, bf16[768,2304]{1,0:T(8,128)(2,1)S(1)} %copy-done.1, f32[4,768]{1,0:T(4,128)S(1)} %pad_maximum_fusion.norms_ref), custom_call_target="tpu_custom_call" | custom-call | flops 3623878656 | bytes 8257536 | tf_op jit(solution)/shard_map/project/pallas_call | solution.py:135
  18.7 14.0 %attend.1 = (bf16[1024,768]{1,0:T(8,128)(2,1)S(1)}, f32[1024,128]{1,0:T(8,128)S(1)}) custom-call(s32[1]{0:T(128)S(6)} %copy.23.length_ref, bf16[1024,2304]{1,0:T(8,128)(2,1)S(1)} %project.1.query_ref.key_ref.value_ref, bf16[1024,2304]{1,0:T(8,128)(2,1)S(1)} %project.1.query_ref.key_ref.value_ref, bf16[1024,2304]{1,0:T(8,128)(2,1)S(1)} %project.1.query_ref.key_ref.value_ref), custom_call_target="tpu_custom_call" | custom-call | flops 12884901888 | bytes 9437184 | tf_op jit(solution)/shard_map/attend/pallas_call | solution.py:216
  32.7 2.2 copy-done.14
  34.9 1.1 copy-done.16
  36.0 8.0 %hidden_rows.1 = (f32[1024,768]{1,0:T(8,128)}, f32[1024,128]{1,0:T(8,128)}, bf16[1024,768]{1,0:T(8,128)(2,1)}) custom-call(s32[1]{0:T(128)S(6)} %copy.23.length_ref, bf16[1024,768]{1,0:T(8,128)(2,1)} %copy-done.16, bf16[1024,768]{1,0:T(8,128)(2,1)} %tokens_ref.6, bf16[768,768]{1,0:T(8,128)(2,1)} %weight_ref.7, f32[4,768]{1,0:T(4,128)} %copy-done.12, ...), custom_call_target="tpu_custom_call" | custom-call | flops 2818572288 | bytes 9437184 | tf_op jit(solution)/shard_map/hidden_rows/pallas_call | solution.py:395
  44.0 4.3 %all-to-all-start.1 = ((bf16[8,128,768]{2,1,0:T(8,128)(2,1)}), bf16[8,128,768]{2,1,0:T(8,128)(2,1)S(1)}, u32[]{:S(2)}, u32[]{:S(2)}) async-start(bf16[8,128,768]{2,1,0:T(8,128)(2,1)} %bitcast.23), calls=%async_computation.1 | async-start | bytes 3145728 | tf_op jit(solution)/shard_map/all_to_all | solution.py:1140
  48.3 21.0 %all-to-all-done.1 = bf16[8,128,768]{2,1,0:T(8,128)(2,1)S(1)} async-done(((bf16[8,128,768]{2,1,0:T(8,128)(2,1)}), bf16[8,128,768]{2,1,0:T(8,128)(2,1)S(1)}, u32[]{:S(2)}, u32[]{:S(2)}) %all-to-all-start.1) | async-done | bytes 1572896 | tf_op jit(solution)/shard_map/all_to_all | solution.py:1140
  69.3 1.1 copy-done.21
  70.5 38.4 %expert.1 = (bf16[1024,768]{1,0:T(8,128)(2,1)}, bf16[1024,768]{1,0:T(8,128)(2,1)}, bf16[8,192,768]{2,1,0:T(8,128)(2,1)}, bf16[8,192,768]{2,1,0:T(8,128)(2,1)}, b...) custom-call(s32[1]{0:T(128)} %bitcast.me_ref, s32[1]{0:T(128)} %bitcast.1.place_ref, ...), custom_call_target="tpu_custom_call" | custom-call | flops 28991029248 | bytes 18874368 | tf_op jit(solution)/shard_map/expert/pallas_call | solution.py:556
  108.9 5.3 %collective-permute-start.1 = (bf16[8,192,768]{2,1,0:T(8,128)(2,1)}, bf16[8,192,768]{2,1,0:T(8,128)(2,1)}, u32[]{:S(2)}, u32[]{:S(2)}) collective-permute-start(bf16[8,192,768]{2,1,0:T(8,128)(2,1)} %get-tuple-element.97.left_ref), channel_id=1, source_target_pairs={{0,8},{24,16},{1,9},{25,17},{2,10},{26,18},{3,11},{27,19},{4,12},{... | collective-permute-start | bytes 7077896 | tf_op jit(solution)/shard_map/ppermute | solution.py:923
  114.2 3.6 %all-to-all-start.2 = ((bf16[8,128,768]{2,1,0:T(8,128)(2,1)}), bf16[8,128,768]{2,1,0:T(8,128)(2,1)S(1)}, u32[]{:S(2)}, u32[]{:S(2)}) async-start(bf16[8,128,768]{2,1,0:T(8,128)(2,1)} %bitcast.21), calls=%async_computation.2 | async-start | bytes 3145728 | tf_op jit(solution)/shard_map/all_to_all | solution.py:1140
  117.8 2.7 collective-permute-start
  120.5 18.3 %all-to-all-done.2 = bf16[8,128,768]{2,1,0:T(8,128)(2,1)S(1)} async-done(((bf16[8,128,768]{2,1,0:T(8,128)(2,1)}), bf16[8,128,768]{2,1,0:T(8,128)(2,1)S(1)}, u32[]{:S(2)}, u32[]{:S(2)}) %all-to-all-start.2) | async-done | bytes 1572896 | tf_op jit(solution)/shard_map/all_to_all | solution.py:1140
  138.8 1.1 copy-done.22
  139.9 12.0 %combine.1 = (f32[1024,768]{1,0:T(8,128)}, bf16[1024,768]{1,0:T(8,128)(2,1)}, bf16[768,768]{1,0:T(8,128)(2,1)}, f32[8,768]{1,0:T(8,128)}) custom-call(s32[1]{0:T(128)S(6)} %copy.23.length_ref, bf16[1024,768]{1,0:T(8,128)(2,1)} %bitcast.24, s32[1024,128]{1,0:T(8,128)} %get-tuple-element.92.column_ref, bf16[1024,768]{1,0:T(8,128)(2,1)} %cotangent_ref.3, ...), custom_call_target="tpu_custom_call" | custom-call | flops 5637144576 | bytes 18874368 | tf_op jit(solution)/shard_map/combine/pallas_call | solution.py:644
  151.9 4.4 %all-to-all-start.3 = ((bf16[8,128,768]{2,1,0:T(8,128)(2,1)}), bf16[8,128,768]{2,1,0:T(8,128)(2,1)}, u32[]{:S(2)}, u32[]{:S(2)}) async-start(bf16[8,128,768]{2,1,0:T(8,128)(2,1)} %bitcast.19), calls=%async_computation.3 | async-start | bytes 3145728 | tf_op jit(solution)/shard_map/all_to_all | solution.py:1140
  156.4 8.4 %collective-permute-done.1.right_ref = bf16[8,192,768]{2,1,0:T(8,128)(2,1)} collective-permute-done((bf16[8,192,768]{2,1,0:T(8,128)(2,1)}, bf16[8,192,768]{2,1,0:T(8,128)(2,1)}, u32[]{:S(2)}, u32[]{:S(2)}) %collective-permute-start.1) | collective-permute-done | bytes 2359328 | tf_op jit(solution)/shard_map/ppermute | solution.py:923
  164.8 3.0 add.15
  167.8 2.1 collective-permute-start.5
  169.9 2.3 copy-done.15
  172.2 26.6 %attend_back.1.grads_ref = bf16[3,1024,768]{2,1,0:T(8,128)(2,1)S(1)} custom-call(s32[1]{0:T(128)S(6)} %copy.23.length_ref, bf16[1024,2304]{1,0:T(8,128)(2,1)S(1)} %copy-done.15, bf16[1024,2304]{1,0:T(8,128)(2,1)S(1)} %copy-done.15, bf16[1024,2304]{1,0:T(8,128)(2,1)S(1)} %copy-done.15, bf16[1024,768]{1,0:T(8,128)(2,1)S(1)} %copy-done.17, ...), custom_call_target="tpu_custom_call" | custom-call | flops 24159191040 | bytes 15728640 | tf_op jit(solution)/shard_map/attend_back/pallas_call | solution.py:314
  198.8 2.2 copy-done.4
  201.0 2.3 copy-done.5
  203.4 1.3 copy-done.18
  204.6 7.0 %pack.1 = (bf16[4,448,384]{2,1,0:T(8,128)(2,1)S(1)}, bf16[4,384,384]{2,1,0:T(8,128)(2,1)S(1)}, bf16[4,448,384]{2,1,0:T(8,128)(2,1)S(1)}, bf16[4,384,384]{2,1,0:T(8,128)(2,1)S(1)}) custom-call(s32[1]{0:T(128)} %bitcast.me_ref, bf16[3,1024,768]{2,1,0:T(8,128)(2,1)S(1)} %copy-done.5, bf16[1024,768]{1,0:T(8,128)(2,1)S(1)} %copy-done.10, ...), custom_call_target="tpu_custom_call" | custom-call | flops 3623878656 | bytes 15728640 | tf_op jit(solution)/shard_map/pack/pallas_call | solution.py:776
  211.7 0.5 collective-permute-start.3
  212.2 6.1 %collective-permute-start.7 = (bf16[4,192,768]{2,1,0:T(8,128)(2,1)S(1)}, bf16[4,192,768]{2,1,0:T(8,128)(2,1)S(1)}, u32[]{:S(2)}, u32[]{:S(2)}) collective-permute-start(bf16[4,192,768]{2,1,0:T(8,128)(2,1)S(1)} %copy-done.23), channel_id=1, source_target_pairs={{0,8},{24,16},{1,9},{25,17},{2,10},{26,18},{3,11},{27,19},{4,12},{... | collective-permute-start | bytes 3538952 | tf_op jit(solution)/shard_map/ppermute | solution.py:923
  218.3 0.7 halves.2
  219.1 0.9 copy-done
  220.0 1.4 add.16
  221.4 1.3 collective-permute-start.6
  222.7 1.9 add.14
  224.7 0.9 collective-permute-start.4
  225.5 0.5 collective-permute-start.8
  226.0 0.7 collective-permute-start.9
  226.7 14.1 %collective-permute-done.9.refs_3_ = bf16[4,192,384]{2,1,0:T(8,128)(2,1)S(1)} collective-permute-done((bf16[4,192,384]{2,1,0:T(8,128)(2,1)S(1)}, bf16[4,192,384]{2,1,0:T(8,128)(2,1)S(1)}, u32[]{:S(2)}, u32[]{:S(2)}) %collective-permute-start.9) | collective-permute-done | bytes 589856 | tf_op jit(solution)/shard_map/ppermute | solution.py:1177
  240.8 1.9 collective-permute-done.8.refs_1_
  242.7 0.4 halves.3
  243.1 0.6 collective-permute-start.10
  243.8 0.6 collective-permute-start.11
  244.4 6.6 %project_back.1 = bf16[1024,768]{1,0:T(8,128)(2,1)} custom-call(bf16[3,1024,768]{2,1,0:T(8,128)(2,1)S(1)} %copy-done.5, bf16[1024,768]{1,0:T(8,128)(2,1)S(1)} %copy-done.11, f32[1024,768]{1,0:T(8,128)S(1)} %copy-done.6, bf16[768,2304]{1,0:T(8,128)(2,1)S(1)} %copy-done.2, f32[4,768]{1,0:T(4,128)S(1)} %copy-done.13), custom_call_target="tpu_custom_call" | custom-call | flops 1087163648 | bytes 4718592 | tf_op jit(solution)/shard_map/project_back/pallas_call | solution.py:821
  251.0 0.3 collective-permute-done.11.refs_3_
  251.3 0.8 collective-permute-done.10.refs_1_
  252.1 1.1 copy-done.25
  253.2 1.0 copy-done.26
  254.4 0.8 copy-done.7
  255.3 6.2 %all-to-all-start.4 = ((bf16[4,208,384]{2,1,0:T(8,128)(2,1)}), bf16[4,208,384]{2,1,0:T(8,128)(2,1)S(1)}, u32[]{:S(2)}, u32[]{:S(2)}) async-start(bf16[4,208,384]{2,1,0:T(8,128)(2,1)} %copy-done.7), calls=%async_computation.4 | async-start | bytes 1277952 | tf_op jit(solution)/shard_map/all_to_all | solution.py:1140
  261.4 2.2 add.18
  263.7 1.3 collective-permute-start.14
  265.0 2.6 add.17
  267.5 1.7 collective-permute-start.13
  269.3 9.7 %collective-permute-start.12 = (bf16[4,192,768]{2,1,0:T(8,128)(2,1)}, bf16[4,192,768]{2,1,0:T(8,128)(2,1)}, u32[]{:S(2)}, u32[]{:S(2)}) collective-permute-start(bf16[4,192,768]{2,1,0:T(8,128)(2,1)} %get-tuple-element.150.middle_ref), channel_id=1, source_target_pairs={{0,8},{24,16},{1,9},{25,17},{2,10},{26,18},{3,11},{27,19},{4,12},{... | collective-permute-start | bytes 3538952 | tf_op jit(solution)/shard_map/ppermute | solution.py:923
  278.9 1.2 spread.1
  280.1 4.3 %all-to-all-start.5 = ((bf16[8,208,384]{2,1,0:T(8,128)(2,1)}), bf16[8,208,384]{2,1,0:T(8,128)(2,1)}, u32[]{:S(2)}, u32[]{:S(2)}) async-start(bf16[8,208,384]{2,1,0:T(8,128)(2,1)} %spread.1), calls=%async_computation.5 | async-start | bytes 2555904 | tf_op jit(solution)/shard_map/all_to_all | solution.py:1140
  284.4 4.0 %line_total.3 = f32[768,768]{1,0:T(8,128)} custom-call(s32[1]{0:T(128)} %bitcast.1.place_ref, bf16[4,192,768]{2,1,0:T(8,128)(2,1)} %get-tuple-element.120.middle_ref, bf16[8,192,768]{2,1,0:T(8,128)(2,1)} %get-tuple-element.116.left_ref.end_ref, bf16[4,192,768]{2,1,0:T(8,128)(2,1)} %copy-done.24, bf16[4,192,768]{2,1,0:T(8,128)(2,1)} %copy-done.26, ...), custom_call_target="tpu_custom_call" | custom-call | tf_op jit(solution)/shard_map/line_total/pallas_call | solution.py:877
  288.4 6.3 %layer.1 = bf16[1024,768]{1,0:T(8,128)(2,1)} custom-call(s32[1]{0:T(128)S(6)} %copy.23.length_ref, bf16[1024,768]{1,0:T(8,128)(2,1)} %bitcast.12.returned_ref, s32[1024,128]{1,0:T(8,128)} %get-tuple-element.92.column_ref, f32[1024,768]{1,0:T(8,128)} %get-tuple-element.102.residual_ref, f32[1024,128]{1,0:T(8,128)} %get-tuple-element.145.gate_ref), custom_call_target="tpu_custom_call" | custom-call | flops 1610612736 | bytes 7864320 | tf_op jit(solution)/shard_map/layer/pallas_call | solution.py:689
  294.7 7.5 %all-to-all-done.5.gathered_ref = bf16[8,208,384]{2,1,0:T(8,128)(2,1)} async-done(((bf16[8,208,384]{2,1,0:T(8,128)(2,1)}), bf16[8,208,384]{2,1,0:T(8,128)(2,1)}, u32[]{:S(2)}, u32[]{:S(2)}) %all-to-all-start.5) | async-done | bytes 1277984 | tf_op jit(solution)/shard_map/all_to_all | solution.py:1140
  302.3 3.1 assemble.1
  305.6 1.3 dynamic-slice_divide_fusion
  306.9 0.6 fusion
  307.6 4.0 %line_total.2 = f32[192,3072]{1,0:T(8,128)} custom-call(s32[1]{0:T(128)} %bitcast.1.place_ref, bf16[4,192,768]{2,1,0:T(8,128)(2,1)} %get-tuple-element.150.middle_ref, bf16[8,192,768]{2,1,0:T(8,128)(2,1)} %get-tuple-element.116.left_ref.end_ref, bf16[4,192,768]{2,1,0:T(8,128)(2,1)} %collective-permute-done.12.refs_0_, ...), custom_call_target="tpu_custom_call" | custom-call | tf_op jit(solution)/shard_map/line_total/pallas_call | solution.py:877
  (73 shorter events, 0.6 us)
Async XLA Ops:
  1.3 10.8 %copy-start.1 = (bf16[768,2304]{1,0:T(8,128)(2,1)S(1)}, bf16[768,2304]{1,0:T(8,128)(2,1)}, u32[]{:S(2)}) copy-start(bf16[768,2304]{1,0:T(8,128)(2,1)} %weight_ref.9) | copy-start | bytes 10616836
  6.6 5.3 %copy-start.28 = (f32[768]{0:T(1024)S(1)}, f32[768]{0:T(1024)}, u32[]{:S(2)}) copy-start(f32[768]{0:T(1024)} %param.19) | copy-start | bytes 9220
  6.6 5.4 %copy-start.27 = (f32[768]{0:T(1024)S(1)}, f32[768]{0:T(1024)}, u32[]{:S(2)}) copy-start(f32[768]{0:T(1024)} %param.20) | copy-start | bytes 9220
  6.6 5.4 %copy-start.30 = (f32[768]{0:T(1024)S(1)}, f32[768]{0:T(1024)}, u32[]{:S(2)}) copy-start(f32[768]{0:T(1024)} %param.21) | copy-start | bytes 9220
  6.6 5.4 %copy-start.31 = (f32[768]{0:T(1024)S(1)}, f32[768]{0:T(1024)}, u32[]{:S(2)}) copy-start(f32[768]{0:T(1024)} %param.22) | copy-start | bytes 9220
  6.6 29.4 %all-to-all-start = ((bf16[8,128,768]{2,1,0:T(8,128)(2,1)}), bf16[8,128,768]{2,1,0:T(8,128)(2,1)}, u32[]{:S(2)}, u32[]{:S(2)}) async-start(bf16[8,128,768]{2,1,0:T(8,128)(2,1)} %bitcast.22), calls=%async_computation | async-start | bytes 3145728 | tf_op jit(solution)/shard_map/all_to_all | solution.py:1140
  12.1 1.4 copy-start.9
  13.5 5.2 %copy-start.12 = (f32[4,768]{1,0:T(4,128)}, f32[4,768]{1,0:T(4,128)S(1)}, u32[]{:S(2)}) copy-start(f32[4,768]{1,0:T(4,128)S(1)} %pad_maximum_fusion.norms_ref) | copy-start | bytes 36868
  32.7 2.2 copy-start.14
  34.8 1.1 copy-start.16
  44.0 25.3 %all-to-all-start.1 = ((bf16[8,128,768]{2,1,0:T(8,128)(2,1)}), bf16[8,128,768]{2,1,0:T(8,128)(2,1)S(1)}, u32[]{:S(2)}, u32[]{:S(2)}) async-start(bf16[8,128,768]{2,1,0:T(8,128)(2,1)} %bitcast.23), calls=%async_computation.1 | async-start | bytes 3145728 | tf_op jit(solution)/shard_map/all_to_all | solution.py:1140
  69.3 1.1 copy-start.21
  108.9 55.9 %collective-permute-start.1 = (bf16[8,192,768]{2,1,0:T(8,128)(2,1)}, bf16[8,192,768]{2,1,0:T(8,128)(2,1)}, u32[]{:S(2)}, u32[]{:S(2)}) collective-permute-start(bf16[8,192,768]{2,1,0:T(8,128)(2,1)} %get-tuple-element.97.left_ref), channel_id=1, source_target_pairs={{0,8},{24,16},{1,9},{25,17},{2,10},{26,18},{3,11},{27,19},{4,12},{... | collective-permute-start | bytes 7077896 | tf_op jit(solution)/shard_map/ppermute | solution.py:923
  114.2 24.5 %all-to-all-start.2 = ((bf16[8,128,768]{2,1,0:T(8,128)(2,1)}), bf16[8,128,768]{2,1,0:T(8,128)(2,1)S(1)}, u32[]{:S(2)}, u32[]{:S(2)}) async-start(bf16[8,128,768]{2,1,0:T(8,128)(2,1)} %bitcast.21), calls=%async_computation.2 | async-start | bytes 3145728 | tf_op jit(solution)/shard_map/all_to_all | solution.py:1140
  117.8 101.3 %collective-permute-start = (bf16[8,192,768]{2,1,0:T(8,128)(2,1)}, bf16[8,192,768]{2,1,0:T(8,128)(2,1)}, u32[]{:S(2)}, u32[]{:S(2)}) collective-permute-start(bf16[8,192,768]{2,1,0:T(8,128)(2,1)} %get-tuple-element.95.left_ref), channel_id=1, source_target_pairs={{0,8},{24,16},{1,9},{25,17},{2,10},{26,18},{3,11},{27,19},{4,12},{... | collective-permute-start | bytes 7077896 | tf_op jit(solution)/shard_map/ppermute | solution.py:923
  138.8 1.1 copy-start.22
  151.9 12.9 %copy-start.8 = (bf16[8,192,768]{2,1,0:T(8,128)(2,1)S(1)}, bf16[8,192,768]{2,1,0:T(8,128)(2,1)}, u32[]{:S(2)}) copy-start(bf16[8,192,768]{2,1,0:T(8,128)(2,1)} %get-tuple-element.97.left_ref) | copy-start | bytes 7077892
  151.9 49.1 %all-to-all-start.3 = ((bf16[8,128,768]{2,1,0:T(8,128)(2,1)}), bf16[8,128,768]{2,1,0:T(8,128)(2,1)}, u32[]{:S(2)}, u32[]{:S(2)}) async-start(bf16[8,128,768]{2,1,0:T(8,128)(2,1)} %bitcast.19), calls=%async_computation.3 | async-start | bytes 3145728 | tf_op jit(solution)/shard_map/all_to_all | solution.py:1140
  156.4 13.5 %copy-start.17 = (bf16[1024,768]{1,0:T(8,128)(2,1)S(1)}, bf16[1024,768]{1,0:T(8,128)(2,1)}, u32[]{:S(2)}) copy-start(bf16[1024,768]{1,0:T(8,128)(2,1)} %copy-done.16) | copy-start | bytes 4718596
  156.4 13.5 %copy-start.19 = (bf16[1024,768]{1,0:T(8,128)(2,1)S(1)}, bf16[1024,768]{1,0:T(8,128)(2,1)}, u32[]{:S(2)}) copy-start(bf16[1024,768]{1,0:T(8,128)(2,1)} %get-tuple-element.105.incoming_ref) | copy-start | bytes 4718596
  167.8 51.3 %collective-permute-start.5 = (bf16[8,192,768]{2,1,0:T(8,128)(2,1)}, bf16[8,192,768]{2,1,0:T(8,128)(2,1)}, u32[]{:S(2)}, u32[]{:S(2)}) collective-permute-start(bf16[8,192,768]{2,1,0:T(8,128)(2,1)} %add.15), channel_id=1, source_target_pairs={{8,16},{16,8},{9,17},{17,9},{10,18},{18,10},{11,19},{19,11},{12,20... | collective-permute-start | bytes 7077896 | tf_op jit(solution)/shard_map/ppermute | solution.py:923
  169.9 2.3 copy-start.15
  172.2 28.8 %copy-start.10 = (bf16[1024,768]{1,0:T(8,128)(2,1)S(1)}, bf16[1024,768]{1,0:T(8,128)(2,1)}, u32[]{:S(2)}) copy-start(bf16[1024,768]{1,0:T(8,128)(2,1)} %tokens_ref.6) | copy-start | bytes 4718596
  172.2 28.8 %copy-start.13 = (f32[4,768]{1,0:T(4,128)S(1)}, f32[4,768]{1,0:T(4,128)}, u32[]{:S(2)}) copy-start(f32[4,768]{1,0:T(4,128)} %copy-done.12) | copy-start | bytes 36868
  172.2 28.8 %copy-start.20 = (f32[8,768]{1,0:T(8,128)S(1)}, f32[8,768]{1,0:T(8,128)}, u32[]{:S(2)}) copy-start(f32[8,768]{1,0:T(8,128)} %get-tuple-element.109.second_ref) | copy-start | bytes 73732
  198.8 2.2 copy-start.4
  201.0 2.3 copy-start.5
  203.4 1.3 copy-start.18
  204.6 7.6 %copy-start.23 = (bf16[4,192,768]{2,1,0:T(8,128)(2,1)S(1)}, bf16[4,192,768]{2,1,0:T(8,128)(2,1)}, u32[]{:S(2)}) copy-start(bf16[4,192,768]{2,1,0:T(8,128)(2,1)} %get-tuple-element.120.middle_ref) | copy-start | bytes 3538948
  211.6 6.7 %collective-permute-start.2 = (bf16[4,448,384]{2,1,0:T(8,128)(2,1)S(1)}, bf16[4,448,384]{2,1,0:T(8,128)(2,1)S(1)}, u32[]{:S(2)}, u32[]{:S(2)}) collective-permute-start(bf16[4,448,384]{2,1,0:T(8,128)(2,1)S(1)} %get-tuple-element.111), channel_id=1, source_target_pairs={{0,1},{1,0},{2,3},{3,2},{4,5},{5,4},{6,7},{7,6},{8,9},{9,8},{10,11... | collective-permute-start | bytes 4128776 | tf_op jit(solution)/shard_map/ppermute | solution.py:1177
  211.7 6.6 %collective-permute-start.3 = (bf16[4,384,384]{2,1,0:T(8,128)(2,1)S(1)}, bf16[4,384,384]{2,1,0:T(8,128)(2,1)S(1)}, u32[]{:S(2)}, u32[]{:S(2)}) collective-permute-start(bf16[4,384,384]{2,1,0:T(8,128)(2,1)S(1)} %get-tuple-element.113), channel_id=1, source_target_pairs={{0,1},{1,0},{2,3},{3,2},{4,5},{5,4},{6,7},{7,6},{8,9},{9,8},{10,11... | collective-permute-start | bytes 3538952 | tf_op jit(solution)/shard_map/ppermute | solution.py:1177
  212.2 32.2 %collective-permute-start.7 = (bf16[4,192,768]{2,1,0:T(8,128)(2,1)S(1)}, bf16[4,192,768]{2,1,0:T(8,128)(2,1)S(1)}, u32[]{:S(2)}, u32[]{:S(2)}) collective-permute-start(bf16[4,192,768]{2,1,0:T(8,128)(2,1)S(1)} %copy-done.23), channel_id=1, source_target_pairs={{0,8},{24,16},{1,9},{25,17},{2,10},{26,18},{3,11},{27,19},{4,12},{... | collective-permute-start | bytes 3538952 | tf_op jit(solution)/shard_map/ppermute | solution.py:923
  218.3 1.7 copy-start
  221.4 30.7 %collective-permute-start.6 = (bf16[4,192,768]{2,1,0:T(8,128)(2,1)S(1)}, bf16[4,192,768]{2,1,0:T(8,128)(2,1)S(1)}, u32[]{:S(2)}, u32[]{:S(2)}) collective-permute-start(bf16[4,192,768]{2,1,0:T(8,128)(2,1)S(1)} %add.16), channel_id=1, source_target_pairs={{16,24},{8,0},{17,25},{9,1},{18,26},{10,2},{19,27},{11,3},{20,28},... | collective-permute-start | bytes 3538952 | tf_op jit(solution)/shard_map/ppermute | solution.py:923
  222.7 21.6 %copy-start.2 = (bf16[768,2304]{1,0:T(8,128)(2,1)S(1)}, bf16[768,2304]{1,0:T(8,128)(2,1)}, u32[]{:S(2)}) copy-start(bf16[768,2304]{1,0:T(8,128)(2,1)} %weight_ref.9) | copy-start | bytes 10616836
  222.7 21.6 %copy-start.6 = (f32[1024,768]{1,0:T(8,128)S(1)}, f32[1024,768]{1,0:T(8,128)}, u32[]{:S(2)}) copy-start(f32[1024,768]{1,0:T(8,128)} %get-tuple-element.122.residual_grad_ref) | copy-start | bytes 9437188
  224.6 19.7 %copy-start.11 = (bf16[1024,768]{1,0:T(8,128)(2,1)S(1)}, bf16[1024,768]{1,0:T(8,128)(2,1)}, u32[]{:S(2)}) copy-start(bf16[1024,768]{1,0:T(8,128)(2,1)} %tokens_ref.6) | copy-start | bytes 4718596
  224.7 27.4 %collective-permute-start.4 = (bf16[4,192,768]{2,1,0:T(8,128)(2,1)S(1)}, bf16[4,192,768]{2,1,0:T(8,128)(2,1)S(1)}, u32[]{:S(2)}, u32[]{:S(2)}) collective-permute-start(bf16[4,192,768]{2,1,0:T(8,128)(2,1)S(1)} %add.14), channel_id=1, source_target_pairs={{8,16},{16,8},{9,17},{17,9},{10,18},{18,10},{11,19},{19,11},{12,20... | collective-permute-start | bytes 3538952 | tf_op jit(solution)/shard_map/ppermute | solution.py:923
  225.5 17.2 %collective-permute-start.8 = (bf16[4,224,384]{2,1,0:T(8,128)(2,1)S(1)}, bf16[4,224,384]{2,1,0:T(8,128)(2,1)S(1)}, u32[]{:S(2)}, u32[]{:S(2)}) collective-permute-start(bf16[4,224,384]{2,1,0:T(8,128)(2,1)S(1)} %get-tuple-element.124), channel_id=1, source_target_pairs={{0,2},{1,3},{2,0},{3,1},{4,6},{5,7},{6,4},{7,5},{8,10},{9,11},{10,... | collective-permute-start | bytes 2064392 | tf_op jit(solution)/shard_map/ppermute | solution.py:1177
  226.0 14.8 %collective-permute-start.9 = (bf16[4,192,384]{2,1,0:T(8,128)(2,1)S(1)}, bf16[4,192,384]{2,1,0:T(8,128)(2,1)S(1)}, u32[]{:S(2)}, u32[]{:S(2)}) collective-permute-start(bf16[4,192,384]{2,1,0:T(8,128)(2,1)S(1)} %get-tuple-element.126), channel_id=1, source_target_pairs={{0,4},{1,5},{2,6},{3,7},{4,0},{5,1},{6,2},{7,3},{8,12},{9,13},{10,... | collective-permute-start | bytes 1769480 | tf_op jit(solution)/shard_map/ppermute | solution.py:1177
  243.1 9.0 %collective-permute-start.10 = (bf16[4,112,384]{2,1,0:T(8,128)(2,1)S(1)}, bf16[4,112,384]{2,1,0:T(8,128)(2,1)S(1)}, u32[]{:S(2)}, u32[]{:S(2)}) collective-permute-start(bf16[4,112,384]{2,1,0:T(8,128)(2,1)S(1)} %get-tuple-element.128), channel_id=1, source_target_pairs={{0,4},{1,5},{2,6},{3,7},{4,0},{5,1},{6,2},{7,3},{8,12},{9,13},{10,... | collective-permute-start | bytes 1032200 | tf_op jit(solution)/shard_map/ppermute | solution.py:1177
  243.8 7.6 %collective-permute-start.11 = (bf16[4,96,384]{2,1,0:T(8,128)(2,1)S(1)}, bf16[4,96,384]{2,1,0:T(8,128)(2,1)S(1)}, u32[]{:S(2)}, u32[]{:S(2)}) collective-permute-start(bf16[4,96,384]{2,1,0:T(8,128)(2,1)S(1)} %get-tuple-element.130), channel_id=1, source_target_pairs={{0,2},{1,3},{2,0},{3,1},{4,6},{5,7},{6,4},{7,5},{8,10},{9,11},{10,... | collective-permute-start | bytes 884744 | tf_op jit(solution)/shard_map/ppermute | solution.py:1177
  244.3 6.6 %copy-start.24 = (bf16[4,192,768]{2,1,0:T(8,128)(2,1)}, bf16[4,192,768]{2,1,0:T(8,128)(2,1)S(1)}, u32[]{:S(2)}) copy-start(bf16[4,192,768]{2,1,0:T(8,128)(2,1)S(1)} %collective-permute-done.7.refs_0_) | copy-start | bytes 3538948
  252.1 1.1 copy-start.25
  253.2 1.1 copy-start.26
  254.4 0.8 copy-start.7
  255.3 23.7 %all-to-all-start.4 = ((bf16[4,208,384]{2,1,0:T(8,128)(2,1)}), bf16[4,208,384]{2,1,0:T(8,128)(2,1)S(1)}, u32[]{:S(2)}, u32[]{:S(2)}) async-start(bf16[4,208,384]{2,1,0:T(8,128)(2,1)} %copy-done.7), calls=%async_computation.4 | async-start | bytes 1277952 | tf_op jit(solution)/shard_map/all_to_all | solution.py:1140
  263.7 41.7 %collective-permute-start.14 = (bf16[4,192,768]{2,1,0:T(8,128)(2,1)}, bf16[4,192,768]{2,1,0:T(8,128)(2,1)}, u32[]{:S(2)}, u32[]{:S(2)}) collective-permute-start(bf16[4,192,768]{2,1,0:T(8,128)(2,1)} %add.18), channel_id=1, source_target_pairs={{16,24},{8,0},{17,25},{9,1},{18,26},{10,2},{19,27},{11,3},{20,28},... | collective-permute-start | bytes 3538952 | tf_op jit(solution)/shard_map/ppermute | solution.py:923
  267.5 37.8 %collective-permute-start.13 = (bf16[4,192,768]{2,1,0:T(8,128)(2,1)}, bf16[4,192,768]{2,1,0:T(8,128)(2,1)}, u32[]{:S(2)}, u32[]{:S(2)}) collective-permute-start(bf16[4,192,768]{2,1,0:T(8,128)(2,1)} %add.17), channel_id=1, source_target_pairs={{8,16},{16,8},{9,17},{17,9},{10,18},{18,10},{11,19},{19,11},{12,20... | collective-permute-start | bytes 3538952 | tf_op jit(solution)/shard_map/ppermute | solution.py:923
  269.3 36.1 %collective-permute-start.12 = (bf16[4,192,768]{2,1,0:T(8,128)(2,1)}, bf16[4,192,768]{2,1,0:T(8,128)(2,1)}, u32[]{:S(2)}, u32[]{:S(2)}) collective-permute-start(bf16[4,192,768]{2,1,0:T(8,128)(2,1)} %get-tuple-element.150.middle_ref), channel_id=1, source_target_pairs={{0,8},{24,16},{1,9},{25,17},{2,10},{26,18},{3,11},{27,19},{4,12},{... | collective-permute-start | bytes 3538952 | tf_op jit(solution)/shard_map/ppermute | solution.py:923
  280.1 22.2 %all-to-all-start.5 = ((bf16[8,208,384]{2,1,0:T(8,128)(2,1)}), bf16[8,208,384]{2,1,0:T(8,128)(2,1)}, u32[]{:S(2)}, u32[]{:S(2)}) async-start(bf16[8,208,384]{2,1,0:T(8,128)(2,1)} %spread.1), calls=%async_computation.5 | async-start | bytes 2555904 | tf_op jit(solution)/shard_map/all_to_all | solution.py:1140
  288.4 13.8 %copy-start.3 = (bf16[768,2304]{1,0:T(8,128)(2,1)S(1)}, bf16[768,2304]{1,0:T(8,128)(2,1)}, u32[]{:S(2)}) copy-start(bf16[768,2304]{1,0:T(8,128)(2,1)} %weight_ref.9) | copy-start | bytes 10616836
  305.6 6.0 %copy-start.29 = (f32[192]{0:T(256)}, f32[192]{0:T(256)S(1)}, u32[]{:S(2)}) copy-start(f32[192]{0:T(256)S(1)} %get-tuple-element.162) | copy-start | bytes 2308

commit v2 on v1

--- a/solution.py
+++ b/solution.py
@@ -16,7 +16,6 @@
 SEEN = 1
 EXPERT_MIB = 54
 HIDDEN_MIB = 60
-OWN_EARLY = True
 
 
 def dot(left, right, left_axis=1, right_axis=0):
@@ -322,7 +321,7 @@
             out_specs=pl.BlockSpec((3, rows, 2 * size), lambda i, l: (0, 0, i)),
             scratch_shapes=[pltpu.VMEM((rows, 2 * size), F32)] * 2,
         ),
-        compiler_params=params(24),
+        compiler_params=params(60),
         cost_estimate=cost(
             30 * rows * rows * width, 20 * rows * width
         ),
@@ -379,13 +378,9 @@
         hidden_low[at, :] = hidden.astype(BF)
 
     staggered(range(rows // count), branch_of, finish)
-
-    @pl.loop(0, rows // (2 * count))
-    def _(number):
-        for part in range(2):
-            first = pl.multiple_of((2 * number + part) * count, count)
-            chosen = selection(row_ref[0:1, :], first, count)
-            out_ref[pl.ds(first, count), :] = dot(chosen, hidden_low[...]).astype(BF)
+    for first in range(0, rows, count):
+        chosen = selection(row_ref[0:1, :], first, count)
+        out_ref[first : first + count, :] = dot(chosen, hidden_low[...]).astype(BF)
 
 
 def hidden_rows(length, mixed, tokens, weight, norms, centroids, target_row, target_column):
@@ -826,7 +821,7 @@
         + [pl.BlockSpec(weight.shape, lambda i: (0, 0)), pl.BlockSpec((4, width), lambda i: (0, 0))],
         out_specs=part,
         compiler_params=params(24),
-        cost_estimate=cost(1.8 * rows * width * width, 6 * rows * width),
+        cost_estimate=cost(18 * rows * width * width, 60 * rows * width),
         name="project_back",
     )(grads, tokens, residual_grad, weight, norms)
 
@@ -986,7 +981,7 @@
             num_scalar_prefetch=1, grid=(shares,), in_specs=in_specs, out_specs=out_specs
         ),
         compiler_params=params(20),
-        cost_estimate=cost(0, 60 * size * level),
+        cost_estimate=cost(0, 0 * size * level),
         name="halves",
     )(me, *[array for pair in pairs for array in pair])
     return [(outs[2 * i], outs[2 * i + 1]) for i in range(len(bits))]
@@ -1189,11 +1184,9 @@
             kept = line.hold("far_on", kept)
             line.send("far_out", 0)
             pairs[0] = (kept, got)
-    if OWN_EARLY:
-        grads = line.hold(("own", 0), grads)
     input_gradient = project_back(grads, tokens, residual_grad, input_weight, norms)
     input_gradient, pairs = lax.optimization_barrier((input_gradient, pairs))
-    for name in ("far_out", "near_on") if OWN_EARLY else ("far_out", "near_on", "own"):
+    for name in ("far_out", "near_on", "own"):
         pairs = line.hold((name, 0), pairs)
     streams = [keep.shape[1] for keep, _ in pairs]
     joined = join(pairs)

time: 313 us -> 312 us (level)
  starting transfers between devices: 62 us -> 69.8 us
  local copies, waits for them, and re-layouts: 20 us -> 14.9 us
    ppermute x6, waiting for transfers between devices: 17.1 us -> 5.63 us  [on_device(): lax.ppermute(values, 'expert', partner_pairs('expert', bit))]
    ppermute x9, waiting for transfers between devices: 8.43 us -> 18.1 us  [send(): self.got[key] = lax.ppermute(values, self.axis, route)]
    unnamed x64 -> x58, local copies, waits for them, and re-layouts: 19.1 us -> 14 us
    ppermute x6, starting transfers between devices: 2.96 us -> 7.26 us  [on_device(): lax.ppermute(values, 'expert', partner_pairs('expert', bit))]
    ppermute x9, starting transfers between devices: 31 us -> 34.3 us  [send(): self.got[key] = lax.ppermute(values, self.axis, route)]
  transfers between devices with their start and end apart: 21 -> 21, of which waited for: 8 -> 8; matrix products, arithmetic and copies ran while one was open for 0% -> 0% of each run, Pallas kernels for 32% -> 31%
where the time goes in v2:
time: 312 us; the launch traced here: 311 us
  Pallas kernels  153 us (49%)
  waiting for transfers between devices  70.7 us (23%)
  starting transfers between devices  69.8 us (22%)
  local copies, waits for them, and re-layouts  14.9 us (5%)
    all_to_all x6, waiting for transfers between devices, exchange(): return lax.all_to_all(values, axis, split_axis=0, concat_axis=0, tiled=True)  47 us
    pallas_call x1, Pallas kernels, expert(): pl.pallas_call(functools.partial(expert_kernel, shares=shares, together=t...  38.4 us
    ppermute x9, starting transfers between devices, send(): self.got[key] = lax.ppermute(values, self.axis, route)  34.3 us
    all_to_all x6, starting transfers between devices, exchange(): return lax.all_to_all(values, axis, split_axis=0, concat_axis=0, tiled=True)  28.2 us
    pallas_call x1, Pallas kernels, attend_back(): pl.pallas_call(functools.partial(attend_back_kernel, scale=size ** (-0.5)...  27.3 us
    ppermute x9, waiting for transfers between devices, send(): self.got[key] = lax.ppermute(values, self.axis, route)  18.1 us
    unnamed x58, local copies, waits for them, and re-layouts  14 us
    pallas_call x1, Pallas kernels, attend(): pl.pallas_call(functools.partial(attend_kernel, scale=size ** (-0.5), hal...  13.9 us
  transfers between devices with their start and end apart: 21, of which 8 were waited for; matrix products, arithmetic and copies ran while one was open for 0% of the time, Pallas kernels for 31%

profile of v2, /device:TPU:0, one launch (start us, length us, event | category | flops | bytes accessed | tf_op | source)
XLA Modules:
  0.0 310.6 jit_solution(5842245989296860832)
XLA Ops:
  1.3 5.3 %route.1 = (bf16[1024,768]{1,0:T(8,128)(2,1)}, s32[8,1024]{1,0:T(8,128)}, s32[1024,128]{1,0:T(8,128)}) custom-call(s32[1]{0:T(128)S(6)} %copy.23.length_ref, s32[1,1024]{1,0:T(1,128)} %bitcast.29, bf16[1024,768]{1,0:T(8,128)(2,1)} %cotangent_ref.3), custom_call_target="tpu_custom_call" | custom-call | flops 1610612736 | bytes 3145728 | tf_op jit(solution)/shard_map/route/pallas_call | solution.py:98
  6.6 5.3 %all-to-all-start = ((bf16[8,128,768]{2,1,0:T(8,128)(2,1)}), bf16[8,128,768]{2,1,0:T(8,128)(2,1)}, u32[]{:S(2)}, u32[]{:S(2)}) async-start(bf16[8,128,768]{2,1,0:T(8,128)(2,1)} %bitcast.22), calls=%async_computation | async-start | bytes 3145728 | tf_op jit(solution)/shard_map/all_to_all | solution.py:1135
  12.1 1.4 copy-done.8
  13.5 5.2 %project.1.query_ref.key_ref.value_ref = bf16[1024,2304]{1,0:T(8,128)(2,1)S(1)} custom-call(bf16[1024,768]{1,0:T(8,128)(2,1)S(1)} %copy-done.8, bf16[768,2304]{1,0:T(8,128)(2,1)S(1)} %copy-done.1, f32[4,768]{1,0:T(4,128)S(1)} %pad_maximum_fusion.norms_ref), custom_call_target="tpu_custom_call" | custom-call | flops 3623878656 | bytes 8257536 | tf_op jit(solution)/shard_map/project/pallas_call | solution.py:134
  18.7 13.9 %attend.1 = (bf16[1024,768]{1,0:T(8,128)(2,1)S(1)}, f32[1024,128]{1,0:T(8,128)S(1)}) custom-call(s32[1]{0:T(128)S(6)} %copy.23.length_ref, bf16[1024,2304]{1,0:T(8,128)(2,1)S(1)} %project.1.query_ref.key_ref.value_ref, bf16[1024,2304]{1,0:T(8,128)(2,1)S(1)} %project.1.query_ref.key_ref.value_ref, bf16[1024,2304]{1,0:T(8,128)(2,1)S(1)} %project.1.query_ref.key_ref.value_ref), custom_call_target="tpu_custom_call" | custom-call | flops 12884901888 | bytes 9437184 | tf_op jit(solution)/shard_map/attend/pallas_call | solution.py:215
  32.6 2.2 copy-done.11
  34.7 1.1 copy-done.13
  35.9 0.8 copy-done.17
  36.7 7.5 %hidden_rows.1 = (f32[1024,768]{1,0:T(8,128)}, f32[1024,128]{1,0:T(8,128)}, bf16[1024,768]{1,0:T(8,128)(2,1)}) custom-call(s32[1]{0:T(128)S(6)} %copy.23.length_ref, bf16[1024,768]{1,0:T(8,128)(2,1)} %copy-done.13, bf16[1024,768]{1,0:T(8,128)(2,1)} %tokens_ref.6, bf16[768,768]{1,0:T(8,128)(2,1)} %weight_ref.7, f32[4,768]{1,0:T(4,128)} %copy-done.6, ...), custom_call_target="tpu_custom_call" | custom-call | flops 2818572288 | bytes 9437184 | tf_op jit(solution)/shard_map/hidden_rows/pallas_call | solution.py:390
  44.2 4.3 %all-to-all-start.1 = ((bf16[8,128,768]{2,1,0:T(8,128)(2,1)}), bf16[8,128,768]{2,1,0:T(8,128)(2,1)S(1)}, u32[]{:S(2)}, u32[]{:S(2)}) async-start(bf16[8,128,768]{2,1,0:T(8,128)(2,1)} %bitcast.23), calls=%async_computation.1 | async-start | bytes 3145728 | tf_op jit(solution)/shard_map/all_to_all | solution.py:1135
  48.4 21.0 %all-to-all-done.1 = bf16[8,128,768]{2,1,0:T(8,128)(2,1)S(1)} async-done(((bf16[8,128,768]{2,1,0:T(8,128)(2,1)}), bf16[8,128,768]{2,1,0:T(8,128)(2,1)S(1)}, u32[]{:S(2)}, u32[]{:S(2)}) %all-to-all-start.1) | async-done | bytes 1572896 | tf_op jit(solution)/shard_map/all_to_all | solution.py:1135
  69.4 1.1 copy-done.18
  70.6 38.4 %expert.1 = (bf16[1024,768]{1,0:T(8,128)(2,1)}, bf16[1024,768]{1,0:T(8,128)(2,1)}, bf16[8,192,768]{2,1,0:T(8,128)(2,1)}, bf16[8,192,768]{2,1,0:T(8,128)(2,1)}, b...) custom-call(s32[1]{0:T(128)} %bitcast.me_ref, s32[1]{0:T(128)} %bitcast.1.place_ref, ...), custom_call_target="tpu_custom_call" | custom-call | flops 28991029248 | bytes 18874368 | tf_op jit(solution)/shard_map/expert/pallas_call | solution.py:551
  109.0 5.3 %collective-permute-start.2 = (bf16[8,192,768]{2,1,0:T(8,128)(2,1)}, bf16[8,192,768]{2,1,0:T(8,128)(2,1)}, u32[]{:S(2)}, u32[]{:S(2)}) collective-permute-start(bf16[8,192,768]{2,1,0:T(8,128)(2,1)} %get-tuple-element.101.left_ref), channel_id=1, source_target_pairs={{0,8},{24,16},{1,9},{25,17},{2,10},{26,18},{3,11},{27,19},{4,12},{... | collective-permute-start | bytes 7077896 | tf_op jit(solution)/shard_map/ppermute | solution.py:918
  114.3 3.6 %all-to-all-start.2 = ((bf16[8,128,768]{2,1,0:T(8,128)(2,1)}), bf16[8,128,768]{2,1,0:T(8,128)(2,1)S(1)}, u32[]{:S(2)}, u32[]{:S(2)}) async-start(bf16[8,128,768]{2,1,0:T(8,128)(2,1)} %bitcast.21), calls=%async_computation.2 | async-start | bytes 3145728 | tf_op jit(solution)/shard_map/all_to_all | solution.py:1135
  117.9 2.7 collective-permute-start.1
  120.5 18.3 %all-to-all-done.2 = bf16[8,128,768]{2,1,0:T(8,128)(2,1)S(1)} async-done(((bf16[8,128,768]{2,1,0:T(8,128)(2,1)}), bf16[8,128,768]{2,1,0:T(8,128)(2,1)S(1)}, u32[]{:S(2)}, u32[]{:S(2)}) %all-to-all-start.2) | async-done | bytes 1572896 | tf_op jit(solution)/shard_map/all_to_all | solution.py:1135
  138.8 1.1 copy-done.19
  140.0 12.0 %combine.1 = (f32[1024,768]{1,0:T(8,128)}, bf16[1024,768]{1,0:T(8,128)(2,1)}, bf16[768,768]{1,0:T(8,128)(2,1)}, f32[8,768]{1,0:T(8,128)}) custom-call(s32[1]{0:T(128)S(6)} %copy.23.length_ref, bf16[1024,768]{1,0:T(8,128)(2,1)} %bitcast.24, s32[1024,128]{1,0:T(8,128)} %get-tuple-element.95.column_ref, bf16[1024,768]{1,0:T(8,128)(2,1)} %cotangent_ref.3, ...), custom_call_target="tpu_custom_call" | custom-call | flops 5637144576 | bytes 18874368 | tf_op jit(solution)/shard_map/combine/pallas_call | solution.py:639
  152.0 4.4 %all-to-all-start.3 = ((bf16[8,128,768]{2,1,0:T(8,128)(2,1)}), bf16[8,128,768]{2,1,0:T(8,128)(2,1)}, u32[]{:S(2)}, u32[]{:S(2)}) async-start(bf16[8,128,768]{2,1,0:T(8,128)(2,1)} %bitcast.19), calls=%async_computation.3 | async-start | bytes 3145728 | tf_op jit(solution)/shard_map/all_to_all | solution.py:1135
  156.4 8.5 %collective-permute-done.2.right_ref = bf16[8,192,768]{2,1,0:T(8,128)(2,1)} collective-permute-done((bf16[8,192,768]{2,1,0:T(8,128)(2,1)}, bf16[8,192,768]{2,1,0:T(8,128)(2,1)}, u32[]{:S(2)}, u32[]{:S(2)}) %collective-permute-start.2) | collective-permute-done | bytes 2359328 | tf_op jit(solution)/shard_map/ppermute | solution.py:918
  164.9 2.9 add.15
  167.8 2.1 collective-permute-start.6
  170.0 27.3 %attend_back.1.grads_ref = bf16[3,1024,768]{2,1,0:T(8,128)(2,1)} custom-call(s32[1]{0:T(128)S(6)} %copy.23.length_ref, bf16[1024,2304]{1,0:T(8,128)(2,1)} %copy-done.11, bf16[1024,2304]{1,0:T(8,128)(2,1)} %copy-done.11, bf16[1024,2304]{1,0:T(8,128)(2,1)} %copy-done.11, bf16[1024,768]{1,0:T(8,128)(2,1)} %copy-done.13, f32[1024,128]{1,0:T(8,128)} %copy-done.17, ...), custom_call_target="tpu_custom_call" | custom-call | flops 24159191040 | bytes 15728640 | tf_op jit(solution)/shard_map/attend_back/pallas_call | solution.py:313
  197.3 2.3 copy-done.12
  199.6 7.0 %pack.1 = (bf16[4,448,384]{2,1,0:T(8,128)(2,1)S(1)}, bf16[4,384,384]{2,1,0:T(8,128)(2,1)S(1)}, bf16[4,448,384]{2,1,0:T(8,128)(2,1)S(1)}, bf16[4,384,384]{2,1,0:T(8,128)(2,1)S(1)}) custom-call(s32[1]{0:T(128)} %bitcast.me_ref, bf16[3,1024,768]{2,1,0:T(8,128)(2,1)S(1)} %copy-done.12, bf16[1024,768]{1,0:T(8,128)(2,1)S(1)} %copy-done.9, f32[4,768]{1,0:T(4,128)S(1)} %copy-done.7, ...), custom_call_target="tpu_custom_call" | custom-call | flops 3623878656 | bytes 15728640 | tf_op jit(solution)/shard_map/pack/pallas_call | solution.py:771
  206.6 0.1 collective-permute-start.3
  206.7 0.5 collective-permute-start.4
  207.2 4.3 %collective-permute-done.4.refs_3_ = bf16[4,384,384]{2,1,0:T(8,128)(2,1)S(1)} collective-permute-done((bf16[4,384,384]{2,1,0:T(8,128)(2,1)S(1)}, bf16[4,384,384]{2,1,0:T(8,128)(2,1)S(1)}, u32[]{:S(2)}, u32[]{:S(2)}) %collective-permute-start.4) | collective-permute-done | bytes 1179680 | tf_op jit(solution)/shard_map/ppermute | solution.py:1172
  211.5 0.7 halves.2
  212.2 0.5 collective-permute-start.8
  212.7 0.7 collective-permute-start.9
  213.4 1.5 add.16
  214.9 1.3 collective-permute-start.7
  216.3 1.9 add.14
  218.2 0.9 collective-permute-start.5
  219.1 9.3 %collective-permute-start = (bf16[4,192,768]{2,1,0:T(8,128)(2,1)S(1)}, bf16[4,192,768]{2,1,0:T(8,128)(2,1)S(1)}, u32[]{:S(2)}, u32[]{:S(2)}) collective-permute-start(bf16[4,192,768]{2,1,0:T(8,128)(2,1)S(1)} %copy-done.20), channel_id=1, source_target_pairs={{0,8},{24,16},{1,9},{25,17},{2,10},{26,18},{3,11},{27,19},{4,12},{... | collective-permute-start | bytes 3538952 | tf_op jit(solution)/shard_map/ppermute | solution.py:918
  228.4 1.3 collective-permute-done.8.refs_1_
  229.7 0.4 halves.3
  230.2 1.0 collective-permute-start.10
  231.1 4.5 %collective-permute-start.11 = (bf16[4,96,384]{2,1,0:T(8,128)(2,1)S(1)}, bf16[4,96,384]{2,1,0:T(8,128)(2,1)S(1)}, u32[]{:S(2)}, u32[]{:S(2)}) collective-permute-start(bf16[4,96,384]{2,1,0:T(8,128)(2,1)S(1)} %get-tuple-element.132), channel_id=1, source_target_pairs={{0,2},{1,3},{2,0},{3,1},{4,6},{5,7},{6,4},{7,5},{8,10},{9,11},{10,... | collective-permute-start | bytes 884744 | tf_op jit(solution)/shard_map/ppermute | solution.py:1172
  235.7 6.6 %project_back.1 = bf16[1024,768]{1,0:T(8,128)(2,1)} custom-call(bf16[3,1024,768]{2,1,0:T(8,128)(2,1)S(1)} %copy-done.12, bf16[1024,768]{1,0:T(8,128)(2,1)S(1)} %copy-done.10, f32[1024,768]{1,0:T(8,128)S(1)} %copy-done.15, bf16[768,2304]{1,0:T(8,128)(2,1)S(1)} %copy-done.2, f32[4,768]{1,0:T(4,128)S(1)} %copy-done.7), custom_call_target="tpu_custom_call" | custom-call | flops 10871635968 | bytes 47185920 | tf_op jit(solution)/shard_map/project_back/pallas_call | solution.py:816
  242.3 4.0 %collective-permute-done.7.refs_2_ = bf16[4,192,768]{2,1,0:T(8,128)(2,1)S(1)} collective-permute-done((bf16[4,192,768]{2,1,0:T(8,128)(2,1)S(1)}, bf16[4,192,768]{2,1,0:T(8,128)(2,1)S(1)}, u32[]{:S(2)}, u32[]{:S(2)}) %collective-permute-start.7) | collective-permute-done | bytes 1179680 | tf_op jit(solution)/shard_map/ppermute | solution.py:918
  246.3 5.6 %collective-permute-done.refs_0_ = bf16[4,192,768]{2,1,0:T(8,128)(2,1)S(1)} collective-permute-done((bf16[4,192,768]{2,1,0:T(8,128)(2,1)S(1)}, bf16[4,192,768]{2,1,0:T(8,128)(2,1)S(1)}, u32[]{:S(2)}, u32[]{:S(2)}) %collective-permute-start) | collective-permute-done | bytes 1179680 | tf_op jit(solution)/shard_map/ppermute | solution.py:918
  251.9 1.0 copy-done.23
  252.9 0.2 join.1
  253.1 0.8 copy-done.4
  253.9 4.8 %all-to-all-start.4 = ((bf16[4,208,384]{2,1,0:T(8,128)(2,1)}), bf16[4,208,384]{2,1,0:T(8,128)(2,1)S(1)}, u32[]{:S(2)}, u32[]{:S(2)}) async-start(bf16[4,208,384]{2,1,0:T(8,128)(2,1)} %copy-done.4), calls=%async_computation.4 | async-start | bytes 1277952 | tf_op jit(solution)/shard_map/all_to_all | solution.py:1135
  258.7 2.3 add.18
  260.9 1.3 collective-permute-start.14
  262.2 2.6 add.17
  264.8 1.7 collective-permute-start.13
  266.5 9.8 %collective-permute-start.12 = (bf16[4,192,768]{2,1,0:T(8,128)(2,1)}, bf16[4,192,768]{2,1,0:T(8,128)(2,1)}, u32[]{:S(2)}, u32[]{:S(2)}) collective-permute-start(bf16[4,192,768]{2,1,0:T(8,128)(2,1)} %get-tuple-element.156.middle_ref), channel_id=1, source_target_pairs={{0,8},{24,16},{1,9},{25,17},{2,10},{26,18},{3,11},{27,19},{4,12},{... | collective-permute-start | bytes 3538952 | tf_op jit(solution)/shard_map/ppermute | solution.py:918
  276.3 1.2 spread.1
  277.5 5.8 %all-to-all-start.5 = ((bf16[8,208,384]{2,1,0:T(8,128)(2,1)}), bf16[8,208,384]{2,1,0:T(8,128)(2,1)S(1)}, u32[]{:S(2)}, u32[]{:S(2)}) async-start(bf16[8,208,384]{2,1,0:T(8,128)(2,1)} %spread.1), calls=%async_computation.5 | async-start | bytes 2555904 | tf_op jit(solution)/shard_map/all_to_all | solution.py:1135
  283.3 4.0 %line_total.3 = f32[768,768]{1,0:T(8,128)} custom-call(s32[1]{0:T(128)} %bitcast.1.place_ref, bf16[4,192,768]{2,1,0:T(8,128)(2,1)} %get-tuple-element.98.middle_ref, bf16[8,192,768]{2,1,0:T(8,128)(2,1)} %get-tuple-element.120.left_ref.end_ref, bf16[4,192,768]{2,1,0:T(8,128)(2,1)} %copy-done.23, bf16[4,192,768]{2,1,0:T(8,128)(2,1)} %copy-done.22, ...), custom_call_target="tpu_custom_call" | custom-call | tf_op jit(solution)/shard_map/line_total/pallas_call | solution.py:872
  287.4 6.1 %layer.1 = bf16[1024,768]{1,0:T(8,128)(2,1)} custom-call(s32[1]{0:T(128)S(6)} %copy.23.length_ref, bf16[1024,768]{1,0:T(8,128)(2,1)} %bitcast.12.returned_ref, s32[1024,128]{1,0:T(8,128)} %get-tuple-element.95.column_ref, f32[1024,768]{1,0:T(8,128)} %get-tuple-element.106.residual_ref, f32[1024,128]{1,0:T(8,128)} %get-tuple-element.151.gate_ref), custom_call_target="tpu_custom_call" | custom-call | flops 1610612736 | bytes 7864320 | tf_op jit(solution)/shard_map/layer/pallas_call | solution.py:684
  293.5 7.7 %all-to-all-done.5.gathered_ref = bf16[8,208,384]{2,1,0:T(8,128)(2,1)S(1)} async-done(((bf16[8,208,384]{2,1,0:T(8,128)(2,1)}), bf16[8,208,384]{2,1,0:T(8,128)(2,1)S(1)}, u32[]{:S(2)}, u32[]{:S(2)}) %all-to-all-start.5) | async-done | bytes 1277984 | tf_op jit(solution)/shard_map/all_to_all | solution.py:1135
  301.2 2.0 copy-done.3
  303.2 1.8 assemble.1
  305.0 0.2 slice_reduce_fusion
  305.2 0.6 dynamic-slice_divide_fusion
  305.9 0.6 fusion
  306.5 4.0 %line_total.2 = f32[192,3072]{1,0:T(8,128)} custom-call(s32[1]{0:T(128)} %bitcast.1.place_ref, bf16[4,192,768]{2,1,0:T(8,128)(2,1)} %get-tuple-element.156.middle_ref, bf16[8,192,768]{2,1,0:T(8,128)(2,1)} %get-tuple-element.120.left_ref.end_ref, bf16[4,192,768]{2,1,0:T(8,128)(2,1)} %collective-permute-done.12.refs_0_, ...), custom_call_target="tpu_custom_call" | custom-call | tf_op jit(solution)/shard_map/line_total/pallas_call | solution.py:872
  (67 shorter events, 0.2 us)
Async XLA Ops:
  1.3 10.8 %copy-start.1 = (bf16[768,2304]{1,0:T(8,128)(2,1)S(1)}, bf16[768,2304]{1,0:T(8,128)(2,1)}, u32[]{:S(2)}) copy-start(bf16[768,2304]{1,0:T(8,128)(2,1)} %weight_ref.9) | copy-start | bytes 10616836
  6.6 5.3 %copy-start.25 = (f32[768]{0:T(1024)S(1)}, f32[768]{0:T(1024)}, u32[]{:S(2)}) copy-start(f32[768]{0:T(1024)} %param.19) | copy-start | bytes 9220
  6.6 5.4 %copy-start.24 = (f32[768]{0:T(1024)S(1)}, f32[768]{0:T(1024)}, u32[]{:S(2)}) copy-start(f32[768]{0:T(1024)} %param.20) | copy-start | bytes 9220
  6.6 5.4 %copy-start.27 = (f32[768]{0:T(1024)S(1)}, f32[768]{0:T(1024)}, u32[]{:S(2)}) copy-start(f32[768]{0:T(1024)} %param.21) | copy-start | bytes 9220
  6.6 5.4 %copy-start.28 = (f32[768]{0:T(1024)S(1)}, f32[768]{0:T(1024)}, u32[]{:S(2)}) copy-start(f32[768]{0:T(1024)} %param.22) | copy-start | bytes 9220
  6.6 30.0 %all-to-all-start = ((bf16[8,128,768]{2,1,0:T(8,128)(2,1)}), bf16[8,128,768]{2,1,0:T(8,128)(2,1)}, u32[]{:S(2)}, u32[]{:S(2)}) async-start(bf16[8,128,768]{2,1,0:T(8,128)(2,1)} %bitcast.22), calls=%async_computation | async-start | bytes 3145728 | tf_op jit(solution)/shard_map/all_to_all | solution.py:1135
  12.1 1.4 copy-start.8
  13.5 5.2 %copy-start.6 = (f32[4,768]{1,0:T(4,128)}, f32[4,768]{1,0:T(4,128)S(1)}, u32[]{:S(2)}) copy-start(f32[4,768]{1,0:T(4,128)S(1)} %pad_maximum_fusion.norms_ref) | copy-start | bytes 36868
  32.6 2.2 copy-start.11
  34.7 1.1 copy-start.13
  35.9 0.8 copy-start.17
  44.2 25.3 %all-to-all-start.1 = ((bf16[8,128,768]{2,1,0:T(8,128)(2,1)}), bf16[8,128,768]{2,1,0:T(8,128)(2,1)S(1)}, u32[]{:S(2)}, u32[]{:S(2)}) async-start(bf16[8,128,768]{2,1,0:T(8,128)(2,1)} %bitcast.23), calls=%async_computation.1 | async-start | bytes 3145728 | tf_op jit(solution)/shard_map/all_to_all | solution.py:1135
  69.4 1.1 copy-start.18
  109.0 55.9 %collective-permute-start.2 = (bf16[8,192,768]{2,1,0:T(8,128)(2,1)}, bf16[8,192,768]{2,1,0:T(8,128)(2,1)}, u32[]{:S(2)}, u32[]{:S(2)}) collective-permute-start(bf16[8,192,768]{2,1,0:T(8,128)(2,1)} %get-tuple-element.101.left_ref), channel_id=1, source_target_pairs={{0,8},{24,16},{1,9},{25,17},{2,10},{26,18},{3,11},{27,19},{4,12},{... | collective-permute-start | bytes 7077896 | tf_op jit(solution)/shard_map/ppermute | solution.py:918
  114.3 24.5 %all-to-all-start.2 = ((bf16[8,128,768]{2,1,0:T(8,128)(2,1)}), bf16[8,128,768]{2,1,0:T(8,128)(2,1)S(1)}, u32[]{:S(2)}, u32[]{:S(2)}) async-start(bf16[8,128,768]{2,1,0:T(8,128)(2,1)} %bitcast.21), calls=%async_computation.2 | async-start | bytes 3145728 | tf_op jit(solution)/shard_map/all_to_all | solution.py:1135
  117.9 95.5 %collective-permute-start.1 = (bf16[8,192,768]{2,1,0:T(8,128)(2,1)}, bf16[8,192,768]{2,1,0:T(8,128)(2,1)}, u32[]{:S(2)}, u32[]{:S(2)}) collective-permute-start(bf16[8,192,768]{2,1,0:T(8,128)(2,1)} %get-tuple-element.99.left_ref), channel_id=1, source_target_pairs={{0,8},{24,16},{1,9},{25,17},{2,10},{26,18},{3,11},{27,19},{4,12},{... | collective-permute-start | bytes 7077896 | tf_op jit(solution)/shard_map/ppermute | solution.py:918
  138.8 1.1 copy-start.19
  151.9 12.9 %copy-start.5 = (bf16[8,192,768]{2,1,0:T(8,128)(2,1)S(1)}, bf16[8,192,768]{2,1,0:T(8,128)(2,1)}, u32[]{:S(2)}) copy-start(bf16[8,192,768]{2,1,0:T(8,128)(2,1)} %get-tuple-element.101.left_ref) | copy-start | bytes 7077892
  152.0 45.3 %all-to-all-start.3 = ((bf16[8,128,768]{2,1,0:T(8,128)(2,1)}), bf16[8,128,768]{2,1,0:T(8,128)(2,1)}, u32[]{:S(2)}, u32[]{:S(2)}) async-start(bf16[8,128,768]{2,1,0:T(8,128)(2,1)} %bitcast.19), calls=%async_computation.3 | async-start | bytes 3145728 | tf_op jit(solution)/shard_map/all_to_all | solution.py:1135
  167.8 45.6 %collective-permute-start.6 = (bf16[8,192,768]{2,1,0:T(8,128)(2,1)}, bf16[8,192,768]{2,1,0:T(8,128)(2,1)}, u32[]{:S(2)}, u32[]{:S(2)}) collective-permute-start(bf16[8,192,768]{2,1,0:T(8,128)(2,1)} %add.15), channel_id=1, source_target_pairs={{8,16},{16,8},{9,17},{17,9},{10,18},{18,10},{11,19},{19,11},{12,20... | collective-permute-start | bytes 7077896 | tf_op jit(solution)/shard_map/ppermute | solution.py:918
  169.9 27.3 %copy-start.7 = (f32[4,768]{1,0:T(4,128)S(1)}, f32[4,768]{1,0:T(4,128)}, u32[]{:S(2)}) copy-start(f32[4,768]{1,0:T(4,128)} %copy-done.6) | copy-start | bytes 36868
  169.9 27.3 %copy-start.9 = (bf16[1024,768]{1,0:T(8,128)(2,1)S(1)}, bf16[1024,768]{1,0:T(8,128)(2,1)}, u32[]{:S(2)}) copy-start(bf16[1024,768]{1,0:T(8,128)(2,1)} %tokens_ref.6) | copy-start | bytes 4718596
  169.9 27.3 %copy-start.14 = (bf16[768,768]{1,0:T(8,128)(2,1)S(1)}, bf16[768,768]{1,0:T(8,128)(2,1)}, u32[]{:S(2)}) copy-start(bf16[768,768]{1,0:T(8,128)(2,1)} %get-tuple-element.112.output_grad_ref) | copy-start | bytes 3538948
  169.9 27.3 %copy-start.16 = (f32[8,768]{1,0:T(8,128)S(1)}, f32[8,768]{1,0:T(8,128)}, u32[]{:S(2)}) copy-start(f32[8,768]{1,0:T(8,128)} %get-tuple-element.113.second_ref) | copy-start | bytes 73732
  197.3 2.3 copy-start.12
  206.6 4.9 %collective-permute-start.3 = (bf16[4,448,384]{2,1,0:T(8,128)(2,1)S(1)}, bf16[4,448,384]{2,1,0:T(8,128)(2,1)S(1)}, u32[]{:S(2)}, u32[]{:S(2)}) collective-permute-start(bf16[4,448,384]{2,1,0:T(8,128)(2,1)S(1)} %get-tuple-element.115), channel_id=1, source_target_pairs={{0,1},{1,0},{2,3},{3,2},{4,5},{5,4},{6,7},{7,6},{8,9},{9,8},{10,11... | collective-permute-start | bytes 4128776 | tf_op jit(solution)/shard_map/ppermute | solution.py:1172
  206.7 4.8 %collective-permute-start.4 = (bf16[4,384,384]{2,1,0:T(8,128)(2,1)S(1)}, bf16[4,384,384]{2,1,0:T(8,128)(2,1)S(1)}, u32[]{:S(2)}, u32[]{:S(2)}) collective-permute-start(bf16[4,384,384]{2,1,0:T(8,128)(2,1)S(1)} %get-tuple-element.117), channel_id=1, source_target_pairs={{0,1},{1,0},{2,3},{3,2},{4,5},{5,4},{6,7},{7,6},{8,9},{9,8},{10,11... | collective-permute-start | bytes 3538952 | tf_op jit(solution)/shard_map/ppermute | solution.py:1172
  211.5 1.9 copy-start
  212.2 17.5 %collective-permute-start.8 = (bf16[4,224,384]{2,1,0:T(8,128)(2,1)S(1)}, bf16[4,224,384]{2,1,0:T(8,128)(2,1)S(1)}, u32[]{:S(2)}, u32[]{:S(2)}) collective-permute-start(bf16[4,224,384]{2,1,0:T(8,128)(2,1)S(1)} %get-tuple-element.126), channel_id=1, source_target_pairs={{0,2},{1,3},{2,0},{3,1},{4,6},{5,7},{6,4},{7,5},{8,10},{9,11},{10,... | collective-permute-start | bytes 2064392 | tf_op jit(solution)/shard_map/ppermute | solution.py:1172
  212.7 15.7 %collective-permute-start.9 = (bf16[4,192,384]{2,1,0:T(8,128)(2,1)S(1)}, bf16[4,192,384]{2,1,0:T(8,128)(2,1)S(1)}, u32[]{:S(2)}, u32[]{:S(2)}) collective-permute-start(bf16[4,192,384]{2,1,0:T(8,128)(2,1)S(1)} %get-tuple-element.128), channel_id=1, source_target_pairs={{0,4},{1,5},{2,6},{3,7},{4,0},{5,1},{6,2},{7,3},{8,12},{9,13},{10,... | collective-permute-start | bytes 1769480 | tf_op jit(solution)/shard_map/ppermute | solution.py:1172
  213.4 5.7 %copy-start.20 = (bf16[4,192,768]{2,1,0:T(8,128)(2,1)S(1)}, bf16[4,192,768]{2,1,0:T(8,128)(2,1)}, u32[]{:S(2)}) copy-start(bf16[4,192,768]{2,1,0:T(8,128)(2,1)} %get-tuple-element.98.middle_ref) | copy-start | bytes 3538948
  214.9 31.4 %collective-permute-start.7 = (bf16[4,192,768]{2,1,0:T(8,128)(2,1)S(1)}, bf16[4,192,768]{2,1,0:T(8,128)(2,1)S(1)}, u32[]{:S(2)}, u32[]{:S(2)}) collective-permute-start(bf16[4,192,768]{2,1,0:T(8,128)(2,1)S(1)} %add.16), channel_id=1, source_target_pairs={{16,24},{8,0},{17,25},{9,1},{18,26},{10,2},{19,27},{11,3},{20,28},... | collective-permute-start | bytes 3538952 | tf_op jit(solution)/shard_map/ppermute | solution.py:918
  216.2 19.4 %copy-start.2 = (bf16[768,2304]{1,0:T(8,128)(2,1)S(1)}, bf16[768,2304]{1,0:T(8,128)(2,1)}, u32[]{:S(2)}) copy-start(bf16[768,2304]{1,0:T(8,128)(2,1)} %weight_ref.9) | copy-start | bytes 10616836
  216.3 19.4 %copy-start.15 = (f32[1024,768]{1,0:T(8,128)S(1)}, f32[1024,768]{1,0:T(8,128)}, u32[]{:S(2)}) copy-start(f32[1024,768]{1,0:T(8,128)} %get-tuple-element.124.residual_grad_ref) | copy-start | bytes 9437188
  218.2 17.5 %copy-start.10 = (bf16[1024,768]{1,0:T(8,128)(2,1)S(1)}, bf16[1024,768]{1,0:T(8,128)(2,1)}, u32[]{:S(2)}) copy-start(bf16[1024,768]{1,0:T(8,128)(2,1)} %tokens_ref.6) | copy-start | bytes 4718596
  218.2 28.1 %collective-permute-start.5 = (bf16[4,192,768]{2,1,0:T(8,128)(2,1)S(1)}, bf16[4,192,768]{2,1,0:T(8,128)(2,1)S(1)}, u32[]{:S(2)}, u32[]{:S(2)}) collective-permute-start(bf16[4,192,768]{2,1,0:T(8,128)(2,1)S(1)} %add.14), channel_id=1, source_target_pairs={{8,16},{16,8},{9,17},{17,9},{10,18},{18,10},{11,19},{19,11},{12,20... | collective-permute-start | bytes 3538952 | tf_op jit(solution)/shard_map/ppermute | solution.py:918
  219.1 32.8 %collective-permute-start = (bf16[4,192,768]{2,1,0:T(8,128)(2,1)S(1)}, bf16[4,192,768]{2,1,0:T(8,128)(2,1)S(1)}, u32[]{:S(2)}, u32[]{:S(2)}) collective-permute-start(bf16[4,192,768]{2,1,0:T(8,128)(2,1)S(1)} %copy-done.20), channel_id=1, source_target_pairs={{0,8},{24,16},{1,9},{25,17},{2,10},{26,18},{3,11},{27,19},{4,12},{... | collective-permute-start | bytes 3538952 | tf_op jit(solution)/shard_map/ppermute | solution.py:918
  230.2 12.1 %collective-permute-start.10 = (bf16[4,112,384]{2,1,0:T(8,128)(2,1)S(1)}, bf16[4,112,384]{2,1,0:T(8,128)(2,1)S(1)}, u32[]{:S(2)}, u32[]{:S(2)}) collective-permute-start(bf16[4,112,384]{2,1,0:T(8,128)(2,1)S(1)} %get-tuple-element.130), channel_id=1, source_target_pairs={{0,4},{1,5},{2,6},{3,7},{4,0},{5,1},{6,2},{7,3},{8,12},{9,13},{10,... | collective-permute-start | bytes 1032200 | tf_op jit(solution)/shard_map/ppermute | solution.py:1172
  231.1 11.1 %collective-permute-start.11 = (bf16[4,96,384]{2,1,0:T(8,128)(2,1)S(1)}, bf16[4,96,384]{2,1,0:T(8,128)(2,1)S(1)}, u32[]{:S(2)}, u32[]{:S(2)}) collective-permute-start(bf16[4,96,384]{2,1,0:T(8,128)(2,1)S(1)} %get-tuple-element.132), channel_id=1, source_target_pairs={{0,2},{1,3},{2,0},{3,1},{4,6},{5,7},{6,4},{7,5},{8,10},{9,11},{10,... | collective-permute-start | bytes 884744 | tf_op jit(solution)/shard_map/ppermute | solution.py:1172
  246.3 5.6 %copy-start.21 = (bf16[4,192,768]{2,1,0:T(8,128)(2,1)}, bf16[4,192,768]{2,1,0:T(8,128)(2,1)S(1)}, u32[]{:S(2)}) copy-start(bf16[4,192,768]{2,1,0:T(8,128)(2,1)S(1)} %collective-permute-done.7.refs_2_) | copy-start | bytes 3538948
  246.3 5.6 %copy-start.22 = (bf16[4,192,768]{2,1,0:T(8,128)(2,1)}, bf16[4,192,768]{2,1,0:T(8,128)(2,1)S(1)}, u32[]{:S(2)}) copy-start(bf16[4,192,768]{2,1,0:T(8,128)(2,1)S(1)} %collective-permute-done.5.refs_1_) | copy-start | bytes 3538948
  251.9 1.0 copy-start.23
  253.1 0.8 copy-start.4
  253.9 22.4 %all-to-all-start.4 = ((bf16[4,208,384]{2,1,0:T(8,128)(2,1)}), bf16[4,208,384]{2,1,0:T(8,128)(2,1)S(1)}, u32[]{:S(2)}, u32[]{:S(2)}) async-start(bf16[4,208,384]{2,1,0:T(8,128)(2,1)} %copy-done.4), calls=%async_computation.4 | async-start | bytes 1277952 | tf_op jit(solution)/shard_map/all_to_all | solution.py:1135
  260.9 44.0 %collective-permute-start.14 = (bf16[4,192,768]{2,1,0:T(8,128)(2,1)}, bf16[4,192,768]{2,1,0:T(8,128)(2,1)}, u32[]{:S(2)}, u32[]{:S(2)}) collective-permute-start(bf16[4,192,768]{2,1,0:T(8,128)(2,1)} %add.18), channel_id=1, source_target_pairs={{16,24},{8,0},{17,25},{9,1},{18,26},{10,2},{19,27},{11,3},{20,28},... | collective-permute-start | bytes 3538952 | tf_op jit(solution)/shard_map/ppermute | solution.py:918
  264.8 40.2 %collective-permute-start.13 = (bf16[4,192,768]{2,1,0:T(8,128)(2,1)}, bf16[4,192,768]{2,1,0:T(8,128)(2,1)}, u32[]{:S(2)}, u32[]{:S(2)}) collective-permute-start(bf16[4,192,768]{2,1,0:T(8,128)(2,1)} %add.17), channel_id=1, source_target_pairs={{8,16},{16,8},{9,17},{17,9},{10,18},{18,10},{11,19},{19,11},{12,20... | collective-permute-start | bytes 3538952 | tf_op jit(solution)/shard_map/ppermute | solution.py:918
  266.5 38.5 %collective-permute-start.12 = (bf16[4,192,768]{2,1,0:T(8,128)(2,1)}, bf16[4,192,768]{2,1,0:T(8,128)(2,1)}, u32[]{:S(2)}, u32[]{:S(2)}) collective-permute-start(bf16[4,192,768]{2,1,0:T(8,128)(2,1)} %get-tuple-element.156.middle_ref), channel_id=1, source_target_pairs={{0,8},{24,16},{1,9},{25,17},{2,10},{26,18},{3,11},{27,19},{4,12},{... | collective-permute-start | bytes 3538952 | tf_op jit(solution)/shard_map/ppermute | solution.py:918
  277.5 23.7 %all-to-all-start.5 = ((bf16[8,208,384]{2,1,0:T(8,128)(2,1)}), bf16[8,208,384]{2,1,0:T(8,128)(2,1)S(1)}, u32[]{:S(2)}, u32[]{:S(2)}) async-start(bf16[8,208,384]{2,1,0:T(8,128)(2,1)} %spread.1), calls=%async_computation.5 | async-start | bytes 2555904 | tf_op jit(solution)/shard_map/all_to_all | solution.py:1135
  301.2 2.0 copy-start.3
  305.2 5.3 %copy-start.26 = (f32[192]{0:T(256)}, f32[192]{0:T(256)S(1)}, u32[]{:S(2)}) copy-start(f32[192]{0:T(256)S(1)} %get-tuple-element.168) | copy-start | bytes 2308

commit v3 on v2

--- a/solution.py
+++ b/solution.py
@@ -94,7 +94,7 @@
 
 def route(length, expert_index, cotangent, experts):
     rows, width = cotangent.shape
-    block = 256
+    block = 512
     return pl.pallas_call(
         functools.partial(route_kernel, experts=experts),
         out_shape=[

time: 312 us -> 311 us (level)
  no operation moved by 1% of the time
where the time goes in v3:
time: 311 us; the launch traced here: 310 us
  Pallas kernels  152 us (49%)
  waiting for transfers between devices  70.7 us (23%)
  starting transfers between devices  69.9 us (22%)
  local copies, waits for them, and re-layouts  14.9 us (5%)
    all_to_all x6, waiting for transfers between devices, exchange(): return lax.all_to_all(values, axis, split_axis=0, concat_axis=0, tiled=True)  47 us
    pallas_call x1, Pallas kernels, expert(): pl.pallas_call(functools.partial(expert_kernel, shares=shares, together=t...  38.4 us
    ppermute x9, starting transfers between devices, send(): self.got[key] = lax.ppermute(values, self.axis, route)  34.4 us
    all_to_all x6, starting transfers between devices, exchange(): return lax.all_to_all(values, axis, split_axis=0, concat_axis=0, tiled=True)  28.2 us
    pallas_call x1, Pallas kernels, attend_back(): pl.pallas_call(functools.partial(attend_back_kernel, scale=size ** (-0.5)...  27.3 us
    ppermute x9, waiting for transfers between devices, send(): self.got[key] = lax.ppermute(values, self.axis, route)  18.1 us
    unnamed x58, local copies, waits for them, and re-layouts  14 us
    pallas_call x1, Pallas kernels, attend(): pl.pallas_call(functools.partial(attend_kernel, scale=size ** (-0.5), hal...  13.9 us
  transfers between devices with their start and end apart: 21, of which 8 were waited for; matrix products, arithmetic and copies ran while one was open for 0% of the time, Pallas kernels for 31%

profile of v3, /device:TPU:0, one launch (start us, length us, event | category | flops | bytes accessed | tf_op | source)
XLA Modules:
  0.0 310.2 jit_solution(9016297890990831282)
XLA Ops:
  1.3 4.9 %route.1 = (bf16[1024,768]{1,0:T(8,128)(2,1)}, s32[8,1024]{1,0:T(8,128)}, s32[1024,128]{1,0:T(8,128)}) custom-call(s32[1]{0:T(128)S(6)} %copy.23.length_ref, s32[1,1024]{1,0:T(1,128)} %bitcast.29, bf16[1024,768]{1,0:T(8,128)(2,1)} %cotangent_ref.3), custom_call_target="tpu_custom_call" | custom-call | flops 1610612736 | bytes 3145728 | tf_op jit(solution)/shard_map/route/pallas_call | solution.py:98
  6.3 5.3 %all-to-all-start = ((bf16[8,128,768]{2,1,0:T(8,128)(2,1)}), bf16[8,128,768]{2,1,0:T(8,128)(2,1)}, u32[]{:S(2)}, u32[]{:S(2)}) async-start(bf16[8,128,768]{2,1,0:T(8,128)(2,1)} %bitcast.22), calls=%async_computation | async-start | bytes 3145728 | tf_op jit(solution)/shard_map/all_to_all | solution.py:1135
  11.7 1.4 copy-done.8
  13.1 5.2 %project.1.query_ref.key_ref.value_ref = bf16[1024,2304]{1,0:T(8,128)(2,1)S(1)} custom-call(bf16[1024,768]{1,0:T(8,128)(2,1)S(1)} %copy-done.8, bf16[768,2304]{1,0:T(8,128)(2,1)S(1)} %copy-done.1, f32[4,768]{1,0:T(4,128)S(1)} %pad_maximum_fusion.norms_ref), custom_call_target="tpu_custom_call" | custom-call | flops 3623878656 | bytes 8257536 | tf_op jit(solution)/shard_map/project/pallas_call | solution.py:134
  18.3 13.9 %attend.1 = (bf16[1024,768]{1,0:T(8,128)(2,1)S(1)}, f32[1024,128]{1,0:T(8,128)S(1)}) custom-call(s32[1]{0:T(128)S(6)} %copy.23.length_ref, bf16[1024,2304]{1,0:T(8,128)(2,1)S(1)} %project.1.query_ref.key_ref.value_ref, bf16[1024,2304]{1,0:T(8,128)(2,1)S(1)} %project.1.query_ref.key_ref.value_ref, bf16[1024,2304]{1,0:T(8,128)(2,1)S(1)} %project.1.query_ref.key_ref.value_ref), custom_call_target="tpu_custom_call" | custom-call | flops 12884901888 | bytes 9437184 | tf_op jit(solution)/shard_map/attend/pallas_call | solution.py:215
  32.2 2.2 copy-done.11
  34.4 1.1 copy-done.13
  35.5 0.8 copy-done.17
  36.3 7.5 %hidden_rows.1 = (f32[1024,768]{1,0:T(8,128)}, f32[1024,128]{1,0:T(8,128)}, bf16[1024,768]{1,0:T(8,128)(2,1)}) custom-call(s32[1]{0:T(128)S(6)} %copy.23.length_ref, bf16[1024,768]{1,0:T(8,128)(2,1)} %copy-done.13, bf16[1024,768]{1,0:T(8,128)(2,1)} %tokens_ref.6, bf16[768,768]{1,0:T(8,128)(2,1)} %weight_ref.7, f32[4,768]{1,0:T(4,128)} %copy-done.6, ...), custom_call_target="tpu_custom_call" | custom-call | flops 2818572288 | bytes 9437184 | tf_op jit(solution)/shard_map/hidden_rows/pallas_call | solution.py:390
  43.8 4.3 %all-to-all-start.1 = ((bf16[8,128,768]{2,1,0:T(8,128)(2,1)}), bf16[8,128,768]{2,1,0:T(8,128)(2,1)S(1)}, u32[]{:S(2)}, u32[]{:S(2)}) async-start(bf16[8,128,768]{2,1,0:T(8,128)(2,1)} %bitcast.23), calls=%async_computation.1 | async-start | bytes 3145728 | tf_op jit(solution)/shard_map/all_to_all | solution.py:1135
  48.0 21.0 %all-to-all-done.1 = bf16[8,128,768]{2,1,0:T(8,128)(2,1)S(1)} async-done(((bf16[8,128,768]{2,1,0:T(8,128)(2,1)}), bf16[8,128,768]{2,1,0:T(8,128)(2,1)S(1)}, u32[]{:S(2)}, u32[]{:S(2)}) %all-to-all-start.1) | async-done | bytes 1572896 | tf_op jit(solution)/shard_map/all_to_all | solution.py:1135
  69.1 1.1 copy-done.18
  70.2 38.4 %expert.1 = (bf16[1024,768]{1,0:T(8,128)(2,1)}, bf16[1024,768]{1,0:T(8,128)(2,1)}, bf16[8,192,768]{2,1,0:T(8,128)(2,1)}, bf16[8,192,768]{2,1,0:T(8,128)(2,1)}, b...) custom-call(s32[1]{0:T(128)} %bitcast.me_ref, s32[1]{0:T(128)} %bitcast.1.place_ref, ...), custom_call_target="tpu_custom_call" | custom-call | flops 28991029248 | bytes 18874368 | tf_op jit(solution)/shard_map/expert/pallas_call | solution.py:551
  108.6 5.3 %collective-permute-start.2 = (bf16[8,192,768]{2,1,0:T(8,128)(2,1)}, bf16[8,192,768]{2,1,0:T(8,128)(2,1)}, u32[]{:S(2)}, u32[]{:S(2)}) collective-permute-start(bf16[8,192,768]{2,1,0:T(8,128)(2,1)} %get-tuple-element.101.left_ref), channel_id=1, source_target_pairs={{0,8},{24,16},{1,9},{25,17},{2,10},{26,18},{3,11},{27,19},{4,12},{... | collective-permute-start | bytes 7077896 | tf_op jit(solution)/shard_map/ppermute | solution.py:918
  113.9 3.6 %all-to-all-start.2 = ((bf16[8,128,768]{2,1,0:T(8,128)(2,1)}), bf16[8,128,768]{2,1,0:T(8,128)(2,1)S(1)}, u32[]{:S(2)}, u32[]{:S(2)}) async-start(bf16[8,128,768]{2,1,0:T(8,128)(2,1)} %bitcast.21), calls=%async_computation.2 | async-start | bytes 3145728 | tf_op jit(solution)/shard_map/all_to_all | solution.py:1135
  117.5 2.7 collective-permute-start.1
  120.2 18.3 %all-to-all-done.2 = bf16[8,128,768]{2,1,0:T(8,128)(2,1)S(1)} async-done(((bf16[8,128,768]{2,1,0:T(8,128)(2,1)}), bf16[8,128,768]{2,1,0:T(8,128)(2,1)S(1)}, u32[]{:S(2)}, u32[]{:S(2)}) %all-to-all-start.2) | async-done | bytes 1572896 | tf_op jit(solution)/shard_map/all_to_all | solution.py:1135
  138.4 1.1 copy-done.19
  139.6 12.0 %combine.1 = (f32[1024,768]{1,0:T(8,128)}, bf16[1024,768]{1,0:T(8,128)(2,1)}, bf16[768,768]{1,0:T(8,128)(2,1)}, f32[8,768]{1,0:T(8,128)}) custom-call(s32[1]{0:T(128)S(6)} %copy.23.length_ref, bf16[1024,768]{1,0:T(8,128)(2,1)} %bitcast.24, s32[1024,128]{1,0:T(8,128)} %get-tuple-element.95.column_ref, bf16[1024,768]{1,0:T(8,128)(2,1)} %cotangent_ref.3, ...), custom_call_target="tpu_custom_call" | custom-call | flops 5637144576 | bytes 18874368 | tf_op jit(solution)/shard_map/combine/pallas_call | solution.py:639
  151.6 4.4 %all-to-all-start.3 = ((bf16[8,128,768]{2,1,0:T(8,128)(2,1)}), bf16[8,128,768]{2,1,0:T(8,128)(2,1)}, u32[]{:S(2)}, u32[]{:S(2)}) async-start(bf16[8,128,768]{2,1,0:T(8,128)(2,1)} %bitcast.19), calls=%async_computation.3 | async-start | bytes 3145728 | tf_op jit(solution)/shard_map/all_to_all | solution.py:1135
  156.0 8.5 %collective-permute-done.2.right_ref = bf16[8,192,768]{2,1,0:T(8,128)(2,1)} collective-permute-done((bf16[8,192,768]{2,1,0:T(8,128)(2,1)}, bf16[8,192,768]{2,1,0:T(8,128)(2,1)}, u32[]{:S(2)}, u32[]{:S(2)}) %collective-permute-start.2) | collective-permute-done | bytes 2359328 | tf_op jit(solution)/shard_map/ppermute | solution.py:918
  164.5 2.9 add.15
  167.5 2.1 collective-permute-start.6
  169.6 27.3 %attend_back.1.grads_ref = bf16[3,1024,768]{2,1,0:T(8,128)(2,1)} custom-call(s32[1]{0:T(128)S(6)} %copy.23.length_ref, bf16[1024,2304]{1,0:T(8,128)(2,1)} %copy-done.11, bf16[1024,2304]{1,0:T(8,128)(2,1)} %copy-done.11, bf16[1024,2304]{1,0:T(8,128)(2,1)} %copy-done.11, bf16[1024,768]{1,0:T(8,128)(2,1)} %copy-done.13, f32[1024,128]{1,0:T(8,128)} %copy-done.17, ...), custom_call_target="tpu_custom_call" | custom-call | flops 24159191040 | bytes 15728640 | tf_op jit(solution)/shard_map/attend_back/pallas_call | solution.py:313
  196.9 2.3 copy-done.12
  199.3 7.0 %pack.1 = (bf16[4,448,384]{2,1,0:T(8,128)(2,1)S(1)}, bf16[4,384,384]{2,1,0:T(8,128)(2,1)S(1)}, bf16[4,448,384]{2,1,0:T(8,128)(2,1)S(1)}, bf16[4,384,384]{2,1,0:T(8,128)(2,1)S(1)}) custom-call(s32[1]{0:T(128)} %bitcast.me_ref, bf16[3,1024,768]{2,1,0:T(8,128)(2,1)S(1)} %copy-done.12, bf16[1024,768]{1,0:T(8,128)(2,1)S(1)} %copy-done.9, f32[4,768]{1,0:T(4,128)S(1)} %copy-done.7, ...), custom_call_target="tpu_custom_call" | custom-call | flops 3623878656 | bytes 15728640 | tf_op jit(solution)/shard_map/pack/pallas_call | solution.py:771
  206.2 0.1 collective-permute-start.3
  206.3 0.5 collective-permute-start.4
  206.8 4.3 %collective-permute-done.4.refs_3_ = bf16[4,384,384]{2,1,0:T(8,128)(2,1)S(1)} collective-permute-done((bf16[4,384,384]{2,1,0:T(8,128)(2,1)S(1)}, bf16[4,384,384]{2,1,0:T(8,128)(2,1)S(1)}, u32[]{:S(2)}, u32[]{:S(2)}) %collective-permute-start.4) | collective-permute-done | bytes 1179680 | tf_op jit(solution)/shard_map/ppermute | solution.py:1172
  211.1 0.7 halves.2
  211.8 0.5 collective-permute-start.8
  212.3 0.7 collective-permute-start.9
  213.0 1.5 add.16
  214.6 1.3 collective-permute-start.7
  215.9 1.9 add.14
  217.8 0.9 collective-permute-start.5
  218.7 9.3 %collective-permute-start = (bf16[4,192,768]{2,1,0:T(8,128)(2,1)S(1)}, bf16[4,192,768]{2,1,0:T(8,128)(2,1)S(1)}, u32[]{:S(2)}, u32[]{:S(2)}) collective-permute-start(bf16[4,192,768]{2,1,0:T(8,128)(2,1)S(1)} %copy-done.20), channel_id=1, source_target_pairs={{0,8},{24,16},{1,9},{25,17},{2,10},{26,18},{3,11},{27,19},{4,12},{... | collective-permute-start | bytes 3538952 | tf_op jit(solution)/shard_map/ppermute | solution.py:918
  228.1 1.3 collective-permute-done.8.refs_1_
  229.4 0.4 halves.3
  229.8 1.0 collective-permute-start.10
  230.8 4.5 %collective-permute-start.11 = (bf16[4,96,384]{2,1,0:T(8,128)(2,1)S(1)}, bf16[4,96,384]{2,1,0:T(8,128)(2,1)S(1)}, u32[]{:S(2)}, u32[]{:S(2)}) collective-permute-start(bf16[4,96,384]{2,1,0:T(8,128)(2,1)S(1)} %get-tuple-element.132), channel_id=1, source_target_pairs={{0,2},{1,3},{2,0},{3,1},{4,6},{5,7},{6,4},{7,5},{8,10},{9,11},{10,... | collective-permute-start | bytes 884744 | tf_op jit(solution)/shard_map/ppermute | solution.py:1172
  235.3 6.6 %project_back.1 = bf16[1024,768]{1,0:T(8,128)(2,1)} custom-call(bf16[3,1024,768]{2,1,0:T(8,128)(2,1)S(1)} %copy-done.12, bf16[1024,768]{1,0:T(8,128)(2,1)S(1)} %copy-done.10, f32[1024,768]{1,0:T(8,128)S(1)} %copy-done.15, bf16[768,2304]{1,0:T(8,128)(2,1)S(1)} %copy-done.2, f32[4,768]{1,0:T(4,128)S(1)} %copy-done.7), custom_call_target="tpu_custom_call" | custom-call | flops 10871635968 | bytes 47185920 | tf_op jit(solution)/shard_map/project_back/pallas_call | solution.py:816
  241.9 4.0 %collective-permute-done.7.refs_2_ = bf16[4,192,768]{2,1,0:T(8,128)(2,1)S(1)} collective-permute-done((bf16[4,192,768]{2,1,0:T(8,128)(2,1)S(1)}, bf16[4,192,768]{2,1,0:T(8,128)(2,1)S(1)}, u32[]{:S(2)}, u32[]{:S(2)}) %collective-permute-start.7) | collective-permute-done | bytes 1179680 | tf_op jit(solution)/shard_map/ppermute | solution.py:918
  246.0 5.5 %collective-permute-done.refs_0_ = bf16[4,192,768]{2,1,0:T(8,128)(2,1)S(1)} collective-permute-done((bf16[4,192,768]{2,1,0:T(8,128)(2,1)S(1)}, bf16[4,192,768]{2,1,0:T(8,128)(2,1)S(1)}, u32[]{:S(2)}, u32[]{:S(2)}) %collective-permute-start) | collective-permute-done | bytes 1179680 | tf_op jit(solution)/shard_map/ppermute | solution.py:918
  251.5 1.0 copy-done.23
  252.5 0.2 join.1
  252.7 0.8 copy-done.4
  253.5 4.8 %all-to-all-start.4 = ((bf16[4,208,384]{2,1,0:T(8,128)(2,1)}), bf16[4,208,384]{2,1,0:T(8,128)(2,1)S(1)}, u32[]{:S(2)}, u32[]{:S(2)}) async-start(bf16[4,208,384]{2,1,0:T(8,128)(2,1)} %copy-done.4), calls=%async_computation.4 | async-start | bytes 1277952 | tf_op jit(solution)/shard_map/all_to_all | solution.py:1135
  258.3 2.3 add.18
  260.6 1.3 collective-permute-start.14
  261.9 2.6 add.17
  264.5 1.7 collective-permute-start.13
  266.1 9.8 %collective-permute-start.12 = (bf16[4,192,768]{2,1,0:T(8,128)(2,1)}, bf16[4,192,768]{2,1,0:T(8,128)(2,1)}, u32[]{:S(2)}, u32[]{:S(2)}) collective-permute-start(bf16[4,192,768]{2,1,0:T(8,128)(2,1)} %get-tuple-element.156.middle_ref), channel_id=1, source_target_pairs={{0,8},{24,16},{1,9},{25,17},{2,10},{26,18},{3,11},{27,19},{4,12},{... | collective-permute-start | bytes 3538952 | tf_op jit(solution)/shard_map/ppermute | solution.py:918
  276.0 1.2 spread.1
  277.1 5.8 %all-to-all-start.5 = ((bf16[8,208,384]{2,1,0:T(8,128)(2,1)}), bf16[8,208,384]{2,1,0:T(8,128)(2,1)S(1)}, u32[]{:S(2)}, u32[]{:S(2)}) async-start(bf16[8,208,384]{2,1,0:T(8,128)(2,1)} %spread.1), calls=%async_computation.5 | async-start | bytes 2555904 | tf_op jit(solution)/shard_map/all_to_all | solution.py:1135
  283.0 4.0 %line_total.3 = f32[768,768]{1,0:T(8,128)} custom-call(s32[1]{0:T(128)} %bitcast.1.place_ref, bf16[4,192,768]{2,1,0:T(8,128)(2,1)} %get-tuple-element.98.middle_ref, bf16[8,192,768]{2,1,0:T(8,128)(2,1)} %get-tuple-element.120.left_ref.end_ref, bf16[4,192,768]{2,1,0:T(8,128)(2,1)} %copy-done.23, bf16[4,192,768]{2,1,0:T(8,128)(2,1)} %copy-done.22, ...), custom_call_target="tpu_custom_call" | custom-call | tf_op jit(solution)/shard_map/line_total/pallas_call | solution.py:872
  287.0 6.1 %layer.1 = bf16[1024,768]{1,0:T(8,128)(2,1)} custom-call(s32[1]{0:T(128)S(6)} %copy.23.length_ref, bf16[1024,768]{1,0:T(8,128)(2,1)} %bitcast.12.returned_ref, s32[1024,128]{1,0:T(8,128)} %get-tuple-element.95.column_ref, f32[1024,768]{1,0:T(8,128)} %get-tuple-element.106.residual_ref, f32[1024,128]{1,0:T(8,128)} %get-tuple-element.151.gate_ref), custom_call_target="tpu_custom_call" | custom-call | flops 1610612736 | bytes 7864320 | tf_op jit(solution)/shard_map/layer/pallas_call | solution.py:684
  293.1 7.7 %all-to-all-done.5.gathered_ref = bf16[8,208,384]{2,1,0:T(8,128)(2,1)S(1)} async-done(((bf16[8,208,384]{2,1,0:T(8,128)(2,1)}), bf16[8,208,384]{2,1,0:T(8,128)(2,1)S(1)}, u32[]{:S(2)}, u32[]{:S(2)}) %all-to-all-start.5) | async-done | bytes 1277984 | tf_op jit(solution)/shard_map/all_to_all | solution.py:1135
  300.8 2.0 copy-done.3
  302.8 1.8 assemble.1
  304.6 0.2 slice_reduce_fusion
  304.9 0.6 dynamic-slice_divide_fusion
  305.5 0.6 fusion
  306.2 4.0 %line_total.2 = f32[192,3072]{1,0:T(8,128)} custom-call(s32[1]{0:T(128)} %bitcast.1.place_ref, bf16[4,192,768]{2,1,0:T(8,128)(2,1)} %get-tuple-element.156.middle_ref, bf16[8,192,768]{2,1,0:T(8,128)(2,1)} %get-tuple-element.120.left_ref.end_ref, bf16[4,192,768]{2,1,0:T(8,128)(2,1)} %collective-permute-done.12.refs_0_, ...), custom_call_target="tpu_custom_call" | custom-call | tf_op jit(solution)/shard_map/line_total/pallas_call | solution.py:872
  (67 shorter events, 0.2 us)
Async XLA Ops:
  1.3 10.4 %copy-start.1 = (bf16[768,2304]{1,0:T(8,128)(2,1)S(1)}, bf16[768,2304]{1,0:T(8,128)(2,1)}, u32[]{:S(2)}) copy-start(bf16[768,2304]{1,0:T(8,128)(2,1)} %weight_ref.9) | copy-start | bytes 10616836
  6.2 5.3 %copy-start.25 = (f32[768]{0:T(1024)S(1)}, f32[768]{0:T(1024)}, u32[]{:S(2)}) copy-start(f32[768]{0:T(1024)} %param.19) | copy-start | bytes 9220
  6.2 5.4 %copy-start.24 = (f32[768]{0:T(1024)S(1)}, f32[768]{0:T(1024)}, u32[]{:S(2)}) copy-start(f32[768]{0:T(1024)} %param.20) | copy-start | bytes 9220
  6.2 5.4 %copy-start.27 = (f32[768]{0:T(1024)S(1)}, f32[768]{0:T(1024)}, u32[]{:S(2)}) copy-start(f32[768]{0:T(1024)} %param.21) | copy-start | bytes 9220
  6.2 5.4 %copy-start.28 = (f32[768]{0:T(1024)S(1)}, f32[768]{0:T(1024)}, u32[]{:S(2)}) copy-start(f32[768]{0:T(1024)} %param.22) | copy-start | bytes 9220
  6.3 30.0 %all-to-all-start = ((bf16[8,128,768]{2,1,0:T(8,128)(2,1)}), bf16[8,128,768]{2,1,0:T(8,128)(2,1)}, u32[]{:S(2)}, u32[]{:S(2)}) async-start(bf16[8,128,768]{2,1,0:T(8,128)(2,1)} %bitcast.22), calls=%async_computation | async-start | bytes 3145728 | tf_op jit(solution)/shard_map/all_to_all | solution.py:1135
  11.7 1.4 copy-start.8
  13.1 5.2 %copy-start.6 = (f32[4,768]{1,0:T(4,128)}, f32[4,768]{1,0:T(4,128)S(1)}, u32[]{:S(2)}) copy-start(f32[4,768]{1,0:T(4,128)S(1)} %pad_maximum_fusion.norms_ref) | copy-start | bytes 36868
  32.2 2.2 copy-start.11
  34.4 1.1 copy-start.13
  35.5 0.8 copy-start.17
  43.8 25.3 %all-to-all-start.1 = ((bf16[8,128,768]{2,1,0:T(8,128)(2,1)}), bf16[8,128,768]{2,1,0:T(8,128)(2,1)S(1)}, u32[]{:S(2)}, u32[]{:S(2)}) async-start(bf16[8,128,768]{2,1,0:T(8,128)(2,1)} %bitcast.23), calls=%async_computation.1 | async-start | bytes 3145728 | tf_op jit(solution)/shard_map/all_to_all | solution.py:1135
  69.1 1.1 copy-start.18
  108.6 55.9 %collective-permute-start.2 = (bf16[8,192,768]{2,1,0:T(8,128)(2,1)}, bf16[8,192,768]{2,1,0:T(8,128)(2,1)}, u32[]{:S(2)}, u32[]{:S(2)}) collective-permute-start(bf16[8,192,768]{2,1,0:T(8,128)(2,1)} %get-tuple-element.101.left_ref), channel_id=1, source_target_pairs={{0,8},{24,16},{1,9},{25,17},{2,10},{26,18},{3,11},{27,19},{4,12},{... | collective-permute-start | bytes 7077896 | tf_op jit(solution)/shard_map/ppermute | solution.py:918
  113.9 24.5 %all-to-all-start.2 = ((bf16[8,128,768]{2,1,0:T(8,128)(2,1)}), bf16[8,128,768]{2,1,0:T(8,128)(2,1)S(1)}, u32[]{:S(2)}, u32[]{:S(2)}) async-start(bf16[8,128,768]{2,1,0:T(8,128)(2,1)} %bitcast.21), calls=%async_computation.2 | async-start | bytes 3145728 | tf_op jit(solution)/shard_map/all_to_all | solution.py:1135
  117.5 95.5 %collective-permute-start.1 = (bf16[8,192,768]{2,1,0:T(8,128)(2,1)}, bf16[8,192,768]{2,1,0:T(8,128)(2,1)}, u32[]{:S(2)}, u32[]{:S(2)}) collective-permute-start(bf16[8,192,768]{2,1,0:T(8,128)(2,1)} %get-tuple-element.99.left_ref), channel_id=1, source_target_pairs={{0,8},{24,16},{1,9},{25,17},{2,10},{26,18},{3,11},{27,19},{4,12},{... | collective-permute-start | bytes 7077896 | tf_op jit(solution)/shard_map/ppermute | solution.py:918
  138.4 1.1 copy-start.19
  151.6 12.9 %copy-start.5 = (bf16[8,192,768]{2,1,0:T(8,128)(2,1)S(1)}, bf16[8,192,768]{2,1,0:T(8,128)(2,1)}, u32[]{:S(2)}) copy-start(bf16[8,192,768]{2,1,0:T(8,128)(2,1)} %get-tuple-element.101.left_ref) | copy-start | bytes 7077892
  151.6 45.3 %all-to-all-start.3 = ((bf16[8,128,768]{2,1,0:T(8,128)(2,1)}), bf16[8,128,768]{2,1,0:T(8,128)(2,1)}, u32[]{:S(2)}, u32[]{:S(2)}) async-start(bf16[8,128,768]{2,1,0:T(8,128)(2,1)} %bitcast.19), calls=%async_computation.3 | async-start | bytes 3145728 | tf_op jit(solution)/shard_map/all_to_all | solution.py:1135
  167.5 45.6 %collective-permute-start.6 = (bf16[8,192,768]{2,1,0:T(8,128)(2,1)}, bf16[8,192,768]{2,1,0:T(8,128)(2,1)}, u32[]{:S(2)}, u32[]{:S(2)}) collective-permute-start(bf16[8,192,768]{2,1,0:T(8,128)(2,1)} %add.15), channel_id=1, source_target_pairs={{8,16},{16,8},{9,17},{17,9},{10,18},{18,10},{11,19},{19,11},{12,20... | collective-permute-start | bytes 7077896 | tf_op jit(solution)/shard_map/ppermute | solution.py:918
  169.6 27.3 %copy-start.7 = (f32[4,768]{1,0:T(4,128)S(1)}, f32[4,768]{1,0:T(4,128)}, u32[]{:S(2)}) copy-start(f32[4,768]{1,0:T(4,128)} %copy-done.6) | copy-start | bytes 36868
  169.6 27.3 %copy-start.9 = (bf16[1024,768]{1,0:T(8,128)(2,1)S(1)}, bf16[1024,768]{1,0:T(8,128)(2,1)}, u32[]{:S(2)}) copy-start(bf16[1024,768]{1,0:T(8,128)(2,1)} %tokens_ref.6) | copy-start | bytes 4718596
  169.6 27.3 %copy-start.14 = (bf16[768,768]{1,0:T(8,128)(2,1)S(1)}, bf16[768,768]{1,0:T(8,128)(2,1)}, u32[]{:S(2)}) copy-start(bf16[768,768]{1,0:T(8,128)(2,1)} %get-tuple-element.112.output_grad_ref) | copy-start | bytes 3538948
  169.6 27.3 %copy-start.16 = (f32[8,768]{1,0:T(8,128)S(1)}, f32[8,768]{1,0:T(8,128)}, u32[]{:S(2)}) copy-start(f32[8,768]{1,0:T(8,128)} %get-tuple-element.113.second_ref) | copy-start | bytes 73732
  196.9 2.3 copy-start.12
  206.2 4.9 %collective-permute-start.3 = (bf16[4,448,384]{2,1,0:T(8,128)(2,1)S(1)}, bf16[4,448,384]{2,1,0:T(8,128)(2,1)S(1)}, u32[]{:S(2)}, u32[]{:S(2)}) collective-permute-start(bf16[4,448,384]{2,1,0:T(8,128)(2,1)S(1)} %get-tuple-element.115), channel_id=1, source_target_pairs={{0,1},{1,0},{2,3},{3,2},{4,5},{5,4},{6,7},{7,6},{8,9},{9,8},{10,11... | collective-permute-start | bytes 4128776 | tf_op jit(solution)/shard_map/ppermute | solution.py:1172
  206.3 4.8 %collective-permute-start.4 = (bf16[4,384,384]{2,1,0:T(8,128)(2,1)S(1)}, bf16[4,384,384]{2,1,0:T(8,128)(2,1)S(1)}, u32[]{:S(2)}, u32[]{:S(2)}) collective-permute-start(bf16[4,384,384]{2,1,0:T(8,128)(2,1)S(1)} %get-tuple-element.117), channel_id=1, source_target_pairs={{0,1},{1,0},{2,3},{3,2},{4,5},{5,4},{6,7},{7,6},{8,9},{9,8},{10,11... | collective-permute-start | bytes 3538952 | tf_op jit(solution)/shard_map/ppermute | solution.py:1172
  211.1 1.9 copy-start
  211.8 17.5 %collective-permute-start.8 = (bf16[4,224,384]{2,1,0:T(8,128)(2,1)S(1)}, bf16[4,224,384]{2,1,0:T(8,128)(2,1)S(1)}, u32[]{:S(2)}, u32[]{:S(2)}) collective-permute-start(bf16[4,224,384]{2,1,0:T(8,128)(2,1)S(1)} %get-tuple-element.126), channel_id=1, source_target_pairs={{0,2},{1,3},{2,0},{3,1},{4,6},{5,7},{6,4},{7,5},{8,10},{9,11},{10,... | collective-permute-start | bytes 2064392 | tf_op jit(solution)/shard_map/ppermute | solution.py:1172
  212.3 15.7 %collective-permute-start.9 = (bf16[4,192,384]{2,1,0:T(8,128)(2,1)S(1)}, bf16[4,192,384]{2,1,0:T(8,128)(2,1)S(1)}, u32[]{:S(2)}, u32[]{:S(2)}) collective-permute-start(bf16[4,192,384]{2,1,0:T(8,128)(2,1)S(1)} %get-tuple-element.128), channel_id=1, source_target_pairs={{0,4},{1,5},{2,6},{3,7},{4,0},{5,1},{6,2},{7,3},{8,12},{9,13},{10,... | collective-permute-start | bytes 1769480 | tf_op jit(solution)/shard_map/ppermute | solution.py:1172
  213.0 5.7 %copy-start.20 = (bf16[4,192,768]{2,1,0:T(8,128)(2,1)S(1)}, bf16[4,192,768]{2,1,0:T(8,128)(2,1)}, u32[]{:S(2)}) copy-start(bf16[4,192,768]{2,1,0:T(8,128)(2,1)} %get-tuple-element.98.middle_ref) | copy-start | bytes 3538948
  214.6 31.4 %collective-permute-start.7 = (bf16[4,192,768]{2,1,0:T(8,128)(2,1)S(1)}, bf16[4,192,768]{2,1,0:T(8,128)(2,1)S(1)}, u32[]{:S(2)}, u32[]{:S(2)}) collective-permute-start(bf16[4,192,768]{2,1,0:T(8,128)(2,1)S(1)} %add.16), channel_id=1, source_target_pairs={{16,24},{8,0},{17,25},{9,1},{18,26},{10,2},{19,27},{11,3},{20,28},... | collective-permute-start | bytes 3538952 | tf_op jit(solution)/shard_map/ppermute | solution.py:918
  215.9 19.4 %copy-start.2 = (bf16[768,2304]{1,0:T(8,128)(2,1)S(1)}, bf16[768,2304]{1,0:T(8,128)(2,1)}, u32[]{:S(2)}) copy-start(bf16[768,2304]{1,0:T(8,128)(2,1)} %weight_ref.9) | copy-start | bytes 10616836
  215.9 19.4 %copy-start.15 = (f32[1024,768]{1,0:T(8,128)S(1)}, f32[1024,768]{1,0:T(8,128)}, u32[]{:S(2)}) copy-start(f32[1024,768]{1,0:T(8,128)} %get-tuple-element.124.residual_grad_ref) | copy-start | bytes 9437188
  217.8 17.5 %copy-start.10 = (bf16[1024,768]{1,0:T(8,128)(2,1)S(1)}, bf16[1024,768]{1,0:T(8,128)(2,1)}, u32[]{:S(2)}) copy-start(bf16[1024,768]{1,0:T(8,128)(2,1)} %tokens_ref.6) | copy-start | bytes 4718596
  217.8 28.1 %collective-permute-start.5 = (bf16[4,192,768]{2,1,0:T(8,128)(2,1)S(1)}, bf16[4,192,768]{2,1,0:T(8,128)(2,1)S(1)}, u32[]{:S(2)}, u32[]{:S(2)}) collective-permute-start(bf16[4,192,768]{2,1,0:T(8,128)(2,1)S(1)} %add.14), channel_id=1, source_target_pairs={{8,16},{16,8},{9,17},{17,9},{10,18},{18,10},{11,19},{19,11},{12,20... | collective-permute-start | bytes 3538952 | tf_op jit(solution)/shard_map/ppermute | solution.py:918
  218.7 32.8 %collective-permute-start = (bf16[4,192,768]{2,1,0:T(8,128)(2,1)S(1)}, bf16[4,192,768]{2,1,0:T(8,128)(2,1)S(1)}, u32[]{:S(2)}, u32[]{:S(2)}) collective-permute-start(bf16[4,192,768]{2,1,0:T(8,128)(2,1)S(1)} %copy-done.20), channel_id=1, source_target_pairs={{0,8},{24,16},{1,9},{25,17},{2,10},{26,18},{3,11},{27,19},{4,12},{... | collective-permute-start | bytes 3538952 | tf_op jit(solution)/shard_map/ppermute | solution.py:918
  229.8 12.1 %collective-permute-start.10 = (bf16[4,112,384]{2,1,0:T(8,128)(2,1)S(1)}, bf16[4,112,384]{2,1,0:T(8,128)(2,1)S(1)}, u32[]{:S(2)}, u32[]{:S(2)}) collective-permute-start(bf16[4,112,384]{2,1,0:T(8,128)(2,1)S(1)} %get-tuple-element.130), channel_id=1, source_target_pairs={{0,4},{1,5},{2,6},{3,7},{4,0},{5,1},{6,2},{7,3},{8,12},{9,13},{10,... | collective-permute-start | bytes 1032200 | tf_op jit(solution)/shard_map/ppermute | solution.py:1172
  230.8 11.1 %collective-permute-start.11 = (bf16[4,96,384]{2,1,0:T(8,128)(2,1)S(1)}, bf16[4,96,384]{2,1,0:T(8,128)(2,1)S(1)}, u32[]{:S(2)}, u32[]{:S(2)}) collective-permute-start(bf16[4,96,384]{2,1,0:T(8,128)(2,1)S(1)} %get-tuple-element.132), channel_id=1, source_target_pairs={{0,2},{1,3},{2,0},{3,1},{4,6},{5,7},{6,4},{7,5},{8,10},{9,11},{10,... | collective-permute-start | bytes 884744 | tf_op jit(solution)/shard_map/ppermute | solution.py:1172
  246.0 5.5 %copy-start.21 = (bf16[4,192,768]{2,1,0:T(8,128)(2,1)}, bf16[4,192,768]{2,1,0:T(8,128)(2,1)S(1)}, u32[]{:S(2)}) copy-start(bf16[4,192,768]{2,1,0:T(8,128)(2,1)S(1)} %collective-permute-done.7.refs_2_) | copy-start | bytes 3538948
  246.0 5.5 %copy-start.22 = (bf16[4,192,768]{2,1,0:T(8,128)(2,1)}, bf16[4,192,768]{2,1,0:T(8,128)(2,1)S(1)}, u32[]{:S(2)}) copy-start(bf16[4,192,768]{2,1,0:T(8,128)(2,1)S(1)} %collective-permute-done.5.refs_1_) | copy-start | bytes 3538948
  251.5 1.0 copy-start.23
  252.7 0.8 copy-start.4
  253.5 22.4 %all-to-all-start.4 = ((bf16[4,208,384]{2,1,0:T(8,128)(2,1)}), bf16[4,208,384]{2,1,0:T(8,128)(2,1)S(1)}, u32[]{:S(2)}, u32[]{:S(2)}) async-start(bf16[4,208,384]{2,1,0:T(8,128)(2,1)} %copy-done.4), calls=%async_computation.4 | async-start | bytes 1277952 | tf_op jit(solution)/shard_map/all_to_all | solution.py:1135
  260.6 44.0 %collective-permute-start.14 = (bf16[4,192,768]{2,1,0:T(8,128)(2,1)}, bf16[4,192,768]{2,1,0:T(8,128)(2,1)}, u32[]{:S(2)}, u32[]{:S(2)}) collective-permute-start(bf16[4,192,768]{2,1,0:T(8,128)(2,1)} %add.18), channel_id=1, source_target_pairs={{16,24},{8,0},{17,25},{9,1},{18,26},{10,2},{19,27},{11,3},{20,28},... | collective-permute-start | bytes 3538952 | tf_op jit(solution)/shard_map/ppermute | solution.py:918
  264.5 40.2 %collective-permute-start.13 = (bf16[4,192,768]{2,1,0:T(8,128)(2,1)}, bf16[4,192,768]{2,1,0:T(8,128)(2,1)}, u32[]{:S(2)}, u32[]{:S(2)}) collective-permute-start(bf16[4,192,768]{2,1,0:T(8,128)(2,1)} %add.17), channel_id=1, source_target_pairs={{8,16},{16,8},{9,17},{17,9},{10,18},{18,10},{11,19},{19,11},{12,20... | collective-permute-start | bytes 3538952 | tf_op jit(solution)/shard_map/ppermute | solution.py:918
  266.1 38.5 %collective-permute-start.12 = (bf16[4,192,768]{2,1,0:T(8,128)(2,1)}, bf16[4,192,768]{2,1,0:T(8,128)(2,1)}, u32[]{:S(2)}, u32[]{:S(2)}) collective-permute-start(bf16[4,192,768]{2,1,0:T(8,128)(2,1)} %get-tuple-element.156.middle_ref), channel_id=1, source_target_pairs={{0,8},{24,16},{1,9},{25,17},{2,10},{26,18},{3,11},{27,19},{4,12},{... | collective-permute-start | bytes 3538952 | tf_op jit(solution)/shard_map/ppermute | solution.py:918
  277.1 23.7 %all-to-all-start.5 = ((bf16[8,208,384]{2,1,0:T(8,128)(2,1)}), bf16[8,208,384]{2,1,0:T(8,128)(2,1)S(1)}, u32[]{:S(2)}, u32[]{:S(2)}) async-start(bf16[8,208,384]{2,1,0:T(8,128)(2,1)} %spread.1), calls=%async_computation.5 | async-start | bytes 2555904 | tf_op jit(solution)/shard_map/all_to_all | solution.py:1135
  300.8 2.0 copy-start.3
  304.9 5.3 %copy-start.26 = (f32[192]{0:T(256)}, f32[192]{0:T(256)S(1)}, u32[]{:S(2)}) copy-start(f32[192]{0:T(256)S(1)} %get-tuple-element.168) | copy-start | bytes 2308
